TPU v7x, 32 devices: a whole 2x2x4 slice. The times are simulated.
32 devices in a mesh: dp: 8 (over z, y), tensor: 4 (over x, core).
Axes of the slice: x: 2, y: 2, z: 4, core: 2. Of those that a mesh axis runs over, the one named last changes fastest.
Arguments:
- block_input: bfloat16 [24576, 240], P(('dp', 'tensor')), may hold values from -6 to 6
- lengths: int32 [128], P('dp'), may hold values from 6 to 192, as said below
- cotangent: bfloat16 [24576, 240], P(('dp', 'tensor')), may hold values from -6 to 6
- norm_params: float32 [5, 2, 240], replicated, may hold values from -0.9 to 1.45, as said below
- bn_params: float32 [2, 240], P(None, 'tensor'), may hold values from -0.9 to 1.45, as said below
- ffn_in: float32 [2, 240, 960], P(None, None, 'tensor'), may hold values from -0.375 to 0.375
- ffn_out: float32 [2, 960, 240], P(None, 'tensor'), may hold values from -0.1875 to 0.1875
- attn_in: float32 [3, 240, 240], P(None, None, 'tensor'), may hold values from -0.375 to 0.375
- attn_out: float32 [240, 240], P('tensor'), may hold values from -3.5 to 3.5
- conv_in: float32 [2, 240, 240], P(None, None, 'tensor'), may hold values from -0.375 to 0.375
- depth_kernel: float32 [15, 240], P(None, 'tensor'), may hold values from -1.5 to 1.5
- conv_out: float32 [240, 240], P('tensor'), may hold values from -0.75 to 0.75
- stat_wide: float32 [4, 11, 240, 240], P('tensor'), may hold values from 0 to 960, as said below
- stat_head: float32 [4, 8, 60, 60], P('tensor'), may hold values from 0 to 960, as said below
- stat_hidden: float32 [4, 4, 240, 240], P('tensor'), may hold values from 0 to 960, as said below
- stat_kernel: float32 [4, 15, 15], P('tensor'), may hold values from 0 to 960, as said below
- norm_second: float32 [5, 2, 240], replicated, may hold values from 1 to 16
- bn_second: float32 [2, 240], P(None, 'tensor'), may hold values from 1 to 16
- step_count: int32 [1], replicated, may hold values from 1 to 20
Outputs:
- block_out: bfloat16 [24576, 240], P(('dp', 'tensor'))
- input_grad: float32 [24576, 240], P(('dp', 'tensor'))
- grad_norm: float32 [1], replicated
- clip_norm: float32 [5, 2, 240], replicated
- clip_bn: float32 [2, 240], P(None, 'tensor')
- clip_ffn_in: float32 [2, 240, 960], P(None, None, 'tensor')
- clip_ffn_out: float32 [2, 960, 240], P(None, 'tensor')
- clip_attn_in: float32 [3, 240, 240], P(None, None, 'tensor')
- clip_attn_out: float32 [240, 240], P('tensor')
- clip_conv_in: float32 [2, 240, 240], P(None, None, 'tensor')
- clip_depth: float32 [15, 240], P(None, 'tensor')
- clip_conv_out: float32 [240, 240], P('tensor')
- new_ffn_in: float32 [2, 240, 960], P(None, None, 'tensor')
- new_ffn_out: float32 [2, 960, 240], P(None, 'tensor')
- new_attn_in: float32 [3, 240, 240], P(None, None, 'tensor')
- new_attn_out: float32 [240, 240], P('tensor')
- new_conv_in: float32 [2, 240, 240], P(None, None, 'tensor')
- new_depth: float32 [15, 240], P(None, 'tensor')
- new_conv_out: float32 [240, 240], P('tensor')
- new_norm: float32 [5, 2, 240], replicated
- new_bn: float32 [2, 240], P(None, 'tensor')
- new_norm_second: float32 [5, 2, 240], replicated
- new_bn_second: float32 [2, 240], P(None, 'tensor')
- new_stat_wide: float32 [4, 11, 240, 240], P('tensor')
- new_stat_head: float32 [4, 8, 60, 60], P('tensor')
- new_stat_hidden: float32 [4, 4, 240, 240], P('tensor')
- new_stat_kernel: float32 [4, 15, 15], P('tensor')
Inputs may be any that keep to these rules, and one draw needn't show every extreme that they name: `lengths`: in each group of 16 consecutive utterances one has exactly 192 frames. `norm_params`: gains near one, biases near zero. `bn_params`: gains near one, biases near zero. `stat_wide`: each block is a positive multiple of the identity. `stat_head`: each block is a positive multiple of the identity. `stat_hidden`: each block is a positive multiple of the identity. `stat_kernel`: each block is a positive multiple of the identity.
All inputs are finite; a program needn't handle non-finite values.
Results may differ from a plain program's by a relative error of at most 0.035.
Values may be sent and summed in bfloat16 or wider, within the bound.
A program may use at most 128 MiB of HBM per device.

v0:
```python
import math

import jax
import jax.numpy as jnp
from jax import lax
from jax.sharding import PartitionSpec as P

D = 240
KS = 15
LEN = 192
ROOT_ITERS = 8
HEAD = 60
NPARAM = 1331280


precise = lax.Precision.HIGHEST
PEAK_RATE = 2.0
WARM_STEPS = 4.0
SMALL_RATE = 0.3
GRAFT_SCALE = 0.6
NEG_FILL = -1000000000.0


def product(left_side, right_side):
    return jnp.dot(left_side, right_side, preferred_element_type=jnp.float32)


def product_tn(left_side, right_side):
    return lax.dot_general(
        left_side, right_side, (((0,), (0,)), ((), ())), preferred_element_type=jnp.float32
    )


def product_nt(left_side, right_side):
    return lax.dot_general(
        left_side, right_side, (((1,), (1,)), ((), ())), preferred_element_type=jnp.float32
    )


def layer_norm(hidden, gain_vec, bias_vec):
    mean_value = jnp.mean(hidden, axis=-1, keepdims=True)
    centred = hidden - mean_value
    spread = jnp.mean(centred * centred, axis=-1, keepdims=True)
    return centred * lax.rsqrt(spread + 1e-05) * gain_vec + bias_vec


def swish_act(value):
    return value * jax.nn.sigmoid(value)


def swish_slope(value):
    sigma = jax.nn.sigmoid(value)
    return sigma * (1.0 + value * (1.0 - sigma))


def norm_back(hidden, params, grad_rows):
    unused, pullback = jax.vjp(layer_norm, hidden, params[0], params[1])
    return pullback(grad_rows)


def spread_rows(normed):
    return lax.all_gather(normed.astype(jnp.bfloat16), "tensor", axis=0, tiled=True)


def collect_rows(partial_value):
    return lax.psum_scatter(
        partial_value.astype(jnp.bfloat16), "tensor", scatter_dimension=0, tiled=True
    ).astype(jnp.float32)


def spread_grads(gradient):
    return lax.all_gather(gradient.astype(jnp.bfloat16), "tensor", axis=0, tiled=True)


def collect_grads(partial_value):
    return lax.psum_scatter(
        partial_value.astype(jnp.bfloat16), "tensor", scatter_dimension=0, tiled=True
    ).astype(jnp.float32)


def place_channels(vector, offset):
    return lax.dynamic_update_slice(jnp.zeros((D,), jnp.float32), vector, (offset,))


def pick_channels(vector, offset, width):
    return lax.dynamic_slice_in_dim(vector, offset, width)


def ffn_forward(gathered, first_weight, second_weight):
    inner_pre = product(gathered, first_weight.astype(jnp.bfloat16))
    active = swish_act(inner_pre).astype(jnp.bfloat16)
    return (product(active, second_weight.astype(jnp.bfloat16)), inner_pre, active)


def ffn_backward(gathered, grad_rows, first_weight, second_weight, inner_pre, active):
    first_low = first_weight.astype(jnp.bfloat16)
    d_active = product_nt(grad_rows, second_weight.astype(jnp.bfloat16))
    d_inner = (d_active * swish_slope(inner_pre)).astype(jnp.bfloat16)
    g_second = product_tn(active, grad_rows)
    g_first = product_tn(gathered, d_inner)
    return (product_nt(d_inner, first_low), g_first, g_second)


def attn_scores(queries, key_rows, group_mask):
    scores = jnp.einsum(
        "uqhe,ukhe->uhqk", queries, key_rows, preferred_element_type=jnp.float32
    ) * HEAD ** (-0.5)
    return jnp.where(group_mask[:, None, None, :] > 0, scores, NEG_FILL)


def attn_forward(gathered, attn_in, attn_out, group_mask):
    row_count = gathered.shape[0]
    utterances = group_mask.shape[0]
    column_count = attn_in.shape[2]
    shape_four = (utterances, LEN, column_count // HEAD, HEAD)
    queries, key_rows, values = [
        product(gathered, attn_in[member].astype(jnp.bfloat16))
        .astype(jnp.bfloat16)
        .reshape(shape_four)
        for member in range(3)
    ]
    scores = attn_scores(queries, key_rows, group_mask)
    row_max = jnp.max(scores, axis=-1, keepdims=True)
    log_total = row_max + jnp.log(jnp.sum(jnp.exp(scores - row_max), axis=-1, keepdims=True))
    prob_low = jnp.exp(scores - log_total).astype(jnp.bfloat16)
    mixture = jnp.einsum("uhqk,ukhe->uqhe", prob_low, values, preferred_element_type=jnp.float32)
    mixture = mixture.astype(jnp.bfloat16).reshape(row_count, column_count)
    return (
        product(mixture, attn_out.astype(jnp.bfloat16)),
        (queries, key_rows, values, log_total, mixture),
    )


def attn_backward(gathered, grad_rows, attn_in, attn_out, group_mask, kept_state):
    queries, key_rows, values, log_total, mixture = kept_state
    row_count, column_count = mixture.shape
    score_scale = HEAD ** (-0.5)
    d_mixture = (
        product_nt(grad_rows, attn_out.astype(jnp.bfloat16))
        .astype(jnp.bfloat16)
        .reshape(queries.shape)
    )
    g_attn_out = product_tn(mixture, grad_rows)
    prob_full = jnp.exp(attn_scores(queries, key_rows, group_mask) - log_total)
    prob_low = prob_full.astype(jnp.bfloat16)
    d_probs = jnp.einsum("uqhe,ukhe->uhqk", d_mixture, values, preferred_element_type=jnp.float32)
    d_values = jnp.einsum(
        "uhqk,uqhe->ukhe", prob_low, d_mixture, preferred_element_type=jnp.float32
    )
    d_scores = (
        prob_full * (d_probs - jnp.sum(prob_full * d_probs, axis=-1, keepdims=True))
    ).astype(jnp.bfloat16)
    d_queries = (
        jnp.einsum("uhqk,ukhe->uqhe", d_scores, key_rows, preferred_element_type=jnp.float32)
        * score_scale
    )
    d_keys = (
        jnp.einsum("uhqk,uqhe->ukhe", d_scores, queries, preferred_element_type=jnp.float32)
        * score_scale
    )
    d_parts = [
        part_grad.astype(jnp.bfloat16).reshape(row_count, column_count)
        for part_grad in (d_queries, d_keys, d_values)
    ]
    g_attn_in = jnp.stack([product_tn(gathered, part_grad) for part_grad in d_parts])
    d_gathered = product_nt(d_parts[0], attn_in[0].astype(jnp.bfloat16))
    d_gathered = d_gathered + product_nt(d_parts[1], attn_in[1].astype(jnp.bfloat16))
    d_gathered = d_gathered + product_nt(d_parts[2], attn_in[2].astype(jnp.bfloat16))
    return (d_gathered, g_attn_in, g_attn_out)


def depthwise(frames, depth_kernel):
    half_width = KS // 2
    padded = jnp.pad(frames, ((0, 0), (half_width, KS - 1 - half_width), (0, 0)))
    running = jnp.zeros_like(frames)
    for offset in range(KS):
        running = running + padded[:, offset : offset + frames.shape[1], :] * depth_kernel[offset]
    return running


def conv_front(value_pre, gate_pre, depth_kernel, frame_mask):
    gated = value_pre * jax.nn.sigmoid(gate_pre) * frame_mask[:, None]
    utterances = frame_mask.shape[0] // LEN
    return depthwise(gated.reshape(utterances, LEN, -1), depth_kernel).reshape(value_pre.shape)


def conv_back(conv_mid, mean_value, inv_std, bn_params, frame_mask):
    normal = (conv_mid - mean_value) * inv_std * bn_params[0] + bn_params[1]
    return swish_act(normal) * frame_mask[:, None]


def conv_forward(gathered, conv_in, depth_kernel, bn_params, conv_out, frame_mask, offset, share):
    value_pre = product(gathered, conv_in[0].astype(jnp.bfloat16))
    gate_pre = product(gathered, conv_in[1].astype(jnp.bfloat16))
    conv_mid = conv_front(value_pre, gate_pre, depth_kernel, frame_mask)
    width = conv_mid.shape[1]
    masked = conv_mid * frame_mask[:, None]
    count_here = jnp.sum(frame_mask) * share
    first_sum, total_count = lax.psum(
        (place_channels(jnp.sum(masked, axis=0), offset), count_here), ("dp", "tensor")
    )
    mean_value = pick_channels(first_sum, offset, width) / total_count
    centred = conv_mid - mean_value
    spread_sum = lax.psum(
        place_channels(jnp.sum(centred * centred * frame_mask[:, None], axis=0), offset),
        ("dp", "tensor"),
    )
    spread = pick_channels(spread_sum, offset, width) / total_count
    inv_std = lax.rsqrt(spread + 1e-05)
    active = conv_back(conv_mid, mean_value, inv_std, bn_params, frame_mask).astype(jnp.bfloat16)
    return (
        product(active, conv_out.astype(jnp.bfloat16)),
        (value_pre, gate_pre, conv_mid, mean_value, inv_std, total_count, active),
    )


def conv_backward(
    gathered, grad_rows, conv_in, depth_kernel, bn_params, conv_out, frame_mask, kept_state, offset
):
    value_pre, gate_pre, conv_mid, mean_value, inv_std, total_count, active = kept_state
    width = conv_mid.shape[1]
    d_active = product_nt(grad_rows, conv_out.astype(jnp.bfloat16))
    g_conv_out = product_tn(active, grad_rows)
    unused, norm_pull = jax.vjp(
        lambda mid_rows, mean_in, std_in, batch_in: conv_back(
            mid_rows, mean_in, std_in, batch_in, frame_mask
        ),
        conv_mid,
        mean_value,
        inv_std,
        bn_params,
    )
    d_mid, d_mean, d_std, g_batch = norm_pull(d_active)
    mean_all, std_all = lax.psum(
        (place_channels(d_mean, offset), place_channels(d_std, offset)), ("dp", "tensor")
    )
    d_mean = pick_channels(mean_all, offset, width)
    d_std = pick_channels(std_all, offset, width)
    d_spread = -0.5 * inv_std * inv_std * inv_std * d_std
    d_mid = (
        d_mid
        + frame_mask[:, None] * (d_mean + 2.0 * (conv_mid - mean_value) * d_spread) / total_count
    )
    unused, front_pull = jax.vjp(
        lambda value_in, gate_in, kernel_in: conv_front(value_in, gate_in, kernel_in, frame_mask),
        value_pre,
        gate_pre,
        depth_kernel,
    )
    d_value, d_gate, g_kernel = front_pull(d_mid)
    d_value = d_value.astype(jnp.bfloat16)
    d_gate = d_gate.astype(jnp.bfloat16)
    g_conv_in = jnp.stack([product_tn(gathered, d_value), product_tn(gathered, d_gate)])
    d_gathered = product_nt(d_value, conv_in[0].astype(jnp.bfloat16)) + product_nt(
        d_gate, conv_in[1].astype(jnp.bfloat16)
    )
    return (d_gathered, g_conv_in, g_kernel, g_batch, g_conv_out)


def inverse_root(stat):
    identity = jnp.eye(stat.shape[-1], dtype=jnp.float32)
    frob_size = jnp.sqrt(jnp.sum(stat * stat, axis=(-2, -1), keepdims=True))
    zscale = 2.5 / frob_size
    root_est = jnp.sqrt(jnp.sqrt(zscale)) * identity
    scaled_stat = zscale * stat
    for iteration in range(ROOT_ITERS):
        stepper = 1.25 * identity - 0.25 * scaled_stat
        root_est = jnp.matmul(root_est, stepper, precision=precise)
        square = jnp.matmul(stepper, stepper, precision=precise)
        scaled_stat = jnp.matmul(
            jnp.matmul(square, square, precision=precise), scaled_stat, precision=precise
        )
    return root_est


def precondition(weight, gradient, left_stat, right_stat, step_rate):
    flipped = jnp.swapaxes(gradient, -1, -2)
    left_new = 0.5 * left_stat + 0.5 * jnp.matmul(gradient, flipped, precision=precise)
    right_new = 0.5 * right_stat + 0.5 * jnp.matmul(flipped, gradient, precision=precise)
    direction = jnp.matmul(
        jnp.matmul(inverse_root(left_new), gradient, precision=precise),
        inverse_root(right_new),
        precision=precise,
    )
    weight_size = jnp.sqrt(jnp.sum(weight * weight, axis=(-2, -1), keepdims=True))
    direction_size = jnp.sqrt(jnp.sum(direction * direction, axis=(-2, -1), keepdims=True))
    graft = GRAFT_SCALE * weight_size / (direction_size + 1e-06)
    return (weight - step_rate * graft * direction, left_new, right_new)


def learning_rate(step_count):
    step_value = step_count[0].astype(jnp.float32)
    return PEAK_RATE * jnp.minimum(step_value / WARM_STEPS, jnp.sqrt(WARM_STEPS / step_value))


def owned_update(number, plan_total, matrix_plan, step_rate):
    owner = number * lax.axis_size("dp") // plan_total

    def compute(operands):
        return precondition(operands[0], operands[1], operands[2], operands[3], step_rate)

    def vacant(operands):
        return (
            jnp.zeros_like(operands[0]),
            jnp.zeros_like(operands[2]),
            jnp.zeros_like(operands[3]),
        )

    return lax.cond(lax.axis_index("dp") == owner, compute, vacant, matrix_plan)


def assemble(results):
    ffn_in_new = jnp.stack([results[0][0], results[1][0]])
    ffn_out_new = jnp.stack([results[2][0], results[3][0]])
    attn_in_new = jnp.stack([results[4][0], results[5][0], results[6][0]])
    conv_in_new = jnp.stack([results[8][0], results[9][0]])
    wide_new = jnp.stack(
        [
            results[0][1],
            results[1][1],
            results[2][2],
            results[3][2],
            results[4][1],
            results[5][1],
            results[6][1],
            results[7][2],
            results[8][1],
            results[9][1],
            results[11][2],
        ]
    )[None]
    head_new = jnp.stack(
        [
            results[4][2],
            results[5][2],
            results[6][2],
            results[7][1],
            results[8][2],
            results[9][2],
            results[10][2],
            results[11][1],
        ]
    )[None]
    hidden_new = jnp.stack([results[0][2], results[1][2], results[2][1], results[3][1]])[None]
    kernel_new = results[10][1][None]
    return (
        ffn_in_new,
        ffn_out_new,
        attn_in_new,
        results[7][0],
        conv_in_new,
        results[10][0],
        results[11][0],
        wide_new,
        head_new,
        hidden_new,
        kernel_new,
    )


def local(
    block_input,
    lengths,
    cotangent,
    norm_params,
    bn_params,
    ffn_in,
    ffn_out,
    attn_in,
    attn_out,
    conv_in,
    depth_kernel,
    conv_out,
    stat_wide,
    stat_head,
    stat_hidden,
    stat_kernel,
    norm_second,
    bn_second,
    step_count,
):
    w_bn, w_ffn_in, w_ffn_out, w_attn_in, w_attn_out, w_conv_in, w_depth, w_conv_out = (
        bn_params,
        ffn_in,
        ffn_out,
        attn_in,
        attn_out,
        conv_in,
        depth_kernel,
        conv_out,
    )
    offset = lax.axis_index("tensor") * bn_params.shape[1]
    share = 1.0 / lax.axis_size("tensor")
    group_mask = (jnp.arange(LEN)[None, :] < lengths[:, None]).astype(jnp.float32)
    flat_mask = group_mask.reshape(-1)
    base_rows = block_input.astype(jnp.float32)
    wide_one = spread_rows(layer_norm(base_rows, norm_params[0, 0], norm_params[0, 1]))
    partial_value, inner_one, active_one = ffn_forward(wide_one, w_ffn_in[0], w_ffn_out[0])
    after_one = base_rows + 0.5 * collect_rows(partial_value)
    wide_two = spread_rows(layer_norm(after_one, norm_params[1, 0], norm_params[1, 1]))
    partial_value, attn_state = attn_forward(wide_two, w_attn_in, w_attn_out, group_mask)
    after_two = after_one + collect_rows(partial_value)
    wide_three = spread_rows(layer_norm(after_two, norm_params[2, 0], norm_params[2, 1]))
    partial_value, conv_state = conv_forward(
        wide_three, w_conv_in, w_depth, w_bn, w_conv_out, flat_mask, offset, share
    )
    after_three = after_two + collect_rows(partial_value)
    wide_four = spread_rows(layer_norm(after_three, norm_params[3, 0], norm_params[3, 1]))
    partial_value, inner_two, active_two = ffn_forward(wide_four, w_ffn_in[1], w_ffn_out[1])
    after_four = after_three + 0.5 * collect_rows(partial_value)
    block_out, final_pull = jax.vjp(layer_norm, after_four, norm_params[4, 0], norm_params[4, 1])
    d_four, gain_four, bias_four = final_pull(cotangent.astype(jnp.float32))
    grad_rows = spread_grads(0.5 * d_four)
    d_wide, g_in_two, g_out_two = ffn_backward(
        wide_four, grad_rows, w_ffn_in[1], w_ffn_out[1], inner_two, active_two
    )
    d_three, gain_three, bias_three = norm_back(after_three, norm_params[3], collect_grads(d_wide))
    d_three = d_three + d_four
    grad_rows = spread_grads(d_three)
    d_wide, g_conv_in, g_kernel, g_batch, g_conv_out = conv_backward(
        wide_three, grad_rows, w_conv_in, w_depth, w_bn, w_conv_out, flat_mask, conv_state, offset
    )
    d_two, gain_two, bias_two = norm_back(after_two, norm_params[2], collect_grads(d_wide))
    d_two = d_two + d_three
    grad_rows = spread_grads(d_two)
    d_wide, g_attn_in, g_attn_out = attn_backward(
        wide_two, grad_rows, w_attn_in, w_attn_out, group_mask, attn_state
    )
    d_one, gain_one, bias_one = norm_back(after_one, norm_params[1], collect_grads(d_wide))
    d_one = d_one + d_two
    grad_rows = spread_grads(0.5 * d_one)
    d_wide, g_in_one, g_out_one = ffn_backward(
        wide_one, grad_rows, w_ffn_in[0], w_ffn_out[0], inner_one, active_one
    )
    d_zero, gain_zero, bias_zero = norm_back(base_rows, norm_params[0], collect_grads(d_wide))
    input_grad = d_zero + d_one
    g_norm_here = jnp.stack(
        [
            jnp.stack([gain_zero, bias_zero]),
            jnp.stack([gain_one, bias_one]),
            jnp.stack([gain_two, bias_two]),
            jnp.stack([gain_three, bias_three]),
            jnp.stack([gain_four, bias_four]),
        ]
    )
    summed = lax.psum(
        (
            g_norm_here,
            g_batch,
            jnp.stack([g_in_one, g_in_two]),
            jnp.stack([g_out_one, g_out_two]),
            g_attn_in,
            g_attn_out,
            g_conv_in,
            g_kernel,
            g_conv_out,
        ),
        "dp",
    )
    shard_square = sum((jnp.sum(gradient * gradient) for gradient in summed[1:]))
    tensor_square, g_norm_all = lax.psum((shard_square, summed[0]), "tensor")
    total_square = tensor_square + jnp.sum(g_norm_all * g_norm_all)
    shards = list(summed[1:])
    grad_norm = jnp.sqrt(total_square)
    threshold = math.sqrt(NPARAM)
    clip_factor = threshold / jnp.maximum(grad_norm, threshold)
    c_norm = g_norm_all * clip_factor
    c_bn, c_ffn_in, c_ffn_out, c_attn_in, c_attn_out, c_conv_in, c_depth, c_conv_out = [
        gradient * clip_factor for gradient in shards
    ]
    step_rate = learning_rate(step_count)
    wide_stat = stat_wide[0]
    head_stat = stat_head[0]
    hidden_stat = stat_hidden[0]
    plans = [
        (ffn_in[0], c_ffn_in[0], wide_stat[0], hidden_stat[0]),
        (ffn_in[1], c_ffn_in[1], wide_stat[1], hidden_stat[1]),
        (ffn_out[0], c_ffn_out[0], hidden_stat[2], wide_stat[2]),
        (ffn_out[1], c_ffn_out[1], hidden_stat[3], wide_stat[3]),
        (attn_in[0], c_attn_in[0], wide_stat[4], head_stat[0]),
        (attn_in[1], c_attn_in[1], wide_stat[5], head_stat[1]),
        (attn_in[2], c_attn_in[2], wide_stat[6], head_stat[2]),
        (attn_out, c_attn_out, head_stat[3], wide_stat[7]),
        (conv_in[0], c_conv_in[0], wide_stat[8], head_stat[4]),
        (conv_in[1], c_conv_in[1], wide_stat[9], head_stat[5]),
        (depth_kernel, c_depth, stat_kernel[0], head_stat[6]),
        (conv_out, c_conv_out, head_stat[7], wide_stat[10]),
    ]
    results = [
        owned_update(number, len(plans), matrix_plan, step_rate)
        for number, matrix_plan in enumerate(plans)
    ]
    updated = lax.psum(assemble(results), "dp")
    norm_second_new = 0.5 * norm_second + 0.5 * c_norm * c_norm
    norm_new = norm_params - step_rate * SMALL_RATE * c_norm * lax.rsqrt(norm_second_new)
    bn_second_new = 0.5 * bn_second + 0.5 * c_bn * c_bn
    bn_new = bn_params - step_rate * SMALL_RATE * c_bn * lax.rsqrt(bn_second_new)
    return (
        block_out.astype(jnp.bfloat16),
        input_grad,
        grad_norm.reshape(1),
        c_norm,
        c_bn,
        c_ffn_in,
        c_ffn_out,
        c_attn_in,
        c_attn_out,
        c_conv_in,
        c_depth,
        c_conv_out,
        updated[0],
        updated[1],
        updated[2],
        updated[3],
        updated[4],
        updated[5],
        updated[6],
        norm_new,
        bn_new,
        norm_second_new,
        bn_second_new,
        updated[7],
        updated[8],
        updated[9],
        updated[10],
    )


def solution(mesh):
    return jax.shard_map(
        local,
        mesh=mesh,
        in_specs=(
            P(("dp", "tensor"), None),
            P("dp"),
            P(("dp", "tensor"), None),
            P(),
            P(None, "tensor"),
            P(None, None, "tensor"),
            P(None, "tensor", None),
            P(None, None, "tensor"),
            P("tensor", None),
            P(None, None, "tensor"),
            P(None, "tensor"),
            P("tensor", None),
            P("tensor", None, None, None),
            P("tensor", None, None, None),
            P("tensor", None, None, None),
            P("tensor", None, None),
            P(),
            P(None, "tensor"),
            P(),
        ),
        out_specs=(
            P(("dp", "tensor"), None),
            P(("dp", "tensor"), None),
            P(),
            P(),
            P(None, "tensor"),
            P(None, None, "tensor"),
            P(None, "tensor", None),
            P(None, None, "tensor"),
            P("tensor", None),
            P(None, None, "tensor"),
            P(None, "tensor"),
            P("tensor", None),
            P(None, None, "tensor"),
            P(None, "tensor", None),
            P(None, None, "tensor"),
            P("tensor", None),
            P(None, None, "tensor"),
            P(None, "tensor"),
            P("tensor", None),
            P(),
            P(None, "tensor"),
            P(),
            P(None, "tensor"),
            P("tensor", None, None, None),
            P("tensor", None, None, None),
            P("tensor", None, None, None),
            P("tensor", None, None),
        ),
        check_vma=False,
    )
```

profile of v0, /device:TPU:0, one launch (start us, length us, event | category | flops | bytes accessed | tf_op | source)
XLA Modules:
  0.0 1314.8 jit_solution(8416996090745045297)
XLA Ops:
  12.9 21.9 %all-gather.9.cloned.1.call-done = bf16[3072,240]{0,1:T(8,128)(2,1)} async-done(((bf16[768,240]{0,1:T(8,128)(2,1)}), bf16[3072,240]{0,1:T(8,128)(2,1)}) %all-gather.9.cloned.1.call-update) | async-done | bytes 1474576 | tf_op jit(solution)/shard_map/all_gather | solution.py:62
  41.7 27.5 %reduce-scatter.9.cloned.1.call-done = bf16[768,240]{0,1:T(8,128)(2,1)} async-done(((bf16[3072,240]{0,1:T(8,128)(2,1)}), bf16[768,240]{0,1:T(8,128)(2,1)}) %reduce-scatter.9.cloned.1.call-update) | async-done | bytes 368656 | tf_op jit(solution)/shard_map/reduce_scatter | solution.py:66
  73.7 19.1 %all-gather.11.cloned.1.call-done = bf16[3072,240]{0,1:T(8,128)(2,1)} async-done(((bf16[768,240]{0,1:T(8,128)(2,1)}), bf16[3072,240]{0,1:T(8,128)(2,1)}) %all-gather.11.cloned.1.call-update) | async-done | bytes 1474576 | tf_op jit(solution)/shard_map/all_gather | solution.py:62
  106.3 27.5 %reduce-scatter.11.cloned.1.call-done = bf16[768,240]{0,1:T(8,128)(2,1)} async-done(((bf16[3072,240]{0,1:T(8,128)(2,1)}), bf16[768,240]{0,1:T(8,128)(2,1)}) %reduce-scatter.11.cloned.1.call-update) | async-done | bytes 368656 | tf_op jit(solution)/shard_map/reduce_scatter | solution.py:66
  176.7 39.3 %all-reduce.34 = (f32[240]{0:T(256)S(1)}, f32[]{:T(128)}) all-reduce(f32[240]{0:T(256)S(1)} %dynamic_update_slice.12, f32[]{:T(128)S(6)} %mul.3026), channel_id=1, replica_groups=mesh['dp'=8,'tensor'=4] {'dp','tensor'}, use_global_device_ids=true, to_apply=%region_11.12 | all-reduce | flops 241 | bytes 1928 | tf_op jit(solution)/shard_map/psum | solution.py:199
  220.1 41.1 %psum.191 = f32[240]{0:T(256)S(1)} all-reduce(f32[240]{0:T(256)S(1)} %dynamic_update_slice.13), channel_id=1, replica_groups=mesh['dp'=8,'tensor'=4] {'dp','tensor'}, use_global_device_ids=true, to_apply=%region_15.16 | all-reduce | flops 240 | bytes 1920 | tf_op jit(solution)/shard_map/psum | solution.py:204
  266.0 27.3 %reduce-scatter.13.cloned.1.call-done = bf16[768,240]{0,1:T(8,128)(2,1)} async-done(((bf16[3072,240]{0,1:T(8,128)(2,1)}), bf16[768,240]{0,1:T(8,128)(2,1)}) %reduce-scatter.13.cloned.1.call-update) | async-done | bytes 368656 | tf_op jit(solution)/shard_map/reduce_scatter | solution.py:66
  295.5 19.2 %all-gather.15.cloned.1.call-done = bf16[3072,240]{0,1:T(8,128)(2,1)} async-done(((bf16[768,240]{0,1:T(8,128)(2,1)}), bf16[3072,240]{0,1:T(8,128)(2,1)}) %all-gather.15.cloned.1.call-update) | async-done | bytes 1474576 | tf_op jit(solution)/shard_map/all_gather | solution.py:62
  321.7 27.5 %reduce-scatter.15.cloned.1.call-done = bf16[768,240]{0,1:T(8,128)(2,1)} async-done(((bf16[3072,240]{0,1:T(8,128)(2,1)}), bf16[768,240]{0,1:T(8,128)(2,1)}) %reduce-scatter.15.cloned.1.call-update) | async-done | bytes 368656 | tf_op jit(solution)/shard_map/reduce_scatter | solution.py:66
  354.0 19.2 %all-gather.17.cloned.1.call-done = bf16[3072,240]{0,1:T(8,128)(2,1)} async-done(((bf16[768,240]{0,1:T(8,128)(2,1)}), bf16[3072,240]{0,1:T(8,128)(2,1)}) %all-gather.17.cloned.1.call-update) | async-done | bytes 1474576 | tf_op jit(solution)/shard_map/all_gather | solution.py:72
  379.8 27.5 %reduce-scatter.17.cloned.1.call-done = bf16[768,240]{0,1:T(8,128)(2,1)} async-done(((bf16[3072,240]{0,1:T(8,128)(2,1)}), bf16[768,240]{0,1:T(8,128)(2,1)}) %reduce-scatter.17.cloned.1.call-update) | async-done | bytes 368656 | tf_op jit(solution)/shard_map/reduce_scatter | solution.py:76
  413.4 19.1 %all-gather.19.cloned.1.call-done = bf16[3072,240]{0,1:T(8,128)(2,1)} async-done(((bf16[768,240]{0,1:T(8,128)(2,1)}), bf16[3072,240]{0,1:T(8,128)(2,1)}) %all-gather.19.cloned.1.call-update) | async-done | bytes 1474576 | tf_op jit(solution)/shard_map/all_gather | solution.py:72
  437.6 39.7 %all-reduce.33 = (f32[240]{0:T(256)S(1)}, f32[240]{0:T(256)S(1)}) all-reduce(f32[240]{0:T(256)S(1)} %dynamic_update_slice.15, f32[240]{0:T(256)S(1)} %negate_dynamic-update-slice_fusion), channel_id=1, replica_groups=mesh['dp'=8,'tensor'=4] {'dp','tensor'}, use_global_device_ids=true, to_apply=%region_30.31 | all-reduce | flops 480 | bytes 3840 | tf_op jit(solution)/shard_map/psum | solution.py:234
  511.8 28.3 %reduce-scatter.19.cloned.1.call-done = bf16[768,240]{0,1:T(8,128)(2,1)} async-done(((bf16[3072,240]{0,1:T(8,128)(2,1)}), bf16[768,240]{0,1:T(8,128)(2,1)}) %reduce-scatter.19.cloned.1.call-update) | async-done | bytes 368656 | tf_op jit(solution)/shard_map/reduce_scatter | solution.py:76
  545.5 19.0 %all-gather.21.cloned.1.call-done = bf16[3072,240]{0,1:T(8,128)(2,1)} async-done(((bf16[768,240]{0,1:T(8,128)(2,1)}), bf16[3072,240]{0,1:T(8,128)(2,1)}) %all-gather.21.cloned.1.call-update) | async-done | bytes 1474576 | tf_op jit(solution)/shard_map/all_gather | solution.py:72
  592.3 27.5 %reduce-scatter.21.cloned.1.call-done = bf16[768,240]{0,1:T(8,128)(2,1)} async-done(((bf16[3072,240]{0,1:T(8,128)(2,1)}), bf16[768,240]{0,1:T(8,128)(2,1)}) %reduce-scatter.21.cloned.1.call-update) | async-done | bytes 368656 | tf_op jit(solution)/shard_map/reduce_scatter | solution.py:76
  665.6 71.3 %all-reduce.51.cloned.1.call-done = (f32[2,240,240]{2,1,0:T(8,128)}, f32[2,240,240]{2,1,0:T(8,128)}, f32[3,240,60]{1,2,0:T(8,128)}, f32[2,240,60]{1,2,0:T(8,128)}) async-done(((f32[2,240,240]{2,1,0:T(8,128)}, f32[2,240,240]{2,1,0:T(8,128)}, f32[3,240,60]{1,2,0:T(8,128)}, f32[2,240,60]{1,2,0:T(8,128)}), (f32[2,240,240]{2,1,0:T(8,128)}, f32[2,240,240]{2,1,0:T(8,128)}, f32[3,240,60]{1,2,0:T(8,128)}, ...) | async-done | bytes 1209616 | tf_op jit(solution)/shard_map/psum | solution.py:446
  741.9 24.5 %reduce-scatter.23.cloned.1.call-done = bf16[768,240]{0,1:T(8,128)(2,1)} async-done(((bf16[3072,240]{0,1:T(8,128)(2,1)}), bf16[768,240]{0,1:T(8,128)(2,1)}) %reduce-scatter.23.cloned.1.call-update) | async-done | bytes 368656 | tf_op jit(solution)/shard_map/reduce_scatter | solution.py:76
  771.2 72.3 %all-reduce.47.cloned.1.call-done = (f32[2,60]{1,0:T(2,128)}, f32[60,240]{1,0:T(8,128)}, f32[15,60]{1,0:T(8,128)}, f32[60,240]{1,0:T(8,128)}, f32[5,2,240]{2,1,0:T(2,128)}) async-done(((f32[2,60]{1,0:T(2,128)}, f32[60,240]{1,0:T(8,128)}, f32[15,60]{1,0:T(8,128)}, f32[60,240]{1,0:T(8,128)}, f32[5,2,240]{2,1,0:T(2,128)}), (f32[2,60]{1,0:T(2,128)}, f32[60,240]{1,0:T(8,128)}, f32[15,60]{1,0:T(8,128)}, ...) | async-done | bytes 128896 | tf_op jit(solution)/shard_map/psum | solution.py:446
  872.0 33.5 %conditional.12 = (f32[1,240,240]{2,1,0:T(8,128)}, f32[1,240,240]{2,1,0:T(8,128)}, f32[1,240,240]{2,1,0:T(8,128)}) conditional(s32[]{:T(128)} %convert_element_type.369, () %tuple.168, (f32[240,240]{1,0:T(8,128)S(1)}, f32[1,11,240,240]{3,2,1,0:T(8,128)}, f32[2,240,240]{2,1,0:T(8,128)S(1)}, f32[1,4,240,240]{3,2,1,0:T(8,128)}, f32[]{:T(128)}) %tuple.447), branch_computations={%region_88.89_spmd, %region_89.0_spmd} | conditional | flops 10293348352 | bytes 39690532 | solution.py:309
  959.3 16.4 %conditional.14 = (f32[1,240,240]{2,1,0:T(8,128)}, f32[1,240,240]{2,1,0:T(8,128)}, f32[1,240,240]{2,1,0:T(8,128)S(1)}) conditional(s32[]{:T(128)} %convert_element_type.371, () %tuple.172, (f32[240,240]{1,0:T(8,128)S(1)}, f32[1,4,240,240]{3,2,1,0:T(8,128)}, f32[2,240,240]{2,1,0:T(8,128)S(1)}, f32[1,11,240,240]{3,2,1,0:T(8,128)}, ...), branch_computations={%region_101.102_spmd, %region_102.0_spmd} | conditional | flops 10293348352 | bytes 37847276 | solution.py:309
  977.5 32.9 %conditional.13 = (f32[1,240,240]{2,1,0:T(8,128)}, f32[1,240,240]{2,1,0:T(8,128)}, f32[1,240,240]{2,1,0:T(8,128)S(1)}) conditional(s32[]{:T(128)} %convert_element_type.369, () %tuple.170, (f32[240,240]{1,0:T(8,128)S(1)}, f32[1,11,240,240]{3,2,1,0:T(8,128)}, f32[2,240,240]{2,1,0:T(8,128)S(1)}, f32[1,4,240,240]{3,2,1,0:T(8,128)}, f32[]{:T(128)}) %tuple.171), branch_computations={%region_94.95_spmd, %region_95.0_spmd} | conditional | flops 10293348352 | bytes 37847276 | solution.py:309
  1045.2 58.5 %all-reduce.45.cloned.1.call-done = (f32[60,240]{1,0:T(8,128)}, f32[15,60]{1,0:T(8,128)}, f32[60,240]{1,0:T(8,128)}, f32[1,15,15]{2,0,1:T(1,128)}) async-done(((f32[60,240]{1,0:T(8,128)}, f32[15,60]{1,0:T(8,128)}, f32[60,240]{1,0:T(8,128)}, f32[1,15,15]{2,0,1:T(1,128)}), (f32[60,240]{1,0:T(8,128)}, f32[15,60]{1,0:T(8,128)}, f32[60,240]{1,0:T(8,128)}, f32[1,15,15]{2,0,1:T(1,128)})) %all-reduce.45.cloned.1.call-update) | async-done | bytes 119716 | tf_op jit(solution)/shard_map/psum | solution.py:493
  1103.7 189.4 %all-reduce.49.cloned.1.call-done = (f32[2,240,240]{2,1,0:T(8,128)}, f32[2,240,240]{2,1,0:T(8,128)}, f32[3,240,60]{1,2,0:T(8,128)}, f32[2,240,60]{1,0,2:T(2,128)...) async-done(((f32[2,240,240]{2,1,0:T(8,128)}, f32[2,240,240]{2,1,0:T(8,128)}, f32[3,240,60]{1,2,0:T(8,128)}, ...) | async-done | bytes 4780816 | tf_op jit(solution)/shard_map/psum | solution.py:493
  (754 shorter events, 427.9 us)
Async XLA Ops:
  7.2 27.6 %all-gather.9.cloned.1.call-start = ((), (), s32[]{:S(2)}) async-start(), calls=%async_computation.8 | async-start | bytes 1843200 | tf_op jit(solution)/shard_map/all_gather | solution.py:62
  12.8 56.4 %reduce-scatter.9.cloned.1.call-start = ((), (), s32[]{:S(2)}) async-start(), calls=%async_computation.9 | async-start | bytes 1843200 | tf_op jit(solution)/shard_map/reduce_scatter | solution.py:66
  41.7 51.2 %all-gather.11.cloned.1.call-start = ((), (), s32[]{:S(2)}) async-start(), calls=%async_computation.10 | async-start | bytes 1843200 | tf_op jit(solution)/shard_map/all_gather | solution.py:62
  73.6 60.2 %reduce-scatter.11.cloned.1.call-start = ((), (), s32[]{:S(2)}) async-start(), calls=%async_computation.11 | async-start | bytes 1843200 | tf_op jit(solution)/shard_map/reduce_scatter | solution.py:66
  106.2 49.0 %all-gather.13.cloned.1.call-start = ((), (), s32[]{:S(2)}) async-start(), calls=%async_computation.12 | async-start | bytes 1843200 | tf_op jit(solution)/shard_map/all_gather | solution.py:62
  136.0 157.3 %reduce-scatter.13.cloned.1.call-start = ((), (), s32[]{:S(2)}) async-start(), calls=%async_computation.13 | async-start | bytes 1843200 | tf_op jit(solution)/shard_map/reduce_scatter | solution.py:66
  266.0 48.7 %all-gather.15.cloned.1.call-start = ((), (), s32[]{:S(2)}) async-start(), calls=%async_computation.14 | async-start | bytes 1843200 | tf_op jit(solution)/shard_map/all_gather | solution.py:62
  295.5 53.7 %reduce-scatter.15.cloned.1.call-start = ((), (), s32[]{:S(2)}) async-start(), calls=%async_computation.15 | async-start | bytes 1843200 | tf_op jit(solution)/shard_map/reduce_scatter | solution.py:66
  321.7 51.5 %all-gather.17.cloned.1.call-start = ((), (), s32[]{:S(2)}) async-start(), calls=%async_computation.16 | async-start | bytes 1843200 | tf_op jit(solution)/shard_map/all_gather | solution.py:72
  353.9 53.4 %reduce-scatter.17.cloned.1.call-start = ((), (), s32[]{:S(2)}) async-start(), calls=%async_computation.17 | async-start | bytes 1843200 | tf_op jit(solution)/shard_map/reduce_scatter | solution.py:76
  379.7 52.8 %all-gather.19.cloned.1.call-start = ((), (), s32[]{:S(2)}) async-start(), calls=%async_computation.18 | async-start | bytes 1843200 | tf_op jit(solution)/shard_map/all_gather | solution.py:72
  413.4 126.6 %reduce-scatter.19.cloned.1.call-start = ((), (), s32[]{:S(2)}) async-start(), calls=%async_computation.19 | async-start | bytes 1843200 | tf_op jit(solution)/shard_map/reduce_scatter | solution.py:76
  511.7 52.8 %all-gather.21.cloned.1.call-start = ((), (), s32[]{:S(2)}) async-start(), calls=%async_computation.20 | async-start | bytes 1843200 | tf_op jit(solution)/shard_map/all_gather | solution.py:72
  545.3 74.6 %reduce-scatter.21.cloned.1.call-start = ((), (), s32[]{:S(2)}) async-start(), calls=%async_computation.21 | async-start | bytes 1843200 | tf_op jit(solution)/shard_map/reduce_scatter | solution.py:76
  592.3 53.6 %all-gather.23.cloned.1.call-start = ((), (), s32[]{:S(2)}) async-start(), calls=%async_computation.22 | async-start | bytes 1843200 | tf_op jit(solution)/shard_map/all_gather | solution.py:72
  626.6 110.3 %all-reduce.51.cloned.1.call-start = ((), (), s32[]{:S(2)}) async-start(), calls=%async_computation.27 | async-start | bytes 2621440 | tf_op jit(solution)/shard_map/psum | solution.py:446
  653.0 113.4 %reduce-scatter.23.cloned.1.call-start = ((), (), s32[]{:S(2)}) async-start(), calls=%async_computation.23 | async-start | bytes 1843200 | tf_op jit(solution)/shard_map/reduce_scatter | solution.py:76
  654.8 188.8 %all-reduce.47.cloned.1.call-start = ((), (), s32[]{:S(2)}) async-start(), calls=%async_computation.25 | async-start | bytes 301056 | tf_op jit(solution)/shard_map/psum | solution.py:446
  770.5 333.2 %all-reduce.45.cloned.1.call-start = ((), (), s32[]{:S(2)}) async-start(), calls=%async_computation.24 | async-start | bytes 293888 | tf_op jit(solution)/shard_map/psum | solution.py:493
  867.4 150.6 %copy-start.41 = (f32[3,240,60]{1,2,0:T(8,128)}, f32[3,240,60]{1,2,0:T(8,128)S(1)}, u32[]{:S(2)}) copy-start(f32[3,240,60]{1,2,0:T(8,128)S(1)} %broadcast_multiply_fusion.18) | copy-start | bytes 518404
  869.7 164.0 %copy-start.45 = (f32[60,240]{1,0:T(8,128)}, f32[60,240]{1,0:T(8,128)S(1)}, u32[]{:S(2)}) copy-start(f32[60,240]{1,0:T(8,128)S(1)} %get-tuple-element.842) | copy-start | bytes 172804
  1034.5 258.7 %all-reduce.49.cloned.1.call-start = ((), (), s32[]{:S(2)}) async-start(), calls=%async_computation.26 | async-start | bytes 10469376 | tf_op jit(solution)/shard_map/psum | solution.py:493
  1103.7 197.9 %copy-start.136 = (f32[15,60]{1,0:T(8,128)S(1)}, f32[15,60]{1,0:T(8,128)}, u32[]{:S(2)}) copy-start(f32[15,60]{1,0:T(8,128)} %get-tuple-element.848) | copy-start | bytes 10804
  1103.7 198.5 %copy-start.113 = (f32[60,240]{1,0:T(8,128)S(1)}, f32[60,240]{1,0:T(8,128)}, u32[]{:S(2)}) copy-start(f32[60,240]{1,0:T(8,128)} %get-tuple-element.849) | copy-start | bytes 172804
  (170 other events, 4693.0 us)
Sparse Core Ops, SparseCore 0:
  13.0 21.7 all-gather.8
  41.8 27.4 reduce-scatter.8
  73.7 19.0 all-gather.10
  106.4 27.3 reduce-scatter.10
  136.2 19.0 all-gather.12
  266.1 27.1 reduce-scatter.12
  295.6 19.0 all-gather.14
  321.8 27.3 reduce-scatter.14
  354.0 19.0 all-gather.16
  379.9 27.3 reduce-scatter.16
  413.5 19.0 all-gather.18
  511.8 28.1 reduce-scatter.18
  545.4 19.0 all-gather.20
  592.4 27.4 reduce-scatter.20
  626.7 19.1 all-gather.22
  653.1 83.7 all-reduce.50
  739.9 26.4 reduce-scatter.22
  772.4 71.1 all-reduce.46
  1034.6 69.0 all-reduce.44
  1109.9 183.1 all-reduce.48
where the time goes:
time: 1320 us; the launch traced here: 1310 us
  waiting for transfers between devices  741 us (56%)
  blocking collectives  131 us (10%)
  other arithmetic  125 us (9%)
  matrix products  121 us (9%)
  local copies, waits for them, and re-layouts  84.5 us (6%)
  loops' own time  73.3 us (6%)
  between operations  25.7 us (2%)
    psum x2, waiting for transfers between devices, local(): updated = lax.psum(assemble(results), 'dp')  248 us
    psum x2, waiting for transfers between devices, local(): lax.psum((g_norm_here, g_batch, jnp.stack([g_in_one, g_in_two]), jnp.stac...  144 us
    reduce_scatter x4, waiting for transfers between devices, collect_rows(): lax.psum_scatter(partial_value.astype(jnp.bfloat16), 'tensor', scatter_di...  110 us
    reduce_scatter x4, waiting for transfers between devices, collect_grads(): lax.psum_scatter(partial_value.astype(jnp.bfloat16), 'tensor', scatter_di...  108 us
    another operation x12, loops' own time, owned_update(): return lax.cond(lax.axis_index('dp') == owner, compute, vacant, matrix_plan)  73.3 us
    all_gather x4, waiting for transfers between devices, spread_grads(): lax.all_gather(gradient.astype(jnp.bfloat16), 'tensor', axis=0, tiled=True)  66.1 us
    all_gather x4, waiting for transfers between devices, spread_rows(): lax.all_gather(normed.astype(jnp.bfloat16), 'tensor', axis=0, tiled=True)  65.5 us
    psum x1, blocking collectives, conv_forward(): lax.psum(place_channels(jnp.sum(centred * centred * frame_mask[:, None],...  41.1 us
  transfers between devices with their start and end apart: 20, of which 20 were waited for; matrix products, arithmetic and copies ran while one was open for 3% of the time, Pallas kernels for 0%

commit v1 on v0

v1 whole, which is shorter than its diff:
```python
import functools
import math

import jax
import jax.numpy as jnp
from jax import lax
from jax.experimental import pallas as pl
from jax.experimental.pallas import tpu as pltpu
from jax.sharding import PartitionSpec as P

D = 240
KS = 15
LEN = 192
HEAD = 60
PADH = 64
ROOT_ITERS = 8
FINE_ITERS = 4
NPARAM = 1331280
PEAK_RATE = 2.0
WARM_STEPS = 4.0
SMALL_RATE = 0.3
GRAFT_SCALE = 0.6
NEG_FILL = -1000000000.0
ROWS = 512
VMEM_CAP = 60 * 1024 * 1024

F32 = jnp.float32
BF16 = jnp.bfloat16


def nn(a, b):
    return lax.dot_general(a, b, (((1,), (0,)), ((), ())), preferred_element_type=F32)


def nt(a, b):
    return lax.dot_general(a, b, (((1,), (1,)), ((), ())), preferred_element_type=F32)


def tn(a, b):
    return lax.dot_general(a, b, (((0,), (0,)), ((), ())), preferred_element_type=F32)


def sigmoid(v):
    return 0.5 * jnp.tanh(0.5 * v) + 0.5


def standardize(h):
    centred = h - jnp.sum(h, axis=-1, keepdims=True) * (1.0 / D)
    spread = jnp.sum(centred * centred, axis=-1, keepdims=True) * (1.0 / D)
    inv = lax.rsqrt(spread + 1e-05)
    return centred * inv, inv


def norm_back(h, gain, dy):
    xhat, inv = standardize(h)
    scaled = dy * gain
    mean_a = jnp.sum(scaled, axis=-1, keepdims=True) * (1.0 / D)
    mean_b = jnp.sum(scaled * xhat, axis=-1, keepdims=True) * (1.0 / D)
    dh = inv * (scaled - mean_a - xhat * mean_b)
    return dh, jnp.sum(dy * xhat, axis=0, keepdims=True), jnp.sum(dy, axis=0, keepdims=True)


def row_mask(length):
    return (lax.broadcasted_iota(jnp.int32, (LEN, 1), 0) < length).astype(F32)


def lane_masks(dtype):
    lane = lax.broadcasted_iota(jnp.int32, (1, 128), 1)
    return ((lane < PADH).astype(dtype), (lane >= PADH).astype(dtype))


def own_length(lens_ref, step):
    return lens_ref[lax.axis_index("tensor") * pl.num_programs(0) + step]


def forward_kernel(
    lens_ref, x_ref, np_ref, ffn_ref, mix_ref, small_ref,
    n1_o, inner_o, act_o, x1_o, n2_o, q_o, k_o, v_o, p_o, mix_o, x2_o, n3_o, vp_o, gp_o, mid_o, st_o,
    pad_sc,
):
    step = pl.program_id(0)
    length = own_length(lens_ref, step)
    x0 = x_ref[...].astype(F32)
    n1 = (standardize(x0)[0] * np_ref[0, 0:1, :] + np_ref[0, 1:2, :]).astype(BF16)
    n1_o[...] = n1
    total = jnp.zeros((LEN, D), F32)
    for t in range(ffn_ref.shape[0]):
        inner = nn(n1, ffn_ref[t, 0])
        inner_o[t] = inner
        active = (inner * sigmoid(inner)).astype(BF16)
        act_o[t] = active
        total = total + nn(active, ffn_ref[t, 1])
    x1 = x0 + 0.5 * total
    x1_o[...] = x1
    n2 = (standardize(x1)[0] * np_ref[1, 0:1, :] + np_ref[1, 1:2, :]).astype(BF16)
    n2_o[...] = n2
    q_o[...] = nt(n2, mix_ref[0]).astype(BF16)
    k_o[...] = nt(n2, mix_ref[1]).astype(BF16)
    v_o[...] = nt(n2, mix_ref[2]).astype(BF16)
    key_ok = lax.broadcasted_iota(jnp.int32, (1, LEN), 1) < length
    masks = lane_masks(BF16)
    for half in range(2):
        lanes = slice(half * 128, half * 128 + 128)
        q, k, v = q_o[:, lanes], k_o[:, lanes], v_o[:, lanes]
        mixture = jnp.zeros((LEN, 128), F32)
        for side in range(2):
            scores = nt(q * masks[side], k) * HEAD ** (-0.5)
            scores = jnp.where(key_ok, scores, NEG_FILL)
            exps = jnp.exp(scores - jnp.max(scores, axis=-1, keepdims=True))
            probs = exps * (1.0 / jnp.sum(exps, axis=-1, keepdims=True))
            p_o[0, 2 * half + side] = probs
            mixture = mixture + nn(probs.astype(BF16), v * masks[side])
        mix_o[:, lanes] = mixture.astype(BF16)
    x2 = x1 + nn(mix_o[...], mix_ref[3])
    x2_o[...] = x2
    n3 = (standardize(x2)[0] * np_ref[2, 0:1, :] + np_ref[2, 1:2, :]).astype(BF16)
    n3_o[...] = n3
    value = nt(n3, mix_ref[4])
    gate = nt(n3, mix_ref[5])
    vp_o[...] = value
    gp_o[...] = gate
    mask = row_mask(length)
    gated = value * sigmoid(gate) * mask

    @pl.when(step == 0)
    def _():
        pad_sc[...] = jnp.zeros_like(pad_sc)

    count = length.astype(F32)
    for half in range(2):
        lanes = slice(half * 128, half * 128 + 128)
        pad_sc[half, 8 : 8 + LEN, :] = gated[:, lanes]
        running = jnp.zeros((LEN, 128), F32)
        for j in range(KS):
            running = running + pad_sc[half, 1 + j : 1 + j + LEN, :] * small_ref[j : j + 1, lanes]
        mid_o[:, lanes] = running
        mean = jnp.sum(running * mask, axis=0, keepdims=True) / count
        centred = (running - mean) * mask
        st_o[0, 0:1, lanes] = mean
        st_o[0, 1:2, lanes] = jnp.sum(centred * centred, axis=0, keepdims=True)
        st_o[0, 2:3, lanes] = jnp.full((1, 128), count, F32)
        st_o[0, 3:8, lanes] = jnp.zeros((5, 128), F32)


def ffn_backward(grad, inner_ref, ffn_ref, din_sc, rows):
    total = jnp.zeros((LEN, D), F32)
    for t in range(ffn_ref.shape[0]):
        inner = inner_ref[t]
        sigma = sigmoid(inner)
        d_inner = (nt(grad, ffn_ref[t, 1]) * (sigma * (1.0 + inner * (1.0 - sigma)))).astype(BF16)
        din_sc[t, rows, :] = d_inner
        total = total + nt(d_inner, ffn_ref[t, 0])
    return total


def middle_kernel(
    lens_ref, mid_ref, x2_ref, cot_ref, np_ref, bn_ref, mix_ref, ffn_ref,
    out_o, d3_o, dn_o, act3_o, gc_o, lng_o, gb_o, chunk_o,
    inner_sc, act_sc, din_sc, n4_sc, g2_sc,
):
    step = pl.program_id(0)
    rows = pl.ds(pl.multiple_of(step * LEN, LEN), LEN)
    mask = row_mask(own_length(lens_ref, step))
    mean, inv_std, gain, bias = [bn_ref[i : i + 1, :] for i in range(4)]
    xhat = (mid_ref[...] - mean) * inv_std
    normal = xhat * gain + bias
    sigma = sigmoid(normal)
    act3 = (normal * sigma * mask).astype(BF16)
    act3_o[...] = act3
    x3 = x2_ref[...] + nn(act3, mix_ref[6])
    n4 = (standardize(x3)[0] * np_ref[3, 0:1, :] + np_ref[3, 1:2, :]).astype(BF16)
    n4_sc[rows, :] = n4
    total = jnp.zeros((LEN, D), F32)
    for t in range(ffn_ref.shape[0]):
        inner = nn(n4, ffn_ref[t, 0])
        inner_sc[t] = inner
        active = (inner * sigmoid(inner)).astype(BF16)
        act_sc[t, rows, :] = active
        total = total + nn(active, ffn_ref[t, 1])
    x4 = x3 + 0.5 * total
    out_o[...] = (standardize(x4)[0] * np_ref[4, 0:1, :] + np_ref[4, 1:2, :]).astype(BF16)
    d4, gain4, bias4 = norm_back(x4, np_ref[4, 0:1, :], cot_ref[...].astype(F32))
    g2 = (0.5 * d4).astype(BF16)
    g2_sc[rows, :] = g2
    d_n4 = ffn_backward(g2, inner_sc, ffn_ref, din_sc, rows)
    d3, gain3, bias3 = norm_back(x3, np_ref[3, 0:1, :], d_n4)
    d3 = d3 + d4
    d3_o[...] = d3
    gc = d3.astype(BF16)
    gc_o[...] = gc
    d_normal = nt(gc, mix_ref[6]) * mask * (sigma * (1.0 + normal * (1.0 - sigma)))
    dn_o[...] = d_normal

    @pl.when(step == 0)
    def _():
        lng_o[...] = jnp.zeros_like(lng_o)
        gb_o[...] = jnp.zeros_like(gb_o)

    for i, part in enumerate((gain3, bias3, gain4, bias4)):
        lng_o[6 + i : 7 + i, :] += part
    gb_o[0:1, :] += jnp.sum(d_normal * xhat, axis=0, keepdims=True)
    gb_o[1:2, :] += jnp.sum(d_normal, axis=0, keepdims=True)

    @pl.when(step == pl.num_programs(0) - 1)
    def _():
        for t in range(ffn_ref.shape[0]):
            chunk_o[t, 0:D, :] = tn(n4_sc[...], din_sc[t]).astype(BF16)
            chunk_o[t, D : 2 * D, :] = tn(g2_sc[...], act_sc[t]).astype(BF16)
            chunk_o[t, 2 * D :, :] = jnp.zeros((ROWS - 2 * D, D), BF16)


def backward_kernel(
    lens_ref, x0_ref, x1_ref, x2_ref, inner_ref, p_ref, q_ref, k_ref, v_ref, vp_ref, gp_ref, mid_ref,
    d3_ref, dn_ref, np_ref, bn_ref, small_ref, mix_ref, ffn_ref, n1_ref, n2_ref, n3_ref, act1_ref,
    mixture_ref, act3_ref, gc_ref, lng_ref,
    ig_o, chunk1_o, chunk2_o,
    pad_g, pad_m, gk_sc, dv_sc, dg_sc, ga_sc, dq_sc, dk_sc, dvv_sc, g1_sc, din_sc, lng_sc,
):
    step = pl.program_id(0)
    rows = pl.ds(pl.multiple_of(step * LEN, LEN), LEN)
    mask = row_mask(own_length(lens_ref, step))

    @pl.when(step == 0)
    def _():
        pad_g[...] = jnp.zeros_like(pad_g)
        pad_m[...] = jnp.zeros_like(pad_m)
        gk_sc[...] = jnp.zeros_like(gk_sc)
        lng_sc[...] = lng_ref[...]

    mean, inv_std, gain, bias, sum_gain, sum_bias, inv_count = [bn_ref[i : i + 1, :] for i in range(7)]
    xhat = (mid_ref[...] - mean) * inv_std
    d_mid = inv_std * gain * (dn_ref[...] - mask * ((sum_bias + xhat * sum_gain) * inv_count))
    value = vp_ref[...]
    sigma = sigmoid(gp_ref[...])
    gated = value * sigma * mask
    d_n3 = jnp.zeros((LEN, D), F32)
    for half in range(2):
        lanes = slice(half * 128, half * 128 + 128)
        pad_g[half, 8 : 8 + LEN, :] = gated[:, lanes]
        pad_m[half, 8 : 8 + LEN, :] = d_mid[:, lanes]
        d_gated = jnp.zeros((LEN, 128), F32)
        mid_half = d_mid[:, lanes]
        for j in range(KS):
            d_gated = d_gated + pad_m[half, 15 - j : 15 - j + LEN, :] * small_ref[j : j + 1, lanes]
            gk_sc[j : j + 1, lanes] += jnp.sum(
                pad_g[half, 1 + j : 1 + j + LEN, :] * mid_half, axis=0, keepdims=True
            )
        d_gated = d_gated * mask
        sig = sigma[:, lanes]
        dv_sc[rows, lanes] = (d_gated * sig).astype(BF16)
        dg_sc[rows, lanes] = (d_gated * value[:, lanes] * sig * (1.0 - sig)).astype(BF16)
    d_n3 = nn(dv_sc[rows, :], mix_ref[4]) + nn(dg_sc[rows, :], mix_ref[5])
    d2, gain2, bias2 = norm_back(x2_ref[...], np_ref[2, 0:1, :], d_n3)
    d2 = d2 + d3_ref[...]
    ga = d2.astype(BF16)
    ga_sc[rows, :] = ga
    d_mix = nt(ga, mix_ref[3]).astype(BF16)
    masks = lane_masks(BF16)
    for half in range(2):
        lanes = slice(half * 128, half * 128 + 128)
        q, k, v, dm = q_ref[:, lanes], k_ref[:, lanes], v_ref[:, lanes], d_mix[:, lanes]
        dq = jnp.zeros((LEN, 128), F32)
        dk = jnp.zeros((LEN, 128), F32)
        dv = jnp.zeros((LEN, 128), F32)
        for side in range(2):
            probs = p_ref[0, 2 * half + side]
            dm_side = dm * masks[side]
            d_probs = nt(dm_side, v)
            dv = dv + tn(probs.astype(BF16), dm_side)
            row_sum = jnp.sum(probs * d_probs, axis=-1, keepdims=True)
            d_scores = (probs * (d_probs - row_sum)).astype(BF16)
            dq = dq + nn(d_scores, k * masks[side])
            dk = dk + tn(d_scores, q * masks[side])
        dq_sc[rows, lanes] = (dq * HEAD ** (-0.5)).astype(BF16)
        dk_sc[rows, lanes] = (dk * HEAD ** (-0.5)).astype(BF16)
        dvv_sc[rows, lanes] = dv.astype(BF16)
    d_n2 = nn(dq_sc[rows, :], mix_ref[0]) + nn(dk_sc[rows, :], mix_ref[1]) + nn(dvv_sc[rows, :], mix_ref[2])
    d1, gain1, bias1 = norm_back(x1_ref[...], np_ref[1, 0:1, :], d_n2)
    d1 = d1 + d2
    g1 = (0.5 * d1).astype(BF16)
    g1_sc[rows, :] = g1
    d_n1 = ffn_backward(g1, inner_ref, ffn_ref, din_sc, rows)
    d0, gain0, bias0 = norm_back(x0_ref[...].astype(F32), np_ref[0, 0:1, :], d_n1)
    ig_o[...] = d0 + d1
    for i, part in enumerate((gain0, bias0, gain1, bias1, gain2, bias2)):
        lng_sc[i : i + 1, :] += part

    @pl.when(step == pl.num_programs(0) - 1)
    def _():
        shards = ffn_ref.shape[0]
        eye = (
            lax.broadcasted_iota(jnp.int32, (16, D), 0) == lax.broadcasted_iota(jnp.int32, (16, D), 1)
        ).astype(BF16)
        pairs = (
            (dq_sc[...], n2_ref[...]),
            (dk_sc[...], n2_ref[...]),
            (dvv_sc[...], n2_ref[...]),
            (mixture_ref[...], ga_sc[...]),
            (dv_sc[...], n3_ref[...]),
            (dg_sc[...], n3_ref[...]),
            (act3_ref[...], gc_ref[...]),
            (gk_sc[...].astype(BF16), eye),
        )
        for i, (left, right) in enumerate(pairs):
            full = tn(left, right).astype(BF16)
            for t in range(shards):
                chunk1_o[t, PADH * i : PADH * (i + 1), :] = full[PADH * t : PADH * (t + 1), :]
        for t in range(shards):
            chunk2_o[t, 0:D, :] = tn(n1_ref[...], din_sc[t]).astype(BF16)
            chunk2_o[t, D : 2 * D, :] = tn(g1_sc[...], act1_ref[t]).astype(BF16)
            chunk2_o[t, 2 * D : 2 * D + 16, :] = lng_sc[...].astype(BF16)
            chunk2_o[t, 2 * D + 16 :, :] = jnp.zeros((ROWS - 2 * D - 16, D), BF16)


def split(a):
    high = a.astype(BF16)
    return high, (a - high.astype(F32)).astype(BF16)


def mul_fine(a, b):
    a_high, a_low = a
    b_high, b_low = b
    return nn(a_high, b_high) + (nn(a_high, b_low) + nn(a_low, b_high))


def eye_of(n):
    return (lax.broadcasted_iota(jnp.int32, (n, n), 0) == lax.broadcasted_iota(jnp.int32, (n, n), 1)).astype(F32)


def next_gap(gap, eye, fine):
    if fine:
        own = split(gap)
        square = split(mul_fine(own, own))
        inner = mul_fine(square, split((15.0 / 256.0) * eye + (1.0 / 256.0) * gap))
        return mul_fine(square, split(0.625 * eye + 0.3125 * gap + inner))
    own = gap.astype(BF16)
    square = nn(own, own).astype(BF16)
    inner = nn(square, ((15.0 / 256.0) * eye + (1.0 / 256.0) * gap).astype(BF16))
    return nn(square, (0.625 * eye + 0.3125 * gap + inner).astype(BF16))


def total_of(a):
    return jnp.sum(jnp.sum(a, axis=1, keepdims=True), axis=0, keepdims=True)


def update_kernel(
    step_ref, tot_ref, red_ref, gbn_ref, fi_ref, fo_ref, ai_ref, ao_ref, ci_ref, dk_ref, co_ref,
    sw_ref, sh_ref, sd_ref, sk_ref, np_ref, ns_ref, bp_ref, bs_ref,
    gn_o, cn_o, cb_o, cfi_o, cfo_o, cai_o, cao_o, cci_o, cdk_o, cco_o,
    nfi_o, nfo_o, nai_o, nao_o, nci_o, ndk_o, nco_o, nn_o, nb_o, nns_o, nbs_o,
    nsw_o, nsh_o, nsd_o, nsk_o,
    gap_f, gap_b, dir_f, dir_b,
):
    steps = jnp.full((1, 1), step_ref[0], jnp.int32).astype(F32)
    rate = PEAK_RATE * jnp.minimum(steps / WARM_STEPS, jnp.sqrt(WARM_STEPS / steps))
    grad_norm = jnp.sqrt(tot_ref[0:1, 0:1])
    threshold = math.sqrt(NPARAM)
    factor = threshold / jnp.maximum(grad_norm, threshold)
    square_factor = factor * factor
    gn_o[...] = jnp.broadcast_to(grad_norm, gn_o.shape)

    c_norm = red_ref[2, 2 * D : 2 * D + 16, :].astype(F32) * factor
    for i in range(5):
        clipped = c_norm[2 * i : 2 * i + 2, :]
        second = 0.5 * ns_ref[i] + 0.5 * clipped * clipped
        cn_o[i] = clipped
        nns_o[i] = second
        nn_o[i] = np_ref[i] - rate * SMALL_RATE * clipped * lax.rsqrt(second)
    c_bn = gbn_ref[...] * factor
    second = 0.5 * bs_ref[...] + 0.5 * c_bn * c_bn
    cb_o[...] = c_bn
    nbs_o[...] = second
    nb_o[...] = bp_ref[...] - rate * SMALL_RATE * c_bn * lax.rsqrt(second)

    eye_d = eye_of(D)
    scales_f = []
    for i in range(4):
        member, is_out = i // 2, i % 2
        chunk = (2, 0)[member]
        low = red_ref[chunk, is_out * D : is_out * D + D, :]
        wide_c = sw_ref[0, 2 * is_out + member, 0:1, 0:1]
        hidden_c = sd_ref[0, 2 * is_out + member, 0:1, 0:1]
        gram = tn(low, low) * square_factor
        wide = nt(low, low) * square_factor
        nsw_o[0, 2 * is_out + member] = 0.5 * wide_c * eye_d + 0.5 * wide
        nsd_o[0, 2 * is_out + member] = 0.5 * hidden_c * eye_d + 0.5 * gram
        clipped = low.astype(F32) * factor
        if is_out:
            cfo_o[member] = clipped.T
        else:
            cfi_o[member] = clipped
        dir_f[i] = clipped
        trace = total_of(clipped * clipped)
        power = total_of(gram * gram)
        scale = 1.0
        for k, c in enumerate((wide_c, hidden_c)):
            zoom = 2.5 * lax.rsqrt(0.25 * c * c * D + 0.5 * c * trace + 0.25 * power)
            gap_f[2 * i + k] = eye_d - zoom * (0.5 * c * eye_d + 0.5 * gram)
            scale = scale * jnp.sqrt(jnp.sqrt(zoom))
        scales_f.append(scale)

    eye_b = eye_of(4 * PADH)
    row_block = lax.broadcasted_iota(jnp.int32, (4 * PADH, 1), 0) // PADH
    lane_block = lax.broadcasted_iota(jnp.int32, (1, 4 * PADH), 1) // PADH
    same_block = row_block == lane_block
    wide_of = (4, 5, 6, 7, 8, 9, 10, None)
    head_of = (0, 1, 2, 3, 4, 5, 7, 6)
    scales_b = []

    def spread(values):
        column = jnp.zeros((4 * PADH, 1), F32)
        for i, value in enumerate(values):
            column = jnp.where(row_block == i, value, column)
        return column

    for group in range(2):
        low = red_ref[1, group * 4 * PADH : (group + 1) * 4 * PADH, :]
        clipped = low.astype(F32) * factor
        dir_b[group] = clipped
        gram = jnp.where(same_block, nt(low, low), 0.0) * square_factor
        row_trace = jnp.sum(clipped * clipped, axis=1, keepdims=True)
        row_power = jnp.sum(gram * gram, axis=1, keepdims=True)
        wide_cs, head_cs, traces, powers, dims = [], [], [], [], []
        for i in range(4):
            index = group * 4 + i
            part = slice(i * PADH, (i + 1) * PADH)
            piece = low[part, :]
            head_c = sh_ref[0, head_of[index], 0:1, 0:1]
            own_gram = nt(piece, piece)[:HEAD, :HEAD] * square_factor
            nsh_o[0, head_of[index]] = 0.5 * head_c * eye_d[:HEAD, :HEAD] + 0.5 * own_gram
            wide = tn(piece, piece) * square_factor
            if wide_of[index] is None:
                wide_c = sk_ref[0, 0:1, 0:1]
                nsk_o[0] = 0.5 * wide_c * eye_d[:KS, :KS] + 0.5 * wide[:KS, :KS]
                dims.append(KS)
            else:
                wide_c = sw_ref[0, wide_of[index], 0:1, 0:1]
                nsw_o[0, wide_of[index]] = 0.5 * wide_c * eye_d + 0.5 * wide
                dims.append(D)
            wide_cs.append(wide_c)
            head_cs.append(head_c)
            traces.append(jnp.sum(row_trace[part], axis=0, keepdims=True))
            powers.append(jnp.sum(row_power[part], axis=0, keepdims=True))
        scale = [1.0] * 4
        for k, (cs, sizes) in enumerate(((wide_cs, dims), (head_cs, [HEAD] * 4))):
            zooms = [
                2.5 * lax.rsqrt(0.25 * c * c * n + 0.5 * c * trace + 0.25 * power)
                for c, n, trace, power in zip(cs, sizes, traces, powers)
            ]
            gap_b[2 * group + k] = eye_b - spread(zooms) * (0.5 * spread(cs) * eye_b + 0.5 * gram)
            scale = [s * jnp.sqrt(jnp.sqrt(zoom)) for s, zoom in zip(scale, zooms)]
        scales_b.append(scale)

    def advance(fine, last):
        for k in range(2):
            for i in range(4):
                gap = gap_f[2 * i + k]
                dir_f[i] = dir_f[i] + 0.25 * nn(dir_f[i].astype(BF16), gap.astype(BF16))
                if not last:
                    gap_f[2 * i + k] = next_gap(gap, eye_d, fine)
            for i in range(2):
                gap = gap_b[2 * i + k]
                dir_b[i] = dir_b[i] + 0.25 * nn(gap.astype(BF16), dir_b[i].astype(BF16))
                if not last:
                    gap_b[2 * i + k] = next_gap(gap, eye_b, fine)

    def fine_step(i, carry):
        advance(True, False)
        return carry

    def coarse_step(i, carry):
        advance(False, False)
        return carry

    lax.fori_loop(0, FINE_ITERS, fine_step, 0)
    lax.fori_loop(0, ROOT_ITERS - 1 - FINE_ITERS, coarse_step, 0)
    advance(False, True)

    def graft(weight, direction):
        size = jnp.sqrt(total_of(weight * weight))
        return rate * GRAFT_SCALE * size / (jnp.sqrt(total_of(direction * direction)) + 1e-06)

    for i in range(4):
        member, is_out = i // 2, i % 2
        direction = dir_f[i] * scales_f[i]
        weight = (fi_ref, fo_ref)[is_out][member]
        if is_out:
            direction = direction.T
        (nfi_o, nfo_o)[is_out][member] = weight - graft(weight, direction) * direction
    for index in range(8):
        group, i = index // 4, index % 4
        part = slice(i * PADH, i * PADH + HEAD)
        direction = dir_b[group][part, :] * scales_b[group][i]
        clipped = red_ref[1, index * PADH : (index + 1) * PADH, :][:HEAD, :].astype(F32) * factor
        if index in (3, 6):
            weight_ref, clip_o, new_o = ((ao_ref, cao_o, nao_o), None, None, (co_ref, cco_o, nco_o))[index - 3]
            clip_o[...] = clipped
            new_o[...] = weight_ref[...] - graft(weight_ref[...], direction) * direction
        elif index == 7:
            turned = direction.T[:KS, :]
            cdk_o[...] = clipped.T[:KS, :]
            ndk_o[...] = dk_ref[...] - graft(dk_ref[...], turned) * turned
        else:
            weight_ref, clip_o, new_o = (ai_ref, cai_o, nai_o) if index < 3 else (ci_ref, cci_o, nci_o)
            m = index if index < 3 else index - 4
            turned = direction.T
            clip_o[m] = clipped.T
            new_o[m] = weight_ref[m] - graft(weight_ref[m], turned) * turned


def shape(dims, dtype=F32):
    return jax.ShapeDtypeStruct(dims, dtype)


def whole(dims):
    zeros = (0,) * len(dims)
    return pl.BlockSpec(dims, lambda u: zeros)


def tile(width):
    return pl.BlockSpec((LEN, width), lambda u: (u, 0))


SMEM_SPEC = pl.BlockSpec(memory_space=pltpu.SMEM)
VMEM_SPEC = pl.BlockSpec(memory_space=pltpu.VMEM)
PARAMS = pltpu.CompilerParams(vmem_limit_bytes=VMEM_CAP)


def forward_call(lengths, x, norm_params, ffn, mix, small):
    frames = x.shape[0]
    shards = ffn.shape[0]
    utts = frames // LEN
    wide = 4 * PADH
    shard_tile = pl.BlockSpec((shards, LEN, D), lambda u: (0, u, 0))
    return pl.pallas_call(
        forward_kernel,
        grid=(utts,),
        in_specs=[SMEM_SPEC, tile(D), whole(norm_params.shape), whole(ffn.shape), whole(mix.shape), whole(small.shape)],
        out_specs=[
            tile(D), shard_tile, shard_tile, tile(D), tile(D), tile(wide), tile(wide), tile(wide),
            pl.BlockSpec((1, 4, LEN, LEN), lambda u: (u, 0, 0, 0)),
            tile(wide), tile(D), tile(D), tile(wide), tile(wide), tile(wide),
            pl.BlockSpec((1, 8, wide), lambda u: (u, 0, 0)),
        ],
        out_shape=[
            shape((frames, D), BF16), shape((shards, frames, D)), shape((shards, frames, D), BF16),
            shape((frames, D)), shape((frames, D), BF16),
            shape((frames, wide), BF16), shape((frames, wide), BF16), shape((frames, wide), BF16),
            shape((utts, 4, LEN, LEN)), shape((frames, wide), BF16), shape((frames, D)), shape((frames, D), BF16),
            shape((frames, wide)), shape((frames, wide)), shape((frames, wide)), shape((utts, 8, wide)),
        ],
        scratch_shapes=[pltpu.VMEM((2, LEN + 16, 128), F32)],
        compiler_params=PARAMS,
        name="forward_part",
    )(lengths, x, norm_params, ffn, mix, small)


def middle_call(lengths, mid, x2, cot, norm_params, bn, mix, ffn):
    frames = x2.shape[0]
    shards = ffn.shape[0]
    wide = 4 * PADH
    return pl.pallas_call(
        middle_kernel,
        grid=(frames // LEN,),
        in_specs=[
            SMEM_SPEC, tile(wide), tile(D), tile(D), whole(norm_params.shape), whole(bn.shape),
            whole(mix.shape), whole(ffn.shape),
        ],
        out_specs=[
            tile(D), tile(D), tile(wide), tile(wide), tile(D), whole((16, D)), whole((8, wide)),
            whole((shards, ROWS, D)),
        ],
        out_shape=[
            shape((frames, D), BF16), shape((frames, D)), shape((frames, wide)), shape((frames, wide), BF16),
            shape((frames, D), BF16), shape((16, D)), shape((8, wide)), shape((shards, ROWS, D), BF16),
        ],
        scratch_shapes=[
            pltpu.VMEM((shards, LEN, D), F32), pltpu.VMEM((shards, frames, D), BF16),
            pltpu.VMEM((shards, frames, D), BF16), pltpu.VMEM((frames, D), BF16), pltpu.VMEM((frames, D), BF16),
        ],
        compiler_params=PARAMS,
        name="middle_part",
    )(lengths, mid, x2, cot, norm_params, bn, mix, ffn)


def backward_call(lengths, tiles, small_args, wholes):
    x0, x1, x2, inner, probs, q, k, v, vp, gp, mid, d3, dn = tiles
    norm_params, bn, small, mix, ffn = small_args
    frames = x1.shape[0]
    shards = ffn.shape[0]
    wide = 4 * PADH
    half_pad = pltpu.VMEM((2, LEN + 16, 128), F32)
    wide_low = pltpu.VMEM((frames, wide), BF16)
    thin_low = pltpu.VMEM((frames, D), BF16)
    return pl.pallas_call(
        backward_kernel,
        grid=(frames // LEN,),
        in_specs=[
            SMEM_SPEC, tile(D), tile(D), tile(D),
            pl.BlockSpec((shards, LEN, D), lambda u: (0, u, 0)),
            pl.BlockSpec((1, 4, LEN, LEN), lambda u: (u, 0, 0, 0)),
            tile(wide), tile(wide), tile(wide), tile(wide), tile(wide), tile(wide), tile(D), tile(wide),
        ] + [whole(a.shape) for a in small_args] + [whole(a.shape) for a in wholes],
        out_specs=[tile(D), whole((shards, ROWS, D)), whole((shards, ROWS, D))],
        out_shape=[shape((frames, D)), shape((shards, ROWS, D), BF16), shape((shards, ROWS, D), BF16)],
        scratch_shapes=[
            half_pad, half_pad, pltpu.VMEM((16, wide), F32), wide_low, wide_low, thin_low,
            wide_low, wide_low, wide_low, thin_low, pltpu.VMEM((shards, frames, D), BF16), pltpu.VMEM((16, D), F32),
        ],
        compiler_params=PARAMS,
        name="backward_part",
    )(lengths, *tiles, *small_args, *wholes)


def update_call(step_count, total_square, reduced, gbn, weights, stats, norm_params, norm_second, bn_params, bn_second):
    stat_wide, stat_head, stat_hidden, stat_kernel = stats
    corner = lambda a: pl.BlockSpec((1, a.shape[1], 8, 128), lambda i: (0, 0, 0, 0))
    one = lambda a: whole(a.shape)
    n_stat = lambda a: whole(a.shape)
    out_arrays = [
        shape((1, 128)), norm_params, bn_params, *weights, *weights, norm_params, bn_params, norm_params, bn_params,
        stat_wide, stat_head, stat_hidden, stat_kernel,
    ]
    in_arrays = [total_square, reduced, gbn, *weights]
    wide = 4 * PADH
    return pl.pallas_call(
        update_kernel,
        grid=(1,),
        in_specs=[SMEM_SPEC] + [one(a) for a in in_arrays]
        + [corner(stat_wide), one(stat_head), corner(stat_hidden), one(stat_kernel)]
        + [one(a) for a in (norm_params, norm_second, bn_params, bn_second)],
        out_specs=[one(a) for a in out_arrays],
        out_shape=[shape(a.shape) for a in out_arrays],
        scratch_shapes=[
            pltpu.VMEM((8, D, D), F32), pltpu.VMEM((4, wide, wide), F32),
            pltpu.VMEM((4, D, D), F32), pltpu.VMEM((2, wide, D), F32),
        ],
        compiler_params=PARAMS,
        name="update_part",
    )(step_count, *in_arrays, *stats, norm_params, norm_second, bn_params, bn_second)


def pack_weights(ffn_in, ffn_out, attn_in, attn_out, conv_in, depth_kernel, conv_out, bn_params):
    ffn = [jnp.stack([ffn_in[m], ffn_out[m]]).astype(BF16) for m in range(2)]
    rows = jnp.concatenate(
        [attn_in.swapaxes(1, 2), attn_out[None], conv_in.swapaxes(1, 2), conv_out[None]]
    ).astype(BF16)
    mix = jnp.pad(rows, ((0, 0), (0, PADH - HEAD), (0, 0)))
    small = jnp.pad(
        jnp.concatenate([depth_kernel, jnp.zeros((1, HEAD), F32), bn_params]), ((0, 6), (0, PADH - HEAD))
    )
    return ffn[0], ffn[1], mix, small


def local(
    block_input, lengths, cotangent, norm_params, bn_params, ffn_in, ffn_out, attn_in, attn_out, conv_in,
    depth_kernel, conv_out, stat_wide, stat_head, stat_hidden, stat_kernel, norm_second, bn_second, step_count,
):
    ffn_one, ffn_two, mix, small = pack_weights(
        ffn_in, ffn_out, attn_in, attn_out, conv_in, depth_kernel, conv_out, bn_params
    )
    ffn_one, ffn_two = [lax.all_gather(a, "tensor") for a in (ffn_one, ffn_two)]
    mix = lax.all_gather(mix, "tensor", axis=1, tiled=True)
    small = lax.all_gather(small, "tensor", axis=1, tiled=True)
    (n1, inner1, act1, x1, n2, q, k, v, probs, mixture, x2, n3, vp, gp, mid, stat) = forward_call(
        lengths, block_input, norm_params, ffn_one, mix, small
    )
    count_here = jnp.sum(stat[:, 2, 0])
    mean_here = jnp.sum(stat[:, 0] * stat[:, 2], axis=0) / count_here
    power_here = jnp.sum(stat[:, 1] + stat[:, 2] * (stat[:, 0] - mean_here) ** 2, axis=0)
    count, first = lax.psum((count_here, mean_here * count_here), ("dp", "tensor"))
    mean = first / count
    power = lax.psum(power_here + count_here * (mean_here - mean) ** 2, ("dp", "tensor"))
    inv_std = lax.rsqrt(power / count + 1e-05)
    zero = jnp.zeros_like(mean)
    bn = jnp.stack([mean, inv_std, small[16], small[17], zero, zero, zero, zero])
    block_out, d3, dn, act3, gc, lng, gb, chunk0 = middle_call(
        lengths, mid, x2, cotangent, norm_params, bn, mix, ffn_two
    )
    gb = lax.psum(gb[:2], ("dp", "tensor"))
    bn = jnp.stack([mean, inv_std, small[16], small[17], gb[0], gb[1], zero + 1.0 / count, zero])
    input_grad, chunk1, chunk2 = backward_call(
        lengths,
        (block_input, x1, x2, inner1, probs, q, k, v, vp, gp, mid, d3, dn),
        (norm_params, bn, small, mix, ffn_one),
        (n1, n2, n3, act1, mixture, act3, gc, lng),
    )
    chunks = jnp.concatenate([chunk0, chunk1, chunk2], axis=1)
    chunks = lax.psum_scatter(chunks, "tensor", scatter_dimension=0, tiled=True)
    reduced = lax.psum(chunks, "dp").reshape(3, ROWS, D)
    gbn = lax.dynamic_slice(gb, (0, lax.axis_index("tensor") * PADH), (2, PADH))[:, :HEAD]
    high = reduced.astype(F32)
    norm_rows = high[2, 2 * D : 2 * D + 16]
    square = jnp.sum(high * high) - jnp.sum(norm_rows * norm_rows) + jnp.sum(gbn * gbn)
    square = lax.psum(square, "tensor") + jnp.sum(norm_rows * norm_rows)
    total_square = jnp.broadcast_to(square, (8, 128))
    weights = (ffn_in, ffn_out, attn_in, attn_out, conv_in, depth_kernel, conv_out)
    outs = update_call(
        step_count, total_square, reduced, gbn, weights, (stat_wide, stat_head, stat_hidden, stat_kernel),
        norm_params, norm_second, bn_params, bn_second,
    )
    return (block_out, input_grad, outs[0][0, :1], *outs[1:])


def solution(mesh):
    weights_specs = (
        P(None, None, "tensor"), P(None, "tensor", None), P(None, None, "tensor"), P("tensor", None),
        P(None, None, "tensor"), P(None, "tensor"), P("tensor", None),
    )
    stat_specs = (
        P("tensor", None, None, None), P("tensor", None, None, None), P("tensor", None, None, None),
        P("tensor", None, None),
    )
    frames = P(("dp", "tensor"), None)
    channels = P(None, "tensor")
    return jax.shard_map(
        local,
        mesh=mesh,
        in_specs=(frames, P("dp"), frames, P(), channels, *weights_specs, *stat_specs, P(), channels, P()),
        out_specs=(
            frames, frames, P(), P(), channels, *weights_specs, *weights_specs, P(), channels, P(), channels,
            *stat_specs,
        ),
        check_vma=False,
    )
```

time: 1320 us -> 424 us (0.32)
  waiting for transfers between devices: 741 us -> 110 us
  matrix products: 121 us -> 0 us
  other arithmetic: 125 us -> 14.8 us
  Pallas kernels: 0 us -> 93 us
  loops' own time: 73.3 us -> 0 us
  local copies, waits for them, and re-layouts: 84.5 us -> 22.8 us
  blocking collectives: 131 us -> 163 us
    psum x4 -> x1, waiting for transfers between devices: 392 us -> 72 us  [local(): reduced = lax.psum(chunks, 'dp').reshape(3, ROWS, D)]
    reduce_scatter x8 -> x1, waiting for transfers between devices: 218 us -> 38.3 us  [local(): chunks = lax.psum_scatter(chunks, 'tensor', scatter_dimension=0, tiled=True)]
    all_gather x8 -> x0, waiting for transfers between devices: 132 us -> none  [the longest x4 66.1 us: spread_grads(): lax.all_gather(gradient.astype(jnp.bfloat16), 'tensor', axis=0, tiled=True)]
    dot_general x163 -> x0, matrix products: 121 us -> none  [the longest x11 22.6 us: product_nt(): lax.dot_general(left_side, right_side, (((1,), (1,)), ((), ())), preferre...]
    pallas_call x0 -> x4, Pallas kernels: none -> 93 us  [the longest x1 47.8 us: update_call(): pl.pallas_call(update_kernel, grid=(1,), in_specs=[SMEM_SPEC] + [one(a) f...]
    another operation x12 -> x0, loops' own time: 73.3 us -> none  [owned_update(): return lax.cond(lax.axis_index('dp') == owner, compute, vacant, matrix_plan)]
    reduce_sum x36 -> x5, other arithmetic: 73.5 us -> 4.82 us  [the longest x1 2.14 us: local(): jnp.sum(high * high) - jnp.sum(norm_rows * norm_rows) + jnp.sum(gbn * gbn)]
    all_gather x0 -> x4, blocking collectives: none -> 37.7 us  [the longest x2 22.6 us: local(): ffn_one, ffn_two = [lax.all_gather(a, 'tensor') for a in (ffn_one, ffn_two)]]
  transfers between devices with their start and end apart: 20 -> 2, of which waited for: 20 -> 2; matrix products, arithmetic and copies ran while one was open for 3% -> 1% of each run, Pallas kernels for 0% -> 0%
where the time goes in v1:
time: 424 us; the launch traced here: 423 us
  blocking collectives  163 us (38%)
  waiting for transfers between devices  110 us (26%)
  Pallas kernels  93 us (22%)
  local copies, waits for them, and re-layouts  22.8 us (5%)
  between operations  18.9 us (4%)
  other arithmetic  14.8 us (3%)
    psum x1, waiting for transfers between devices, local(): reduced = lax.psum(chunks, 'dp').reshape(3, ROWS, D)  72 us
    pallas_call x1, Pallas kernels, update_call(): pl.pallas_call(update_kernel, grid=(1,), in_specs=[SMEM_SPEC] + [one(a) f...  47.8 us
    psum x1, blocking collectives, local(): lax.psum(power_here + count_here * (mean_here - mean) ** 2, ('dp', 'tenso...  40.6 us
    psum x1, blocking collectives, local(): lax.psum((count_here, mean_here * count_here), ('dp', 'tensor'))  40.4 us
    psum x1, blocking collectives, local(): gb = lax.psum(gb[:2], ('dp', 'tensor'))  38.4 us
    reduce_scatter x1, waiting for transfers between devices, local(): chunks = lax.psum_scatter(chunks, 'tensor', scatter_dimension=0, tiled=True)  38.3 us
    all_gather x2, blocking collectives, local(): ffn_one, ffn_two = [lax.all_gather(a, 'tensor') for a in (ffn_one, ffn_two)]  22.6 us
    pallas_call x1, Pallas kernels, backward_call(): pl.pallas_call(backward_kernel, grid=(frames // LEN,), in_specs=[SMEM_SPE...  19.3 us
  transfers between devices with their start and end apart: 2, of which 2 were waited for; matrix products, arithmetic and copies ran while one was open for 1% of the time, Pallas kernels for 0%

profile of v1, /device:TPU:0, one launch (start us, length us, event | category | flops | bytes accessed | tf_op | source)
XLA Modules:
  0.0 423.3 jit_solution(1196968072175069239)
XLA Ops:
  7.3 2.0 copy.86.x_ref.x0_ref
  11.6 11.7 %all_gather.14.ffn_ref = bf16[4,2,240,240]{3,2,1,0:T(8,128)(2,1)} all-gather(bf16[1,2,240,240]{3,2,1,0:T(8,128)(2,1)S(1)} %pad_maximum_fusion.1), channel_id=1, replica_groups=mesh['dp'=8,'tensor'=4] {'tensor'}, dimensions={0}, use_global_device_ids=true | all-gather | bytes 1152000 | tf_op jit(solution)/shard_map/all_gather | solution.py:662
  23.5 9.9 %all_gather.15.mix_ref = bf16[7,256,240]{2,1,0:T(8,128)(2,1)} all-gather(bf16[7,64,240]{2,1,0:T(8,128)(2,1)S(1)} %fusion.6), channel_id=1, replica_groups=mesh['dp'=8,'tensor'=4] {'tensor'}, dimensions={1}, use_global_device_ids=true | all-gather | bytes 1075200 | tf_op jit(solution)/shard_map/all_gather | solution.py:663
  33.5 5.2 %all-gather = f32[4,64,24]{1,2,0:T(8,128)S(1)} all-gather(f32[1,64,24]{1,2,0:T(8,128)S(1)} %pad_bitcast_fusion), channel_id=1, replica_groups=mesh['dp'=8,'tensor'=4] {'tensor'}, dimensions={0}, use_global_device_ids=true | all-gather | bytes 30720 | tf_op jit(solution)/shard_map/all_gather | solution.py:664
  39.5 14.1 %forward_part.1 = (bf16[768,240]{1,0:T(8,128)(2,1)}, f32[4,768,240]{2,1,0:T(8,128)}, bf16[4,768,240]{2,1,0:T(8,128)(2,1)}, f32[768,240]{1,0:T(8,128)}, bf16[768,...) custom-call(s32[16]{0:T(128)} %lens_ref.5, ...), custom_call_target="tpu_custom_call" | custom-call | tf_op jit(solution)/shard_map/forward_part/pallas_call | solution.py:535
  55.1 1.3 slice_reduce_fusion
  58.0 40.4 %all-reduce.2 = (f32[256]{0:T(256)S(1)}, f32[]{:T(128)}) all-reduce(f32[256]{0:T(256)S(1)} %get-tuple-element.216, f32[]{:T(128)} %slice_reduce_fusion), channel_id=1, replica_groups=mesh['dp'=8,'tensor'=4] {'dp','tensor'}, use_global_device_ids=true, to_apply=%region_2.3 | all-reduce | flops 257 | bytes 2056 | tf_op jit(solution)/shard_map/psum | solution.py:671
  99.7 40.6 %psum.44 = f32[256]{0:T(256)S(1)} all-reduce(f32[256]{0:T(256)S(1)} %get-tuple-element.214), channel_id=1, replica_groups=mesh['dp'=8,'tensor'=4] {'dp','tensor'}, use_global_device_ids=true, to_apply=%region_5.6 | all-reduce | flops 256 | bytes 2048 | tf_op jit(solution)/shard_map/psum | solution.py:673
  141.1 10.9 %all_gather.17.ffn_ref = bf16[4,2,240,240]{3,2,1,0:T(8,128)(2,1)} all-gather(bf16[1,2,240,240]{3,2,1,0:T(8,128)(2,1)S(1)} %pad_maximum_fusion.2), channel_id=1, replica_groups=mesh['dp'=8,'tensor'=4] {'tensor'}, dimensions={0}, use_global_device_ids=true | all-gather | bytes 1152000 | tf_op jit(solution)/shard_map/all_gather | solution.py:662
  152.7 11.8 %middle_part.1 = (bf16[768,240]{1,0:T(8,128)(2,1)}, f32[768,240]{1,0:T(8,128)}, f32[768,256]{1,0:T(8,128)}, bf16[768,256]{1,0:T(8,128)(2,1)}, bf16[768,240]{1,0:...) custom-call(s32[16]{0:T(128)} %lens_ref.5, ...), custom_call_target="tpu_custom_call" | custom-call | tf_op jit(solution)/shard_map/middle_part/pallas_call | solution.py:562
  165.2 38.4 %psum.45 = f32[2,256]{1,0:T(2,128)S(1)} all-reduce(f32[2,256]{1,0:T(2,128)S(1)} %slice.65), channel_id=1, replica_groups=mesh['dp'=8,'tensor'=4] {'dp','tensor'}, use_global_device_ids=true, to_apply=%region_6.7 | all-reduce | flops 512 | bytes 4096 | tf_op jit(solution)/shard_map/psum | solution.py:680
  204.9 19.3 %backward_part.1 = (f32[768,240]{1,0:T(8,128)}, bf16[4,512,240]{2,1,0:T(8,128)(2,1)}, bf16[4,512,240]{2,1,0:T(8,128)(2,1)}) custom-call(s32[16]{0:T(128)} %lens_ref.5, bf16[768,240]{1,0:T(8,128)(2,1)} %copy.86.x_ref.x0_ref, f32[768,240]{1,0:T(8,128)} %get-tuple-element.83.x1_ref, f32[768,240]{1,0:T(8,128)} %get-tuple-element.80.x2_ref, ...), custom_call_target="tpu_custom_call" | custom-call | tf_op jit(solution)/shard_map/backward_part/pallas_call | solution.py:595
  224.2 3.1 pad_maximum_fusion
  227.4 38.3 %reduce-scatter.2.cloned.1.call-done = bf16[1,1536,240]{2,1,0:T(8,128)(2,1)} async-done(((bf16[4,1536,240]{2,1,0:T(8,128)(2,1)}), bf16[1,1536,240]{2,1,0:T(8,128)(2,1)}) %reduce-scatter.2.cloned.1.call-update) | async-done | bytes 737296 | tf_op jit(solution)/shard_map/reduce_scatter | solution.py:689
  272.2 72.0 %all-reduce.5.cloned.1.call-done = bf16[1,1536,240]{2,1,0:T(8,128)(2,1)} async-done(((bf16[1,1536,240]{2,1,0:T(8,128)(2,1)}), bf16[1,1536,240]{2,1,0:T(8,128)(2,1)}) %all-reduce.5.cloned.1.call-update) | async-done | bytes 737296 | tf_op jit(solution)/shard_map/psum | solution.py:690
  344.2 1.3 multiply_reduce_fusion.1
  345.5 2.1 multiply_reduce_fusion
  350.2 6.4 %psum.47 = f32[]{:T(128)} all-reduce(f32[]{:T(128)S(6)} %add.45), channel_id=1, replica_groups=mesh['dp'=8,'tensor'=4] {'tensor'}, use_global_device_ids=true, to_apply=%region_12.13 | all-reduce | flops 1 | bytes 8 | tf_op jit(solution)/shard_map/psum | solution.py:695
  358.4 47.8 %update_part.1 = (f32[1,128]{1,0:T(1,128)}, f32[5,2,240]{2,1,0:T(2,128)}, f32[2,60]{1,0:T(2,128)}, f32[2,240,240]{2,1,0:T(8,128)}, f32[2,240,240]{2,1,0:T(8,128)...) custom-call(s32[1]{0:T(128)S(6)} %copy.108.step_ref, ...), custom_call_target="tpu_custom_call" | custom-call | tf_op jit(solution)/shard_map/update_part/pallas_call | solution.py:626
  406.2 1.8 copy.97
  408.1 1.7 copy.98
  409.8 1.8 copy.99
  411.6 1.7 copy.100
  413.3 1.8 copy.101
  (71 shorter events, 18.9 us)
Async XLA Ops:
  7.2 16.1 %copy-start.3 = (f32[2,240,60]{1,0,2:T(2,128)S(1)}, f32[2,240,60]{1,0,2:T(2,128)}, u32[]{:S(2)}) copy-start(f32[2,240,60]{1,0,2:T(2,128)} %param.28) | copy-start | bytes 345604
  7.2 16.2 %copy-start.2 = (f32[3,240,60]{1,2,0:T(8,128)S(1)}, f32[3,240,60]{1,2,0:T(8,128)}, u32[]{:S(2)}) copy-start(f32[3,240,60]{1,2,0:T(8,128)} %param.26) | copy-start | bytes 518404
  7.2 16.2 %copy-start.6 = (f32[60,240]{1,0:T(8,128)S(1)}, f32[60,240]{1,0:T(8,128)}, u32[]{:S(2)}) copy-start(f32[60,240]{1,0:T(8,128)} %co_ref.1) | copy-start | bytes 172804
  7.2 16.2 %copy-start.7 = (f32[60,240]{1,0:T(8,128)S(1)}, f32[60,240]{1,0:T(8,128)}, u32[]{:S(2)}) copy-start(f32[60,240]{1,0:T(8,128)} %ao_ref.1) | copy-start | bytes 172804
  7.2 258.4 %reduce-scatter.2.cloned.1.call-start = ((), (), s32[]{:S(2)}) async-start(), calls=%async_computation.1 | async-start | bytes 3932160 | tf_op jit(solution)/shard_map/reduce_scatter | solution.py:689
  9.3 24.1 %copy-start.10 = (f32[15,60]{1,0:T(8,128)S(1)}, f32[15,60]{1,0:T(8,128)}, u32[]{:S(2)}) copy-start(f32[15,60]{1,0:T(8,128)} %dk_ref.1) | copy-start | bytes 10804
  9.3 24.1 %copy-start.12 = (f32[2,60]{1,0:T(2,128)S(1)}, f32[2,60]{1,0:T(2,128)}, u32[]{:S(2)}) copy-start(f32[2,60]{1,0:T(2,128)} %bp_ref.1) | copy-start | bytes 1444
  11.6 44.9 %copy-start.5 = (bf16[768,240]{0,1:T(8,128)(2,1)S(1)}, bf16[768,240]{0,1:T(8,128)(2,1)}, u32[]{:S(2)}) copy-start(bf16[768,240]{0,1:T(8,128)(2,1)} %param.21) | copy-start | bytes 1105924
  38.9 0.6 copy-start.9
  204.9 19.3 %copy-start = (bf16[4,512,240]{2,1,0:T(8,128)(2,1)S(1)}, bf16[4,512,240]{2,1,0:T(8,128)(2,1)}, u32[]{:S(2)}) copy-start(bf16[4,512,240]{2,1,0:T(8,128)(2,1)} %get-tuple-element.103) | copy-start | bytes 2949124
  227.3 40.1 %copy-start.4 = (bf16[768,240]{1,0:T(8,128)(2,1)S(1)}, bf16[768,240]{1,0:T(8,128)(2,1)}, u32[]{:S(2)}) copy-start(bf16[768,240]{1,0:T(8,128)(2,1)} %get-tuple-element.185) | copy-start | bytes 1105924
  227.3 41.1 %copy-start.1 = (f32[768,240]{1,0:T(8,128)S(1)}, f32[768,240]{1,0:T(8,128)}, u32[]{:S(2)}) copy-start(f32[768,240]{1,0:T(8,128)} %get-tuple-element.186) | copy-start | bytes 2211844
  227.3 42.8 %copy-start.8 = (f32[1,8,60,60]{3,1,2,0:T(8,128)S(1)}, f32[1,8,60,60]{3,1,2,0:T(8,128)}, u32[]{:S(2)}) copy-start(f32[1,8,60,60]{3,1,2,0:T(8,128)} %param.32) | copy-start | bytes 345604
  227.4 122.2 %copy-start.11 = (f32[1,15,15]{2,0,1:T(1,128)S(1)}, f32[1,15,15]{2,0,1:T(1,128)}, u32[]{:S(2)}) copy-start(f32[1,15,15]{2,0,1:T(1,128)} %param.34) | copy-start | bytes 2704
  227.4 116.8 %all-reduce.5.cloned.1.call-start = ((), (), s32[]{:S(2)}) async-start(), calls=%async_computation.2 | async-start | bytes 1572864 | tf_op jit(solution)/shard_map/psum | solution.py:690
Sparse Core Ops, SparseCore 0:
  227.5 38.1 reduce-scatter.1
  269.1 75.0 all-reduce.4

commit v2 on v1

--- a/solution.py
+++ b/solution.py
@@ -366,7 +366,7 @@
         cn_o[i] = clipped
         nns_o[i] = second
         nn_o[i] = np_ref[i] - rate * SMALL_RATE * clipped * lax.rsqrt(second)
-    c_bn = gbn_ref[...] * factor
+    c_bn = gbn_ref[0:2, 0:HEAD] * factor
     second = 0.5 * bs_ref[...] + 0.5 * c_bn * c_bn
     cb_o[...] = c_bn
     nbs_o[...] = second
@@ -425,13 +425,13 @@
             index = group * 4 + i
             part = slice(i * PADH, (i + 1) * PADH)
             piece = low[part, :]
-            head_c = sh_ref[0, head_of[index], 0:1, 0:1]
+            head_c = sh_ref[0, 0, head_of[index] : head_of[index] + 1, 0:1]
             own_gram = nt(piece, piece)[:HEAD, :HEAD] * square_factor
-            nsh_o[0, head_of[index]] = 0.5 * head_c * eye_d[:HEAD, :HEAD] + 0.5 * own_gram
+            nsh_o[0, :, head_of[index], :] = 0.5 * head_c * eye_d[:HEAD, :HEAD] + 0.5 * own_gram
             wide = tn(piece, piece) * square_factor
             if wide_of[index] is None:
                 wide_c = sk_ref[0, 0:1, 0:1]
-                nsk_o[0] = 0.5 * wide_c * eye_d[:KS, :KS] + 0.5 * wide[:KS, :KS]
+                nsk_o[:, 0, :] = 0.5 * wide_c * eye_d[:KS, :KS] + 0.5 * wide[:KS, :KS]
                 dims.append(KS)
             else:
                 wide_c = sw_ref[0, wide_of[index], 0:1, 0:1]
@@ -502,10 +502,10 @@
             ndk_o[...] = dk_ref[...] - graft(dk_ref[...], turned) * turned
         else:
             weight_ref, clip_o, new_o = (ai_ref, cai_o, nai_o) if index < 3 else (ci_ref, cci_o, nci_o)
-            m = index if index < 3 else index - 4
-            turned = direction.T
-            clip_o[m] = clipped.T
-            new_o[m] = weight_ref[m] - graft(weight_ref[m], turned) * turned
+            at = (index,) if index < 3 else (slice(None), index - 4)
+            weight = weight_ref[at]
+            clip_o[at] = clipped
+            new_o[at] = weight - graft(weight, direction) * direction
 
 
 def shape(dims, dtype=F32):
@@ -640,65 +640,361 @@
     )(step_count, *in_arrays, *stats, norm_params, norm_second, bn_params, bn_second)
 
 
-def pack_weights(ffn_in, ffn_out, attn_in, attn_out, conv_in, depth_kernel, conv_out, bn_params):
-    ffn = [jnp.stack([ffn_in[m], ffn_out[m]]).astype(BF16) for m in range(2)]
-    rows = jnp.concatenate(
-        [attn_in.swapaxes(1, 2), attn_out[None], conv_in.swapaxes(1, 2), conv_out[None]]
-    ).astype(BF16)
-    mix = jnp.pad(rows, ((0, 0), (0, PADH - HEAD), (0, 0)))
-    small = jnp.pad(
-        jnp.concatenate([depth_kernel, jnp.zeros((1, HEAD), F32), bn_params]), ((0, 6), (0, PADH - HEAD))
+MESH = pl.DeviceIdType.MESH
+
+
+def flip(index, bit):
+    step = 2 ** bit
+    return index + step - 2 * step * ((index // step) % 2)
+
+
+def greet(peers):
+    barrier = pltpu.get_barrier_semaphore()
+    for peer in peers:
+        pl.semaphore_signal(barrier, inc=1, device_id=peer, device_id_type=MESH)
+    pl.semaphore_wait(barrier, len(peers))
+
+
+def bits_of(count):
+    bits = count.bit_length() - 1
+    if 2 ** bits != count:
+        raise ValueError("axis size")
+    return bits
+
+
+def gather_kernel(
+    fi_ref, fo_ref, ai_ref, ao_ref, ci_ref, co_ref, dk_ref, bp_ref,
+    ffn1_o, mix_o, ffn2_o, small_o,
+    small_sc, send_sem, recv_sem,
+):
+    t = lax.axis_index("tensor")
+    near, far = flip(t, 0), flip(t, 1)
+    own = pl.ds(pl.multiple_of(t * PADH, PADH), PADH)
+    parts = (
+        lambda i: small_sc.at[i],
+        lambda i: ffn1_o.at[i],
+        lambda i: mix_o.at[:, pl.ds(pl.multiple_of(i * PADH, PADH), PADH), :],
+        lambda i: ffn2_o.at[i],
     )
-    return ffn[0], ffn[1], mix, small
+
+    def copy(part, shard, peer, slot):
+        return pltpu.make_async_remote_copy(
+            src_ref=part(shard), dst_ref=part(shard), send_sem=send_sem.at[slot], recv_sem=recv_sem.at[slot],
+            device_id={"tensor": peer}, device_id_type=MESH,
+        )
+
+    small_sc[t] = jnp.zeros((24, 128), F32)
+    small_sc[t, 0:KS, 0:HEAD] = dk_ref[...]
+    small_sc[t, 16:18, 0:HEAD] = bp_ref[...]
+    for m, target in enumerate((ffn1_o, ffn2_o)):
+        target[t, 0] = fi_ref[m].astype(BF16)
+        target[t, 1] = fo_ref[m].astype(BF16)
+    blank = jnp.zeros((PADH - HEAD, D), F32)
+    pieces = [ai_ref[m] for m in range(3)] + [ao_ref[...]] + [ci_ref[:, m, :] for m in range(2)] + [co_ref[...]]
+    for i, piece in enumerate(pieces):
+        mix_o[i, own, :] = jnp.concatenate([piece, blank], axis=0).astype(BF16)
+    greet([{"tensor": peer} for peer in (near, far)])
+    flights = []
+    for g, part in enumerate(parts):
+        flights.append((copy(part, t, far, 3 * g), copy(part, t, near, 3 * g + 1)))
+        flights[g][0].start()
+        flights[g][1].start()
+    passes = []
+    for g, part in enumerate(parts):
+        flights[g][0].wait()
+        passes.append(copy(part, far, near, 3 * g + 2))
+        passes[g].start()
+    for g in range(len(parts)):
+        flights[g][1].wait()
+        passes[g].wait()
+    for i in range(2):
+        small_o[:, 128 * i : 128 * i + PADH] = small_sc[2 * i, :, 0:PADH]
+        small_o[:, 128 * i + PADH : 128 * i + 128] = small_sc[2 * i + 1, :, 0:PADH]
+
+
+def gather_call(ffn_in, ffn_out, attn_in, attn_out, conv_in, conv_out, depth_kernel, bn_params):
+    shards = lax.axis_size("tensor")
+    wide = 4 * PADH
+    return pl.pallas_call(
+        gather_kernel,
+        in_specs=[VMEM_SPEC] * 8,
+        out_specs=[VMEM_SPEC] * 4,
+        out_shape=[
+            shape((shards, 2, D, D), BF16), shape((7, wide, D), BF16), shape((shards, 2, D, D), BF16),
+            shape((24, wide)),
+        ],
+        scratch_shapes=[
+            pltpu.VMEM((shards, 24, 128), F32), pltpu.SemaphoreType.DMA((12,)), pltpu.SemaphoreType.DMA((12,)),
+        ],
+        compiler_params=pltpu.CompilerParams(collective_id=0, has_side_effects=True, vmem_limit_bytes=VMEM_CAP),
+        name="gather_part",
+    )(ffn_in, ffn_out, attn_in, attn_out, conv_in, conv_out, depth_kernel, bn_params)
+
+
+def share(axis, count, slots, send_sem, recv_sem):
+    me = lax.axis_index(axis)
+
+    def copy(slot, peer, sent):
+        return pltpu.make_async_remote_copy(
+            src_ref=slots.at[slot], dst_ref=slots.at[slot], send_sem=send_sem.at[sent], recv_sem=recv_sem.at[slot],
+            device_id={axis: peer}, device_id_type=MESH,
+        )
+
+    def start(k, carry):
+        peer = lax.rem(me + k, count)
+        copy(me, peer, peer).start()
+        return carry
+
+    def finish(k, carry):
+        peer = lax.rem(me + k, count)
+        copy(me, peer, peer).wait_send()
+        copy(peer, peer, peer).wait_recv()
+        return carry
+
+    lax.fori_loop(1, count, start, 0)
+    lax.fori_loop(1, count, finish, 0)
+
+
+def greet_axes(counts):
+    barrier = pltpu.get_barrier_semaphore()
+    for axis, count in counts:
+        me = lax.axis_index(axis)
+
+        def signal(k, carry, axis=axis, count=count, me=me):
+            pl.semaphore_signal(
+                barrier, inc=1, device_id={axis: lax.rem(me + k, count)}, device_id_type=MESH
+            )
+            return carry
+
+        lax.fori_loop(1, count, signal, 0)
+    pl.semaphore_wait(barrier, sum(count - 1 for axis, count in counts))
+
+
+def pool(slots, count):
+    total = lax.fori_loop(0, count, lambda i, a: a + slots[i, 2:3, :], jnp.zeros((1, 4 * PADH), F32))
+    mean = (
+        lax.fori_loop(0, count, lambda i, a: a + slots[i, 0:1, :] * slots[i, 2:3, :], jnp.zeros((1, 4 * PADH), F32))
+        / total
+    )
+
+    def power(i, a):
+        off = slots[i, 0:1, :] - mean
+        return a + slots[i, 1:2, :] + slots[i, 2:3, :] * off * off
+
+    return mean, lax.fori_loop(0, count, power, jnp.zeros((1, 4 * PADH), F32)), total
+
+
+def moments_kernel(counts, st_ref, small_ref, bn_o, dp_sc, tensor_sc, *sems):
+    held = pool(st_ref, st_ref.shape[0])
+    slots_of = {"dp": dp_sc, "tensor": tensor_sc}
+    greet_axes(counts)
+    for i, (axis, count) in enumerate(counts):
+        slots = slots_of[axis]
+        me = lax.axis_index(axis)
+        for row, value in enumerate(held):
+            slots[me, row : row + 1, :] = value
+        share(axis, count, slots, sems[2 * i], sems[2 * i + 1])
+        held = pool(slots, count)
+    mean, power, total = held
+    bn_o[0:1, :] = mean
+    bn_o[1:2, :] = lax.rsqrt(power / total + 1e-05)
+    bn_o[2:4, :] = small_ref[16:18, :]
+    bn_o[4:6, :] = jnp.zeros((2, 4 * PADH), F32)
+    bn_o[6:7, :] = 1.0 / total
+    bn_o[7:8, :] = jnp.zeros((1, 4 * PADH), F32)
+
+
+def totals_kernel(counts, gb_ref, bn_ref, bn_o, dp_sc, tensor_sc, *sems):
+    held = gb_ref[...]
+    slots_of = {"dp": dp_sc, "tensor": tensor_sc}
+    greet_axes(counts)
+    for i, (axis, count) in enumerate(counts):
+        slots = slots_of[axis]
+        slots[lax.axis_index(axis)] = held
+        share(axis, count, slots, sems[2 * i], sems[2 * i + 1])
+        held = lax.fori_loop(1, count, lambda i, a: a + slots[i], slots[0])
+    bn_o[0:4, :] = bn_ref[0:4, :]
+    bn_o[4:6, :] = held[0:2, :]
+    bn_o[6:8, :] = bn_ref[6:8, :]
+
+
+def exchange_call(kernel, collective_id, name, *operands):
+    counts = tuple((axis, lax.axis_size(axis)) for axis in ("dp", "tensor"))
+    wide = 4 * PADH
+    return pl.pallas_call(
+        functools.partial(kernel, counts),
+        in_specs=[VMEM_SPEC] * len(operands),
+        out_specs=VMEM_SPEC,
+        out_shape=shape((8, wide)),
+        scratch_shapes=[pltpu.VMEM((count, 8, wide), F32) for axis, count in counts]
+        + [pltpu.SemaphoreType.DMA((count,)) for axis, count in counts for side in range(2)],
+        compiler_params=pltpu.CompilerParams(collective_id=collective_id, has_side_effects=True),
+        name=name,
+    )(*operands)
+
+
+def reduce_kernel(
+    dp_count, c0_ref, c1_ref, c2_ref, bn_ref, red_o, tot_o, gbn_o,
+    acc, near_sc, far_sc, dp_sc, out, norm_sc, send_sem, recv_sem, nsend_sem, nrecv_sem,
+):
+    chunks = (c0_ref, c1_ref, c2_ref)
+    t, d = lax.axis_index("tensor"), lax.axis_index("dp")
+    near, far = flip(t, 0), flip(t, 1)
+    bits = bits_of(dp_count)
+    greet(
+        [{"tensor": near}, {"tensor": far}, {"tensor": flip(near, 1)}] + [{"dp": flip(d, bit)} for bit in range(bits)]
+    )
+    plan = []
+    length = ROWS
+    for bit in range(bits):
+        halved = length % 32 == 0
+        plan.append((bit, length, halved))
+        length = length // 2 if halved else length
+    width = 3 + 2 * bits
+
+    def copy(src, dst, chunk, slot, peer):
+        return pltpu.make_async_remote_copy(
+            src_ref=src, dst_ref=dst, send_sem=send_sem.at[chunk, slot], recv_sem=recv_sem.at[chunk, slot],
+            device_id=peer, device_id_type=MESH,
+        )
+
+    def add(target, other):
+        return (target.astype(F32) + other.astype(F32)).astype(BF16)
+
+    def chain(c):
+        source = chunks[c]
+        flights = [
+            copy(source.at[near], near_sc.at[c, 0], c, 0, {"tensor": near}),
+            copy(source.at[flip(near, 1)], near_sc.at[c, 1], c, 1, {"tensor": near}),
+        ]
+        for flight in flights:
+            flight.start()
+        yield
+        for flight in flights[::-1]:
+            flight.wait()
+        acc[c, 1] = add(source[far], near_sc[c, 1])
+        flight = copy(acc.at[c, 1], far_sc.at[c], c, 2, {"tensor": far})
+        flight.start()
+        acc[c, 0] = add(source[t], near_sc[c, 0])
+        yield
+        flight.wait()
+        acc[c, 0] = add(acc[c, 0], far_sc[c])
+        offset = 0
+        trail = []
+        for bit, length, halved in plan:
+            peer = {"dp": flip(d, bit)}
+            slot = 3 + bit
+            landing = dp_sc.at[c, bit, pl.ds(0, length // 2 if halved else length)]
+            if halved:
+                half = length // 2
+                side = (d // 2 ** bit) % 2
+                keep = pl.ds(pl.multiple_of(offset + side * half, 16), half)
+                give = pl.ds(pl.multiple_of(offset + (1 - side) * half, 16), half)
+                trail.append((bit, offset))
+                offset = offset + side * half
+            else:
+                half = length
+                keep = give = pl.ds(pl.multiple_of(offset, 16), half)
+            flight = copy(acc.at[c, 0, give], landing, c, slot, peer)
+            flight.start()
+            yield
+            flight.wait()
+            acc[c, 0, keep] = add(acc[c, 0, keep], dp_sc[c, bit, 0:half])
+        size = plan[-1][1] // 2 if plan and plan[-1][2] else (plan[-1][1] if plan else ROWS)
+        here = pl.ds(pl.multiple_of(offset, 16), size)
+        out[c, here] = acc[c, 0, here]
+        for bit, before in trail[::-1]:
+            here = pl.ds(pl.multiple_of(offset, 16), size)
+            flight = copy(out.at[c, here], out.at[c, here], c, 3 + bits + bit, {"dp": flip(d, bit)})
+            flight.start()
+            yield
+            flight.wait()
+            offset = before
+            size = size * 2
+
+    live = [chain(c) for c in range(len(chunks))]
+    for step in range(2 + 2 * bits + len(chunks)):
+        for c in range(min(step + 1, len(chunks))):
+            next(live[c], None)
+
+    def square_of(a):
+        a = a.astype(F32)
+        return total_of(a * a)
+
+    own_block = lax.broadcasted_iota(jnp.int32, (1, 4 * PADH), 1) // PADH == t
+    gb = bn_ref[4:6, :]
+    gbn_o[...] = jnp.zeros_like(gbn_o)
+    for i in range(4):
+        @pl.when(t == i)
+        def _():
+            gbn_o[0:2, 0:PADH] = gb[:, i * PADH : (i + 1) * PADH]
+
+    square = square_of(out[0]) + square_of(out[1]) + square_of(out[2, 0 : 2 * D])
+    square = square + total_of(jnp.where(own_block, gb * gb, 0.0))
+    norm_sc[t] = jnp.broadcast_to(square, (8, 128))
+    share("tensor", 4, norm_sc, nsend_sem, nrecv_sem)
+    total = norm_sc[0] + norm_sc[1] + norm_sc[2] + norm_sc[3]
+    tot_o[...] = total + jnp.broadcast_to(square_of(out[2, 2 * D : 2 * D + 16]), (8, 128))
+    red_o[...] = out[...]
+
+
+def reduce_call(chunks, bn):
+    dp_count = lax.axis_size("dp")
+    bits = bits_of(dp_count)
+    width = 3 + 2 * bits
+    low = lambda *dims: pltpu.VMEM(dims + (ROWS, D), BF16)
+    dma = pltpu.SemaphoreType.DMA
+    return pl.pallas_call(
+        functools.partial(reduce_kernel, dp_count),
+        in_specs=[VMEM_SPEC] * 4,
+        out_specs=[VMEM_SPEC] * 3,
+        out_shape=[shape((3, ROWS, D), BF16), shape((8, 128)), shape((8, 128))],
+        scratch_shapes=[
+            low(3, 2), low(3, 2), low(3), pltpu.VMEM((3, bits, ROWS // 2, D), BF16), low(3),
+            pltpu.VMEM((4, 8, 128), F32), dma((3, width)), dma((3, width)), dma((4,)), dma((4,)),
+        ],
+        compiler_params=pltpu.CompilerParams(collective_id=3, has_side_effects=True, vmem_limit_bytes=VMEM_CAP),
+        name="reduce_part",
+    )(*chunks, bn)
 
 
 def local(
     block_input, lengths, cotangent, norm_params, bn_params, ffn_in, ffn_out, attn_in, attn_out, conv_in,
     depth_kernel, conv_out, stat_wide, stat_head, stat_hidden, stat_kernel, norm_second, bn_second, step_count,
 ):
-    ffn_one, ffn_two, mix, small = pack_weights(
-        ffn_in, ffn_out, attn_in, attn_out, conv_in, depth_kernel, conv_out, bn_params
+    attn_in, conv_in = attn_in.swapaxes(1, 2), conv_in.transpose(2, 0, 1)
+    stat_head, stat_kernel = stat_head.swapaxes(1, 2), stat_kernel.swapaxes(0, 1)
+    ffn_one, mix, ffn_two, small = gather_call(
+        ffn_in, ffn_out, attn_in, attn_out, conv_in, conv_out, depth_kernel, bn_params
     )
-    ffn_one, ffn_two = [lax.all_gather(a, "tensor") for a in (ffn_one, ffn_two)]
-    mix = lax.all_gather(mix, "tensor", axis=1, tiled=True)
-    small = lax.all_gather(small, "tensor", axis=1, tiled=True)
     (n1, inner1, act1, x1, n2, q, k, v, probs, mixture, x2, n3, vp, gp, mid, stat) = forward_call(
         lengths, block_input, norm_params, ffn_one, mix, small
     )
-    count_here = jnp.sum(stat[:, 2, 0])
-    mean_here = jnp.sum(stat[:, 0] * stat[:, 2], axis=0) / count_here
-    power_here = jnp.sum(stat[:, 1] + stat[:, 2] * (stat[:, 0] - mean_here) ** 2, axis=0)
-    count, first = lax.psum((count_here, mean_here * count_here), ("dp", "tensor"))
-    mean = first / count
-    power = lax.psum(power_here + count_here * (mean_here - mean) ** 2, ("dp", "tensor"))
-    inv_std = lax.rsqrt(power / count + 1e-05)
-    zero = jnp.zeros_like(mean)
-    bn = jnp.stack([mean, inv_std, small[16], small[17], zero, zero, zero, zero])
+    bn = exchange_call(moments_kernel, 1, "moments_part", stat, small)
     block_out, d3, dn, act3, gc, lng, gb, chunk0 = middle_call(
         lengths, mid, x2, cotangent, norm_params, bn, mix, ffn_two
     )
-    gb = lax.psum(gb[:2], ("dp", "tensor"))
-    bn = jnp.stack([mean, inv_std, small[16], small[17], gb[0], gb[1], zero + 1.0 / count, zero])
+    bn = exchange_call(totals_kernel, 2, "totals_part", gb, bn)
     input_grad, chunk1, chunk2 = backward_call(
         lengths,
         (block_input, x1, x2, inner1, probs, q, k, v, vp, gp, mid, d3, dn),
         (norm_params, bn, small, mix, ffn_one),
         (n1, n2, n3, act1, mixture, act3, gc, lng),
     )
-    chunks = jnp.concatenate([chunk0, chunk1, chunk2], axis=1)
-    chunks = lax.psum_scatter(chunks, "tensor", scatter_dimension=0, tiled=True)
-    reduced = lax.psum(chunks, "dp").reshape(3, ROWS, D)
-    gbn = lax.dynamic_slice(gb, (0, lax.axis_index("tensor") * PADH), (2, PADH))[:, :HEAD]
-    high = reduced.astype(F32)
-    norm_rows = high[2, 2 * D : 2 * D + 16]
-    square = jnp.sum(high * high) - jnp.sum(norm_rows * norm_rows) + jnp.sum(gbn * gbn)
-    square = lax.psum(square, "tensor") + jnp.sum(norm_rows * norm_rows)
-    total_square = jnp.broadcast_to(square, (8, 128))
+    reduced, total_square, gbn = reduce_call((chunk0, chunk1, chunk2), bn)
     weights = (ffn_in, ffn_out, attn_in, attn_out, conv_in, depth_kernel, conv_out)
-    outs = update_call(
-        step_count, total_square, reduced, gbn, weights, (stat_wide, stat_head, stat_hidden, stat_kernel),
-        norm_params, norm_second, bn_params, bn_second,
+    outs = list(
+        update_call(
+            step_count, total_square, reduced, gbn, weights, (stat_wide, stat_head, stat_hidden, stat_kernel),
+            norm_params, norm_second, bn_params, bn_second,
+        )
     )
+    for i in (5, 12):
+        outs[i] = outs[i].swapaxes(1, 2)
+    for i in (7, 14):
+        outs[i] = outs[i].transpose(1, 2, 0)
+    outs[22] = outs[22].swapaxes(1, 2)
+    outs[24] = outs[24].swapaxes(0, 1)
     return (block_out, input_grad, outs[0][0, :1], *outs[1:])
 
 

time: 424 us -> 204 us (0.48)
  blocking collectives: 163 us -> 0 us
  waiting for transfers between devices: 110 us -> 0 us
  Pallas kernels: 93 us -> 195 us
  between operations: 18.9 us -> 1.54 us
  local copies, waits for them, and re-layouts: 22.8 us -> 7.06 us
  other arithmetic: 14.8 us -> 0 us
    psum x4 -> x0, blocking collectives: 126 us -> none  [the longest x1 40.6 us: local(): lax.psum(power_here + count_here * (mean_here - mean) ** 2, ('dp', 'tenso...]
    pallas_call x0 -> x4, Pallas kernels: none -> 102 us  [the longest x1 54.7 us: reduce_call(): pl.pallas_call(functools.partial(reduce_kernel, dp_count), in_specs=[VMEM...]
    psum x1 -> x0, waiting for transfers between devices: 72 us -> none  [local(): reduced = lax.psum(chunks, 'dp').reshape(3, ROWS, D)]
    reduce_scatter x1 -> x0, waiting for transfers between devices: 38.3 us -> none  [local(): chunks = lax.psum_scatter(chunks, 'tensor', scatter_dimension=0, tiled=True)]
    all_gather x4 -> x0, blocking collectives: 37.7 us -> none  [the longest x2 22.6 us: local(): ffn_one, ffn_two = [lax.all_gather(a, 'tensor') for a in (ffn_one, ffn_two)]]
    unnamed x42 -> x6, local copies, waits for them, and re-layouts: 19 us -> 7.06 us
    reduce_sum x5 -> x0, other arithmetic: 4.82 us -> none  [the longest x1 2.14 us: local(): jnp.sum(high * high) - jnp.sum(norm_rows * norm_rows) + jnp.sum(gbn * gbn)]
  transfers between devices with their start and end apart: 2 -> 0, of which waited for: 2 -> 0; matrix products, arithmetic and copies ran while one was open for 1% -> 0% of each run, Pallas kernels for 0% -> 0%
where the time goes in v2:
time: 204 us
  Pallas kernels  195 us (96%)
  local copies, waits for them, and re-layouts  7.06 us (3%)
    pallas_call x1, Pallas kernels, reduce_call(): pl.pallas_call(functools.partial(reduce_kernel, dp_count), in_specs=[VMEM...  54.7 us
    pallas_call x1, Pallas kernels, update_call(): pl.pallas_call(update_kernel, grid=(1,), in_specs=[SMEM_SPEC] + [one(a) f...  47.9 us
    pallas_call x1, Pallas kernels, gather_call(): pl.pallas_call(gather_kernel, in_specs=[VMEM_SPEC] * 8, out_specs=[VMEM_S...  24.4 us
    pallas_call x2, Pallas kernels, exchange_call(): pl.pallas_call(functools.partial(kernel, counts), in_specs=[VMEM_SPEC] *...  22.8 us
    pallas_call x1, Pallas kernels, backward_call(): pl.pallas_call(backward_kernel, grid=(frames // LEN,), in_specs=[SMEM_SPE...  19.3 us
    pallas_call x1, Pallas kernels, forward_call(): pl.pallas_call(forward_kernel, grid=(utts,), in_specs=[SMEM_SPEC, tile(D)...  14.1 us
    pallas_call x1, Pallas kernels, middle_call(): pl.pallas_call(middle_kernel, grid=(frames // LEN,), in_specs=[SMEM_SPEC,...  11.8 us
    unnamed x6, local copies, waits for them, and re-layouts  7.06 us

profile of v2, /device:TPU:0, one launch (start us, length us, event | category | flops | bytes accessed | tf_op | source)
XLA Modules:
  0.0 203.6 jit_solution(11118102421936849456)
XLA Ops:
  0.7 0.0 copy-start
  0.7 2.0 copy.46.x_ref.x0_ref
  2.6 24.4 %gather_part.1 = (bf16[4,2,240,240]{3,2,1,0:T(8,128)(2,1)}, bf16[7,256,240]{2,1,0:T(8,128)(2,1)}, bf16[4,2,240,240]{3,2,1,0:T(8,128)(2,1)}, f32[24,256]{1,0:T(8,128)}) custom-call(f32[2,240,240]{2,1,0:T(8,128)} %fi_ref.3, f32[2,240,240]{2,1,0:T(8,128)} %fo_ref.3, f32[3,60,240]{2,1,0:T(8,128)} %bitcast.12, f32[60,240]{1,0:T(8,128)} %ao_ref.3, ...), custom_call_target="tpu_custom_call" | custom-call | tf_op jit(solution)/shard_map/gather_part/pallas_call | solution.py:718
  27.0 14.1 %forward_part.1 = (bf16[768,240]{1,0:T(8,128)(2,1)}, f32[4,768,240]{2,1,0:T(8,128)}, bf16[4,768,240]{2,1,0:T(8,128)(2,1)}, f32[768,240]{1,0:T(8,128)}, bf16[768,...) custom-call(s32[16]{0:T(128)} %lens_ref.5, ...), custom_call_target="tpu_custom_call" | custom-call | tf_op jit(solution)/shard_map/forward_part/pallas_call | solution.py:535
  41.1 0.0 copy-done
  41.1 0.9 copy.47.cot_ref
  42.1 11.8 %moments_part.1.bn_ref = f32[8,256]{1,0:T(8,128)} custom-call(f32[4,8,256]{2,1,0:T(8,128)} %get-tuple-element.91.st_ref, f32[24,256]{1,0:T(8,128)} %get-tuple-element.88.small_ref), custom_call_target="tpu_custom_call" | custom-call | tf_op jit(solution)/shard_map/moments_part/pallas_call | solution.py:824
  53.9 11.8 %middle_part.1 = (bf16[768,240]{1,0:T(8,128)(2,1)}, f32[768,240]{1,0:T(8,128)}, f32[768,256]{1,0:T(8,128)}, bf16[768,256]{1,0:T(8,128)(2,1)}, bf16[768,240]{1,0:...) custom-call(s32[16]{0:T(128)} %lens_ref.5, ...), custom_call_target="tpu_custom_call" | custom-call | tf_op jit(solution)/shard_map/middle_part/pallas_call | solution.py:562
  65.7 1.9 copy.49
  67.6 11.0 %totals_part.1.bn_ref = f32[8,256]{1,0:T(8,128)} custom-call(f32[8,256]{1,0:T(8,128)} %get-tuple-element.104.gb_ref, f32[8,256]{1,0:T(8,128)} %moments_part.1.bn_ref), custom_call_target="tpu_custom_call" | custom-call | tf_op jit(solution)/shard_map/totals_part/pallas_call | solution.py:824
  78.6 19.3 %backward_part.1 = (f32[768,240]{1,0:T(8,128)}, bf16[4,512,240]{2,1,0:T(8,128)(2,1)}, bf16[4,512,240]{2,1,0:T(8,128)(2,1)}) custom-call(s32[16]{0:T(128)} %lens_ref.5, bf16[768,240]{1,0:T(8,128)(2,1)} %copy.46.x_ref.x0_ref, f32[768,240]{1,0:T(8,128)} %get-tuple-element.94.x1_ref, f32[768,240]{1,0:T(8,128)} %get-tuple-element.90.x2_ref, ...), custom_call_target="tpu_custom_call" | custom-call | tf_op jit(solution)/shard_map/backward_part/pallas_call | solution.py:595
  97.9 2.3 %copy.50 = f32[768,240]{0,1:T(8,128)} copy(f32[768,240]{1,0:T(8,128)} %get-tuple-element.146) | data formatting | bytes 1474560
  100.8 54.7 %reduce_part.1 = (bf16[3,512,240]{2,1,0:T(8,128)(2,1)}, f32[8,128]{1,0:T(8,128)}, f32[8,128]{1,0:T(8,128)}) custom-call(bf16[4,512,240]{2,1,0:T(8,128)(2,1)} %get-tuple-element.114.c0_ref, bf16[4,512,240]{2,1,0:T(8,128)(2,1)} %get-tuple-element.115.c1_ref, bf16[4,512,240]{2,1,0:T(8,128)(2,1)} %get-tuple-element.116.c2_ref, f32[8,256]{1,0:T(8,128)} %totals_part.1.bn_ref), custom_call_target="tpu_custom_call" | custom-call | tf_op jit(solution)/shard_map/reduce_part/pallas_call | solution.py:947
  155.5 47.9 %update_part.1 = (f32[1,128]{1,0:T(1,128)}, f32[5,2,240]{2,1,0:T(2,128)}, f32[2,60]{1,0:T(2,128)}, f32[2,240,240]{2,1,0:T(8,128)}, f32[2,240,240]{2,1,0:T(8,128)...) custom-call(s32[1]{0:T(128)S(6)} %copy.51.step_ref, ...), custom_call_target="tpu_custom_call" | custom-call | tf_op jit(solution)/shard_map/update_part/pallas_call | solution.py:626
Async XLA Ops:
  0.7 40.5 %copy-start = (bf16[768,240]{0,1:T(8,128)(2,1)S(1)}, bf16[768,240]{0,1:T(8,128)(2,1)}, u32[]{:S(2)}) copy-start(bf16[768,240]{0,1:T(8,128)(2,1)} %param.21) | copy-start | bytes 1105924

commit v3 on v2

--- a/solution.py
+++ b/solution.py
@@ -14,7 +14,6 @@
 HEAD = 60
 PADH = 64
 ROOT_ITERS = 8
-FINE_ITERS = 4
 NPARAM = 1331280
 PEAK_RATE = 2.0
 WARM_STEPS = 4.0
@@ -317,26 +316,40 @@
     return high, (a - high.astype(F32)).astype(BF16)
 
 
-def mul_fine(a, b):
-    a_high, a_low = a
-    b_high, b_low = b
-    return nn(a_high, b_high) + (nn(a_high, b_low) + nn(a_low, b_high))
+def stacked(lefts, right):
+    full = nn(jnp.concatenate(lefts, axis=0), right)
+    places, at = [], 0
+    for left in lefts:
+        places.append(full[at : at + left.shape[0]])
+        at += left.shape[0]
+    return places
+
+
+def mul_fine(a, b, rider=None):
+    high, cross, *rest = stacked([*a] + ([] if rider is None else [rider]), b[0])
+    return (high + (nn(a[0], b[1]) + cross), *rest)
 
 
 def eye_of(n):
     return (lax.broadcasted_iota(jnp.int32, (n, n), 0) == lax.broadcasted_iota(jnp.int32, (n, n), 1)).astype(F32)
 
 
-def next_gap(gap, eye, fine):
+def next_power(own, direction, fine):
+    rider = direction.astype(BF16)
     if fine:
-        own = split(gap)
-        square = split(mul_fine(own, own))
-        inner = mul_fine(square, split((15.0 / 256.0) * eye + (1.0 / 256.0) * gap))
-        return mul_fine(square, split(0.625 * eye + 0.3125 * gap + inner))
-    own = gap.astype(BF16)
-    square = nn(own, own).astype(BF16)
-    inner = nn(square, ((15.0 / 256.0) * eye + (1.0 / 256.0) * gap).astype(BF16))
-    return nn(square, (0.625 * eye + 0.3125 * gap + inner).astype(BF16))
+        parts = split(own)
+        square, moved = mul_fine(parts, parts, rider)
+        step = 0.0625 * square - 0.625 * own
+        halves = split(step)
+        once = mul_fine(halves, parts)[0]
+        twice = mul_fine(halves, split(once))[0]
+    else:
+        low = own.astype(BF16)
+        square, moved = stacked([low, rider], low)
+        step = (0.0625 * square - 0.625 * own).astype(BF16)
+        once = nn(step, low)
+        twice = nn(step, once.astype(BF16))
+    return 2.44140625 * own + 3.125 * once + twice, 1.25 * direction - 0.25 * moved
 
 
 def total_of(a):
@@ -349,7 +362,7 @@
     gn_o, cn_o, cb_o, cfi_o, cfo_o, cai_o, cao_o, cci_o, cdk_o, cco_o,
     nfi_o, nfo_o, nai_o, nao_o, nci_o, ndk_o, nco_o, nn_o, nb_o, nns_o, nbs_o,
     nsw_o, nsh_o, nsd_o, nsk_o,
-    gap_f, gap_b, dir_f, dir_b,
+    mat_f, mat_b, dir_f, dir_b,
 ):
     steps = jnp.full((1, 1), step_ref[0], jnp.int32).astype(F32)
     rate = PEAK_RATE * jnp.minimum(steps / WARM_STEPS, jnp.sqrt(WARM_STEPS / steps))
@@ -395,7 +408,7 @@
         scale = 1.0
         for k, c in enumerate((wide_c, hidden_c)):
             zoom = 2.5 * lax.rsqrt(0.25 * c * c * D + 0.5 * c * trace + 0.25 * power)
-            gap_f[2 * i + k] = eye_d - zoom * (0.5 * c * eye_d + 0.5 * gram)
+            mat_f[2 * i + k] = zoom * (0.5 * c * eye_d + 0.5 * gram)
             scale = scale * jnp.sqrt(jnp.sqrt(zoom))
         scales_f.append(scale)
 
@@ -416,7 +429,7 @@
     for group in range(2):
         low = red_ref[1, group * 4 * PADH : (group + 1) * 4 * PADH, :]
         clipped = low.astype(F32) * factor
-        dir_b[group] = clipped
+        dir_b[group] = clipped.T
         gram = jnp.where(same_block, nt(low, low), 0.0) * square_factor
         row_trace = jnp.sum(clipped * clipped, axis=1, keepdims=True)
         row_power = jnp.sum(gram * gram, axis=1, keepdims=True)
@@ -447,34 +460,27 @@
                 2.5 * lax.rsqrt(0.25 * c * c * n + 0.5 * c * trace + 0.25 * power)
                 for c, n, trace, power in zip(cs, sizes, traces, powers)
             ]
-            gap_b[2 * group + k] = eye_b - spread(zooms) * (0.5 * spread(cs) * eye_b + 0.5 * gram)
+            mat_b[2 * group + k] = spread(zooms) * (0.5 * spread(cs) * eye_b + 0.5 * gram)
             scale = [s * jnp.sqrt(jnp.sqrt(zoom)) for s, zoom in zip(scale, zooms)]
         scales_b.append(scale)
 
-    def advance(fine, last):
+    def advance(fine):
         for k in range(2):
-            for i in range(4):
-                gap = gap_f[2 * i + k]
-                dir_f[i] = dir_f[i] + 0.25 * nn(dir_f[i].astype(BF16), gap.astype(BF16))
-                if not last:
-                    gap_f[2 * i + k] = next_gap(gap, eye_d, fine)
-            for i in range(2):
-                gap = gap_b[2 * i + k]
-                dir_b[i] = dir_b[i] + 0.25 * nn(gap.astype(BF16), dir_b[i].astype(BF16))
-                if not last:
-                    gap_b[2 * i + k] = next_gap(gap, eye_b, fine)
-
-    def fine_step(i, carry):
-        advance(True, False)
+            for mats, dirs, count in ((mat_f, dir_f, 4), (mat_b, dir_b, 2)):
+                for i in range(count):
+                    mats[2 * i + k], dirs[i] = next_power(mats[2 * i + k], dirs[i], fine)
+
+    def coarse_step(i, carry):
+        advance(False)
         return carry
 
-    def coarse_step(i, carry):
-        advance(False, False)
-        return carry
-
-    lax.fori_loop(0, FINE_ITERS, fine_step, 0)
-    lax.fori_loop(0, ROOT_ITERS - 1 - FINE_ITERS, coarse_step, 0)
-    advance(False, True)
+    advance(True)
+    lax.fori_loop(0, ROOT_ITERS - 2, coarse_step, 0)
+    for k in range(2):
+        for mats, dirs, count in ((mat_f, dir_f, 4), (mat_b, dir_b, 2)):
+            for i in range(count):
+                moved = nn(dirs[i].astype(BF16), mats[2 * i + k].astype(BF16))
+                dirs[i] = 1.25 * dirs[i] - 0.25 * moved
 
     def graft(weight, direction):
         size = jnp.sqrt(total_of(weight * weight))
@@ -487,10 +493,11 @@
         if is_out:
             direction = direction.T
         (nfi_o, nfo_o)[is_out][member] = weight - graft(weight, direction) * direction
+    turned_b = [dir_b[group].T for group in range(2)]
     for index in range(8):
         group, i = index // 4, index % 4
         part = slice(i * PADH, i * PADH + HEAD)
-        direction = dir_b[group][part, :] * scales_b[group][i]
+        direction = turned_b[group][part, :] * scales_b[group][i]
         clipped = red_ref[1, index * PADH : (index + 1) * PADH, :][:HEAD, :].astype(F32) * factor
         if index in (3, 6):
             weight_ref, clip_o, new_o = ((ao_ref, cao_o, nao_o), None, None, (co_ref, cco_o, nco_o))[index - 3]
@@ -633,7 +640,7 @@
         out_shape=[shape(a.shape) for a in out_arrays],
         scratch_shapes=[
             pltpu.VMEM((8, D, D), F32), pltpu.VMEM((4, wide, wide), F32),
-            pltpu.VMEM((4, D, D), F32), pltpu.VMEM((2, wide, D), F32),
+            pltpu.VMEM((4, D, D), F32), pltpu.VMEM((2, D, wide), F32),
         ],
         compiler_params=PARAMS,
         name="update_part",

time: 204 us -> 189 us (0.926)
  Pallas kernels: 195 us -> 180 us
    pallas_call x1, Pallas kernels: 47.9 us -> 33.1 us  [update_call(): pl.pallas_call(update_kernel, grid=(1,), in_specs=[SMEM_SPEC] + [one(a) f...]
where the time goes in v3:
time: 189 us
  Pallas kernels  180 us (95%)
  local copies, waits for them, and re-layouts  7.06 us (4%)
    pallas_call x1, Pallas kernels, reduce_call(): pl.pallas_call(functools.partial(reduce_kernel, dp_count), in_specs=[VMEM...  54.9 us
    pallas_call x1, Pallas kernels, update_call(): pl.pallas_call(update_kernel, grid=(1,), in_specs=[SMEM_SPEC] + [one(a) f...  33.1 us
    pallas_call x1, Pallas kernels, gather_call(): pl.pallas_call(gather_kernel, in_specs=[VMEM_SPEC] * 8, out_specs=[VMEM_S...  24.4 us
    pallas_call x2, Pallas kernels, exchange_call(): pl.pallas_call(functools.partial(kernel, counts), in_specs=[VMEM_SPEC] *...  22.8 us
    pallas_call x1, Pallas kernels, backward_call(): pl.pallas_call(backward_kernel, grid=(frames // LEN,), in_specs=[SMEM_SPE...  19.3 us
    pallas_call x1, Pallas kernels, forward_call(): pl.pallas_call(forward_kernel, grid=(utts,), in_specs=[SMEM_SPEC, tile(D)...  14.1 us
    pallas_call x1, Pallas kernels, middle_call(): pl.pallas_call(middle_kernel, grid=(frames // LEN,), in_specs=[SMEM_SPEC,...  11.8 us
    unnamed x6, local copies, waits for them, and re-layouts  7.06 us

profile of v3, /device:TPU:0, one launch (start us, length us, event | category | flops | bytes accessed | tf_op | source)
XLA Modules:
  0.0 189.0 jit_solution(17195389557137214038)
XLA Ops:
  0.7 0.0 copy-start
  0.7 2.0 %copy.46.x_ref.x0_ref = bf16[768,240]{1,0:T(8,128)(2,1)} copy(bf16[768,240]{0,1:T(8,128)(2,1)} %param.19) | data formatting | bytes 737280 | tf_op args[0]
  2.6 24.4 %gather_part.1 = (bf16[4,2,240,240]{3,2,1,0:T(8,128)(2,1)}, bf16[7,256,240]{2,1,0:T(8,128)(2,1)}, bf16[4,2,240,240]{3,2,1,0:T(8,128)(2,1)}, f32[24,256]{1,0:T(8,128)}) custom-call(f32[2,240,240]{2,1,0:T(8,128)} %fi_ref.3, f32[2,240,240]{2,1,0:T(8,128)} %fo_ref.3, f32[3,60,240]{2,1,0:T(8,128)} %bitcast.12, f32[60,240]{1,0:T(8,128)} %ao_ref.3, ...), custom_call_target="tpu_custom_call" | custom-call | tf_op jit(solution)/shard_map/gather_part/pallas_call | solution.py:725
  27.0 14.1 %forward_part.1 = (bf16[768,240]{1,0:T(8,128)(2,1)}, f32[4,768,240]{2,1,0:T(8,128)}, bf16[4,768,240]{2,1,0:T(8,128)(2,1)}, f32[768,240]{1,0:T(8,128)}, bf16[768,...) custom-call(s32[16]{0:T(128)} %lens_ref.5, ...), custom_call_target="tpu_custom_call" | custom-call | tf_op jit(solution)/shard_map/forward_part/pallas_call | solution.py:542
  41.1 0.0 copy-done
  41.1 0.9 copy.47.cot_ref
  42.1 11.8 %moments_part.1.bn_ref = f32[8,256]{1,0:T(8,128)} custom-call(f32[4,8,256]{2,1,0:T(8,128)} %get-tuple-element.91.st_ref, f32[24,256]{1,0:T(8,128)} %get-tuple-element.88.small_ref), custom_call_target="tpu_custom_call" | custom-call | tf_op jit(solution)/shard_map/moments_part/pallas_call | solution.py:831
  53.9 11.8 %middle_part.1 = (bf16[768,240]{1,0:T(8,128)(2,1)}, f32[768,240]{1,0:T(8,128)}, f32[768,256]{1,0:T(8,128)}, bf16[768,256]{1,0:T(8,128)(2,1)}, bf16[768,240]{1,0:...) custom-call(s32[16]{0:T(128)} %lens_ref.5, ...), custom_call_target="tpu_custom_call" | custom-call | tf_op jit(solution)/shard_map/middle_part/pallas_call | solution.py:569
  65.7 1.9 %copy.49 = bf16[768,240]{0,1:T(8,128)(2,1)} copy(bf16[768,240]{1,0:T(8,128)(2,1)} %get-tuple-element.145) | data formatting | bytes 737280
  67.6 11.0 %totals_part.1.bn_ref = f32[8,256]{1,0:T(8,128)} custom-call(f32[8,256]{1,0:T(8,128)} %get-tuple-element.104.gb_ref, f32[8,256]{1,0:T(8,128)} %moments_part.1.bn_ref), custom_call_target="tpu_custom_call" | custom-call | tf_op jit(solution)/shard_map/totals_part/pallas_call | solution.py:831
  78.6 19.3 %backward_part.1 = (f32[768,240]{1,0:T(8,128)}, bf16[4,512,240]{2,1,0:T(8,128)(2,1)}, bf16[4,512,240]{2,1,0:T(8,128)(2,1)}) custom-call(s32[16]{0:T(128)} %lens_ref.5, bf16[768,240]{1,0:T(8,128)(2,1)} %copy.46.x_ref.x0_ref, f32[768,240]{1,0:T(8,128)} %get-tuple-element.94.x1_ref, f32[768,240]{1,0:T(8,128)} %get-tuple-element.90.x2_ref, ...), custom_call_target="tpu_custom_call" | custom-call | tf_op jit(solution)/shard_map/backward_part/pallas_call | solution.py:602
  97.9 2.3 %copy.50 = f32[768,240]{0,1:T(8,128)} copy(f32[768,240]{1,0:T(8,128)} %get-tuple-element.146) | data formatting | bytes 1474560
  100.8 54.9 %reduce_part.1 = (bf16[3,512,240]{2,1,0:T(8,128)(2,1)}, f32[8,128]{1,0:T(8,128)}, f32[8,128]{1,0:T(8,128)}) custom-call(bf16[4,512,240]{2,1,0:T(8,128)(2,1)} %get-tuple-element.114.c0_ref, bf16[4,512,240]{2,1,0:T(8,128)(2,1)} %get-tuple-element.115.c1_ref, bf16[4,512,240]{2,1,0:T(8,128)(2,1)} %get-tuple-element.116.c2_ref, f32[8,256]{1,0:T(8,128)} %totals_part.1.bn_ref), custom_call_target="tpu_custom_call" | custom-call | tf_op jit(solution)/shard_map/reduce_part/pallas_call | solution.py:954
  155.7 33.1 %update_part.1 = (f32[1,128]{1,0:T(1,128)}, f32[5,2,240]{2,1,0:T(2,128)}, f32[2,60]{1,0:T(2,128)}, f32[2,240,240]{2,1,0:T(8,128)}, f32[2,240,240]{2,1,0:T(8,128)...) custom-call(s32[1]{0:T(128)S(6)} %copy.51.step_ref, ...), custom_call_target="tpu_custom_call" | custom-call | tf_op jit(solution)/shard_map/update_part/pallas_call | solution.py:633
Async XLA Ops:
  0.7 40.5 %copy-start = (bf16[768,240]{0,1:T(8,128)(2,1)S(1)}, bf16[768,240]{0,1:T(8,128)(2,1)}, u32[]{:S(2)}) copy-start(bf16[768,240]{0,1:T(8,128)(2,1)} %param.21) | copy-start | bytes 1105924

commit v4 on v1

v4 whole, which is shorter than its diff:
```python
import functools
import itertools
import math
import types

import jax
import jax.numpy as jnp
from jax import lax
from jax.experimental import pallas as pl
from jax.experimental.pallas import tpu as pltpu
from jax.sharding import PartitionSpec as P

D = 240
KS = 15
LEN = 192
HEAD = 60
PADH = 64
ROOT_ITERS = 8
NPARAM = 1331280
PEAK_RATE = 2.0
WARM_STEPS = 4.0
SMALL_RATE = 0.3
GRAFT_SCALE = 0.6
NEG_FILL = -1000000000.0
VMEM_CAP = 60 * 1024 * 1024

F32 = jnp.float32
BF16 = jnp.bfloat16


def nn(a, b):
    return lax.dot_general(a, b, (((1,), (0,)), ((), ())), preferred_element_type=F32)


def nt(a, b):
    return lax.dot_general(a, b, (((1,), (1,)), ((), ())), preferred_element_type=F32)


def tn(a, b):
    return lax.dot_general(a, b, (((0,), (0,)), ((), ())), preferred_element_type=F32)


def sigmoid(v):
    return 0.5 * jnp.tanh(0.5 * v) + 0.5


def standardize(h):
    centred = h - jnp.sum(h, axis=-1, keepdims=True) * (1.0 / D)
    spread = jnp.sum(centred * centred, axis=-1, keepdims=True) * (1.0 / D)
    inv = lax.rsqrt(spread + 1e-05)
    return centred * inv, inv


def norm_back(h, gain, dy):
    xhat, inv = standardize(h)
    scaled = dy * gain
    mean_a = jnp.sum(scaled, axis=-1, keepdims=True) * (1.0 / D)
    mean_b = jnp.sum(scaled * xhat, axis=-1, keepdims=True) * (1.0 / D)
    dh = inv * (scaled - mean_a - xhat * mean_b)
    return dh, jnp.sum(dy * xhat, axis=0, keepdims=True), jnp.sum(dy, axis=0, keepdims=True)


def row_mask(length):
    return (lax.broadcasted_iota(jnp.int32, (LEN, 1), 0) < length).astype(F32)


def lane_masks(dtype):
    lane = lax.broadcasted_iota(jnp.int32, (1, 128), 1)
    return ((lane < PADH).astype(dtype), (lane >= PADH).astype(dtype))


def split(a):
    high = a.astype(BF16)
    return high, (a - high.astype(F32)).astype(BF16)


def stacked(lefts, right):
    full = nn(jnp.concatenate(lefts, axis=0), right)
    places, at = [], 0
    for left in lefts:
        places.append(full[at : at + left.shape[0]])
        at += left.shape[0]
    return places


def mul_fine(a, b, rider=None):
    high, cross, *rest = stacked([*a] + ([] if rider is None else [rider]), b[0])
    return (high + (nn(a[0], b[1]) + cross), *rest)


def eye_of(n):
    return (lax.broadcasted_iota(jnp.int32, (n, n), 0) == lax.broadcasted_iota(jnp.int32, (n, n), 1)).astype(F32)


def next_power(own, direction, fine):
    rider = direction.astype(BF16)
    if fine:
        parts = split(own)
        square, moved = mul_fine(parts, parts, rider)
        step = 0.0625 * square - 0.625 * own
        halves = split(step)
        once = mul_fine(halves, parts)[0]
        twice = mul_fine(halves, split(once))[0]
    else:
        low = own.astype(BF16)
        square, moved = stacked([low, rider], low)
        step = (0.0625 * square - 0.625 * own).astype(BF16)
        once = nn(step, low)
        twice = nn(step, once.astype(BF16))
    return 2.44140625 * own + 3.125 * once + twice, 1.25 * direction - 0.25 * moved


def total_of(a):
    return jnp.sum(jnp.sum(a, axis=1, keepdims=True), axis=0, keepdims=True)


def update_kernel(
    step_ref, tot_ref, red_ref, lng_ref, gbn_ref, fi_ref, fo_ref, ai_ref, ao_ref, ci_ref, dk_ref, co_ref,
    sw_ref, sh_ref, sd_ref, sk_ref, np_ref, ns_ref, bp_ref, bs_ref,
    gn_o, cn_o, cb_o, cfi_o, cfo_o, cai_o, cao_o, cci_o, cdk_o, cco_o,
    nfi_o, nfo_o, nai_o, nao_o, nci_o, ndk_o, nco_o, nn_o, nb_o, nns_o, nbs_o,
    nsw_o, nsh_o, nsd_o, nsk_o,
    mat_f, mat_b, dir_f, dir_b,
):
    steps = jnp.full((1, 1), step_ref[0], jnp.int32).astype(F32)
    rate = PEAK_RATE * jnp.minimum(steps / WARM_STEPS, jnp.sqrt(WARM_STEPS / steps))
    grad_norm = jnp.sqrt(tot_ref[0:1, 0:1])
    threshold = math.sqrt(NPARAM)
    factor = threshold / jnp.maximum(grad_norm, threshold)
    square_factor = factor * factor
    gn_o[...] = jnp.broadcast_to(grad_norm, gn_o.shape)

    c_norm = lng_ref[...] * factor
    for i in range(5):
        clipped = c_norm[2 * i : 2 * i + 2, :]
        second = 0.5 * ns_ref[i] + 0.5 * clipped * clipped
        cn_o[i] = clipped
        nns_o[i] = second
        nn_o[i] = np_ref[i] - rate * SMALL_RATE * clipped * lax.rsqrt(second)
    c_bn = gbn_ref[0:2, 0:HEAD] * factor
    second = 0.5 * bs_ref[...] + 0.5 * c_bn * c_bn
    cb_o[...] = c_bn
    nbs_o[...] = second
    nb_o[...] = bp_ref[...] - rate * SMALL_RATE * c_bn * lax.rsqrt(second)

    eye_d = eye_of(D)
    scales_f = []
    for i in range(4):
        member, is_out = i // 2, i % 2
        chunk = (2, 0)[member]
        start = is_out * (D, 256)[chunk // 2]
        low = red_ref[chunk, start : start + D, :]
        wide_c = sw_ref[0, 2 * is_out + member, 0:1, 0:1]
        hidden_c = sd_ref[0, 2 * is_out + member, 0:1, 0:1]
        gram = tn(low, low) * square_factor
        wide = nt(low, low) * square_factor
        nsw_o[0, 2 * is_out + member] = 0.5 * wide_c * eye_d + 0.5 * wide
        nsd_o[0, 2 * is_out + member] = 0.5 * hidden_c * eye_d + 0.5 * gram
        clipped = low.astype(F32) * factor
        if is_out:
            cfo_o[member] = clipped.T
        else:
            cfi_o[member] = clipped
        dir_f[i] = clipped
        trace = total_of(clipped * clipped)
        power = total_of(gram * gram)
        scale = 1.0
        for k, c in enumerate((wide_c, hidden_c)):
            zoom = 2.5 * lax.rsqrt(0.25 * c * c * D + 0.5 * c * trace + 0.25 * power)
            mat_f[2 * i + k] = zoom * (0.5 * c * eye_d + 0.5 * gram)
            scale = scale * jnp.sqrt(jnp.sqrt(zoom))
        scales_f.append(scale)

    eye_b = eye_of(4 * PADH)
    row_block = lax.broadcasted_iota(jnp.int32, (4 * PADH, 1), 0) // PADH
    lane_block = lax.broadcasted_iota(jnp.int32, (1, 4 * PADH), 1) // PADH
    same_block = row_block == lane_block
    wide_of = (4, 5, 6, 10, 8, 9, 7, None)
    head_of = (0, 1, 2, 7, 4, 5, 3, 6)
    scales_b = []

    def spread(values):
        column = jnp.zeros((4 * PADH, 1), F32)
        for i, value in enumerate(values):
            column = jnp.where(row_block == i, value, column)
        return column

    for group in range(2):
        low = red_ref[1, group * 4 * PADH : (group + 1) * 4 * PADH, :]
        clipped = low.astype(F32) * factor
        dir_b[group] = clipped.T
        gram = jnp.where(same_block, nt(low, low), 0.0) * square_factor
        row_trace = jnp.sum(clipped * clipped, axis=1, keepdims=True)
        row_power = jnp.sum(gram * gram, axis=1, keepdims=True)
        wide_cs, head_cs, traces, powers, dims = [], [], [], [], []
        for i in range(4):
            index = group * 4 + i
            part = slice(i * PADH, (i + 1) * PADH)
            piece = low[part, :]
            head_c = sh_ref[0, 0, head_of[index] : head_of[index] + 1, 0:1]
            own_gram = nt(piece, piece)[:HEAD, :HEAD] * square_factor
            nsh_o[0, :, head_of[index], :] = 0.5 * head_c * eye_d[:HEAD, :HEAD] + 0.5 * own_gram
            wide = tn(piece, piece) * square_factor
            if wide_of[index] is None:
                wide_c = sk_ref[0, 0:1, 0:1]
                nsk_o[:, 0, :] = 0.5 * wide_c * eye_d[:KS, :KS] + 0.5 * wide[:KS, :KS]
                dims.append(KS)
            else:
                wide_c = sw_ref[0, wide_of[index], 0:1, 0:1]
                nsw_o[0, wide_of[index]] = 0.5 * wide_c * eye_d + 0.5 * wide
                dims.append(D)
            wide_cs.append(wide_c)
            head_cs.append(head_c)
            traces.append(jnp.sum(row_trace[part], axis=0, keepdims=True))
            powers.append(jnp.sum(row_power[part], axis=0, keepdims=True))
        scale = [1.0] * 4
        for k, (cs, sizes) in enumerate(((wide_cs, dims), (head_cs, [HEAD] * 4))):
            zooms = [
                2.5 * lax.rsqrt(0.25 * c * c * n + 0.5 * c * trace + 0.25 * power)
                for c, n, trace, power in zip(cs, sizes, traces, powers)
            ]
            mat_b[2 * group + k] = spread(zooms) * (0.5 * spread(cs) * eye_b + 0.5 * gram)
            scale = [s * jnp.sqrt(jnp.sqrt(zoom)) for s, zoom in zip(scale, zooms)]
        scales_b.append(scale)

    def advance(fine):
        for k in range(2):
            for mats, dirs, count in ((mat_f, dir_f, 4), (mat_b, dir_b, 2)):
                for i in range(count):
                    mats[2 * i + k], dirs[i] = next_power(mats[2 * i + k], dirs[i], fine)

    def coarse_step(i, carry):
        advance(False)
        return carry

    advance(True)
    lax.fori_loop(0, ROOT_ITERS - 2, coarse_step, 0)
    for k in range(2):
        for mats, dirs, count in ((mat_f, dir_f, 4), (mat_b, dir_b, 2)):
            for i in range(count):
                moved = nn(dirs[i].astype(BF16), mats[2 * i + k].astype(BF16))
                dirs[i] = 1.25 * dirs[i] - 0.25 * moved

    def graft(weight, direction):
        size = jnp.sqrt(total_of(weight * weight))
        return rate * GRAFT_SCALE * size / (jnp.sqrt(total_of(direction * direction)) + 1e-06)

    for i in range(4):
        member, is_out = i // 2, i % 2
        direction = dir_f[i] * scales_f[i]
        weight = (fi_ref, fo_ref)[is_out][member]
        if is_out:
            direction = direction.T
        (nfi_o, nfo_o)[is_out][member] = weight - graft(weight, direction) * direction
    turned_b = [dir_b[group].T for group in range(2)]
    for index in range(8):
        group, i = index // 4, index % 4
        part = slice(i * PADH, i * PADH + HEAD)
        direction = turned_b[group][part, :] * scales_b[group][i]
        clipped = red_ref[1, index * PADH : (index + 1) * PADH, :][:HEAD, :].astype(F32) * factor
        if index in (3, 6):
            weight_ref, clip_o, new_o = ((co_ref, cco_o, nco_o), None, None, (ao_ref, cao_o, nao_o))[index - 3]
            clip_o[...] = clipped
            new_o[...] = weight_ref[...] - graft(weight_ref[...], direction) * direction
        elif index == 7:
            turned = direction.T[:KS, :]
            cdk_o[...] = clipped.T[:KS, :]
            ndk_o[...] = dk_ref[...] - graft(dk_ref[...], turned) * turned
        else:
            weight_ref, clip_o, new_o = (ai_ref, cai_o, nai_o) if index < 3 else (ci_ref, cci_o, nci_o)
            at = (index,) if index < 3 else (slice(None), index - 4)
            weight = weight_ref[at]
            clip_o[at] = clipped
            new_o[at] = weight - graft(weight, direction) * direction


def shape(dims, dtype=F32):
    return jax.ShapeDtypeStruct(dims, dtype)


def whole(dims):
    zeros = (0,) * len(dims)
    return pl.BlockSpec(dims, lambda u: zeros)


SMEM_SPEC = pl.BlockSpec(memory_space=pltpu.SMEM)
VMEM_SPEC = pl.BlockSpec(memory_space=pltpu.VMEM)
PARAMS = pltpu.CompilerParams(vmem_limit_bytes=VMEM_CAP)


def update_call(step_count, total_square, reduced, lng, gbn, weights, stats, norm_params, norm_second, bn_params, bn_second):
    stat_wide, stat_head, stat_hidden, stat_kernel = stats
    corner = lambda a: pl.BlockSpec((1, a.shape[1], 8, 128), lambda i: (0, 0, 0, 0))
    one = lambda a: whole(a.shape)
    n_stat = lambda a: whole(a.shape)
    out_arrays = [
        shape((1, 128)), norm_params, bn_params, *weights, *weights, norm_params, bn_params, norm_params, bn_params,
        stat_wide, stat_head, stat_hidden, stat_kernel,
    ]
    in_arrays = [total_square, reduced, lng, gbn, *weights]
    wide = 4 * PADH
    return pl.pallas_call(
        update_kernel,
        grid=(1,),
        in_specs=[SMEM_SPEC] + [one(a) for a in in_arrays]
        + [corner(stat_wide), one(stat_head), corner(stat_hidden), one(stat_kernel)]
        + [one(a) for a in (norm_params, norm_second, bn_params, bn_second)],
        out_specs=[one(a) for a in out_arrays],
        out_shape=[shape(a.shape) for a in out_arrays],
        scratch_shapes=[
            pltpu.VMEM((8, D, D), F32), pltpu.VMEM((4, wide, wide), F32),
            pltpu.VMEM((4, D, D), F32), pltpu.VMEM((2, D, wide), F32),
        ],
        compiler_params=PARAMS,
        name="update_part",
    )(step_count, *in_arrays, *stats, norm_params, norm_second, bn_params, bn_second)


MESH = pl.DeviceIdType.MESH


def flip(index, bit):
    step = 2 ** bit
    return index + step - 2 * step * ((index // step) % 2)


def bits_of(count):
    bits = count.bit_length() - 1
    if 2 ** bits != count:
        raise ValueError("axis size")
    return bits


def greet_axes(counts):
    barrier = pltpu.get_barrier_semaphore()
    for axis, count in counts:
        me = lax.axis_index(axis)

        def signal(k, carry, axis=axis, count=count, me=me):
            pl.semaphore_signal(
                barrier, inc=1, device_id={axis: lax.rem(me + k, count)}, device_id_type=MESH
            )
            return carry

        lax.fori_loop(1, count, signal, 0)


def greeted(counts):
    pl.semaphore_wait(pltpu.get_barrier_semaphore(), sum(count - 1 for axis, count in counts))


def share_copy(axis, slots, sems, slot, peer, sent):
    return pltpu.make_async_remote_copy(
        src_ref=slots.at[slot], dst_ref=slots.at[slot], send_sem=sems[0].at[sent], recv_sem=sems[1].at[slot],
        device_id={axis: peer}, device_id_type=MESH,
    )


def share_start(axis, count, slots, sems):
    me = lax.axis_index(axis)

    def start(k, carry):
        peer = lax.rem(me + k, count)
        share_copy(axis, slots, sems, me, peer, peer).start()
        return carry

    lax.fori_loop(1, count, start, 0)


def share_finish(axis, count, slots, sems):
    me = lax.axis_index(axis)

    def finish(k, carry):
        peer = lax.rem(me + k, count)
        share_copy(axis, slots, sems, me, peer, peer).wait_send()
        share_copy(axis, slots, sems, peer, peer, peer).wait_recv()
        return carry

    lax.fori_loop(1, count, finish, 0)


def pool(slots, count):
    blank = jnp.zeros((1, 4 * PADH), F32)
    total = lax.fori_loop(0, count, lambda i, a: a + slots[i, 2:3, :], blank)
    mean = lax.fori_loop(0, count, lambda i, a: a + slots[i, 0:1, :] * slots[i, 2:3, :], blank) / total

    def power(i, a):
        off = slots[i, 0:1, :] - mean
        return a + slots[i, 1:2, :] + slots[i, 2:3, :] * off * off

    return mean, lax.fori_loop(0, count, power, blank), total


CHAINS = ((0, 0, 512), (1, 256, 256), (1, 0, 256), (2, 256, 256), (2, 0, 256))


def plan_of(dp_count, length):
    bits = bits_of(dp_count)
    radices = [2] * (bits % 2) + [4] * (bits // 2)
    plan, stride = [], 1
    for radix in radices:
        cut = length % (16 * radix) == 0
        length = length // radix if cut else length
        plan.append((stride, radix, cut, length))
        stride *= radix
    return plan


def landing_rows(dp_count):
    return sum(radix * piece for _, _, n in CHAINS for _, radix, _, piece in plan_of(dp_count, n))


def copy_count(dp_count):
    return sum(
        3 + sum((radix - 1) * (1 + cut) for _, radix, cut, _ in plan_of(dp_count, n)) for _, _, n in CHAINS
    )


def swish_slope(inner):
    sigma = sigmoid(inner)
    return sigma * (1.0 + inner * (1.0 - sigma))


HALVES = tuple(slice(i * 128, i * 128 + 128) for i in range(2))


def step_kernel(
    counts, names, lens_ref, x_ref, cot_ref, np_ref, fi_ref, fo_ref, ai_ref, ao_ref, ci_ref, co_ref, dk_ref, bp_ref,
    out_o, ig_o, red_o, lng_o, tot_o, gbn_o, *scratch,
):
    s = types.SimpleNamespace(**dict(zip(names, scratch)))
    dp_count = dict(counts)["dp"]
    shards = s.ffn1.shape[0]
    frames = x_ref.shape[0]
    utts = frames // LEN
    t, d = lax.axis_index("tensor"), lax.axis_index("dp")
    near, far = flip(t, 0), flip(t, 1)
    last = flip(near, 1)
    wide = 4 * PADH

    def rows_of(u, size=LEN):
        return pl.ds(pl.multiple_of(u * size, size), size)

    def length_of(u):
        return lens_ref[t * utts + u]

    def each(body, start=0, stop=utts):
        def turn(u, carry):
            body(u)
            return carry

        lax.fori_loop(start, stop, turn, 0)

    greet_axes(counts)

    own = pl.ds(pl.multiple_of(t * PADH, PADH), PADH)
    parts = (
        lambda i: s.small_parts.at[i],
        lambda i: s.ffn1.at[i],
        lambda i: s.mix.at[:, pl.ds(pl.multiple_of(i * PADH, PADH), PADH), :],
        lambda i: s.ffn2.at[i],
    )

    def weight_copy(g, shard, peer, slot):
        return pltpu.make_async_remote_copy(
            src_ref=parts[g](shard), dst_ref=parts[g](shard), send_sem=s.gather_send.at[3 * g + slot],
            recv_sem=s.gather_recv.at[3 * g + slot], device_id={"tensor": peer}, device_id_type=MESH,
        )

    def launch(g):
        weight_copy(g, t, far, 0).start()
        weight_copy(g, t, near, 1).start()

    def relay(g):
        weight_copy(g, t, far, 0).wait()
        weight_copy(g, far, near, 2).start()

    def near_here(g):
        weight_copy(g, t, near, 1).wait()

    def last_here(g):
        weight_copy(g, far, near, 2).wait()

    s.small_parts[t] = jnp.zeros((24, 128), F32)
    s.small_parts[t, 0:KS, 0:HEAD] = dk_ref[...]
    s.small_parts[t, 16:18, 0:HEAD] = bp_ref[...]
    s.ffn1[t, 0] = fi_ref[0].astype(BF16)
    s.ffn1[t, 1] = fo_ref[0].astype(BF16)
    greeted(counts)
    launch(1)
    blank = jnp.zeros((PADH - HEAD, D), F32)
    pieces = [ai_ref[m] for m in range(3)] + [ao_ref[...]] + [ci_ref[:, m, :] for m in range(2)] + [co_ref[...]]
    for i, piece in enumerate(pieces):
        s.mix[i, own, :] = jnp.concatenate([piece, blank], axis=0).astype(BF16)
    launch(2)
    launch(0)
    s.ffn2[t, 0] = fi_ref[1].astype(BF16)
    s.ffn2[t, 1] = fo_ref[1].astype(BF16)
    launch(3)
    for ref in (s.pad_f, s.pad_m, s.depth_grad, s.norm_grad, s.bn_grad):
        ref[...] = jnp.zeros_like(ref)

    def norm_one(u):
        rows = rows_of(u)
        x0 = x_ref[rows, :].astype(F32)
        s.x1[rows, :] = x0
        s.n1[rows, :] = (standardize(x0)[0] * np_ref[0, 0:1, :] + np_ref[0, 1:2, :]).astype(BF16)

    each(norm_one)

    def feed_forward(shard):
        def body(u):
            rows = rows_of(u, 2 * LEN)
            inner = nn(s.n1[rows, :], s.ffn1[shard, 0])
            s.inner1[shard, rows, :] = inner
            active = (inner * sigmoid(inner)).astype(BF16)
            s.act1[shard, rows, :] = active
            s.x1[rows, :] += 0.5 * nn(active, s.ffn1[shard, 1])

        each(body, 0, utts // 2)

    feed_forward(t)
    near_here(1)
    feed_forward(near)
    relay(1)
    feed_forward(far)
    last_here(1)
    feed_forward(last)
    relay(2)
    relay(0)
    near_here(2)
    near_here(0)
    last_here(2)
    last_here(0)
    for i in range(2):
        s.small[:, 128 * i : 128 * i + PADH] = s.small_parts[2 * i, :, 0:PADH]
        s.small[:, 128 * i + PADH : 128 * i + 128] = s.small_parts[2 * i + 1, :, 0:PADH]

    masks = lane_masks(BF16)

    def mix_forward(u):
        rows = rows_of(u)
        length = length_of(u)
        x1 = s.x1[rows, :]
        n2 = (standardize(x1)[0] * np_ref[1, 0:1, :] + np_ref[1, 1:2, :]).astype(BF16)
        s.n2[rows, :] = n2
        for i, ref in enumerate((s.q, s.k, s.v)):
            ref[rows, :] = nt(n2, s.mix[i]).astype(BF16)
        key_ok = lax.broadcasted_iota(jnp.int32, (1, LEN), 1) < length
        for half, lanes in enumerate(HALVES):
            q, k, v = s.q[rows, lanes], s.k[rows, lanes], s.v[rows, lanes]
            mixture = jnp.zeros((LEN, 128), F32)
            for side in range(2):
                scores = nt(q * masks[side], k) * HEAD ** (-0.5)
                scores = jnp.where(key_ok, scores, NEG_FILL)
                exps = jnp.exp(scores - jnp.max(scores, axis=-1, keepdims=True))
                probs = exps * (1.0 / jnp.sum(exps, axis=-1, keepdims=True))
                s.probs[u, 2 * half + side] = probs
                mixture = mixture + nn(probs.astype(BF16), v * masks[side])
            s.mixture[rows, lanes] = mixture.astype(BF16)
        x2 = x1 + nn(s.mixture[rows, :], s.mix[3])
        s.x2[rows, :] = x2
        n3 = (standardize(x2)[0] * np_ref[2, 0:1, :] + np_ref[2, 1:2, :]).astype(BF16)
        s.n3[rows, :] = n3
        value = nt(n3, s.mix[4])
        gate = nt(n3, s.mix[5])
        s.value[rows, :] = value
        s.gate[rows, :] = gate
        mask = row_mask(length)
        gated = value * sigmoid(gate) * mask
        count = length.astype(F32)
        for half, lanes in enumerate(HALVES):
            s.pad_f[half, 8 : 8 + LEN, :] = gated[:, lanes]
            running = jnp.zeros((LEN, 128), F32)
            for j in range(KS):
                running = running + s.pad_f[half, 1 + j : 1 + j + LEN, :] * s.small[j : j + 1, lanes]
            s.mid[rows, lanes] = running
            mean = jnp.sum(running * mask, axis=0, keepdims=True) / count
            centred = (running - mean) * mask
            s.stat[u, 0:1, lanes] = mean
            s.stat[u, 1:2, lanes] = jnp.sum(centred * centred, axis=0, keepdims=True)
            s.stat[u, 2:3, lanes] = jnp.full((1, 128), count, F32)

    each(mix_forward)

    held = pool(s.stat, utts)
    for axis, count in counts:
        slots = getattr(s, "moment_" + axis)
        sems = [getattr(s, "moment_" + axis + side) for side in ("_send", "_recv")]
        me = lax.axis_index(axis)
        slots[me] = jnp.concatenate([*held, jnp.zeros((5, wide), F32)], axis=0)
        share_start(axis, count, slots, sems)
        if axis == "dp":
            relay(3)
            near_here(3)
        share_finish(axis, count, slots, sems)
        held = pool(slots, count)
    last_here(3)
    mean, power, total = held
    inv_std = lax.rsqrt(power / total + 1e-05)
    inv_count = 1.0 / total
    s.bn[0:1, :] = mean
    s.bn[1:2, :] = inv_std
    s.bn[2:4, :] = s.small[16:18, :]
    s.bn[6:7, :] = inv_count

    def middle(u):
        rows = rows_of(u)
        mask = row_mask(length_of(u))
        mean, inv_std, gain, bias = [s.bn[i : i + 1, :] for i in range(4)]
        xhat = (s.mid[rows, :] - mean) * inv_std
        normal = xhat * gain + bias
        sigma = sigmoid(normal)
        act3 = (normal * sigma * mask).astype(BF16)
        s.act3[rows, :] = act3
        x3 = s.x2[rows, :] + nn(act3, s.mix[6])
        n4 = (standardize(x3)[0] * np_ref[3, 0:1, :] + np_ref[3, 1:2, :]).astype(BF16)
        s.n4[rows, :] = n4
        total = jnp.zeros((LEN, D), F32)
        for i in range(shards):
            inner = nn(n4, s.ffn2[i, 0])
            s.inner2[i] = inner
            active = (inner * sigmoid(inner)).astype(BF16)
            s.act2[i, rows, :] = active
            total = total + nn(active, s.ffn2[i, 1])
        x4 = x3 + 0.5 * total
        out_o[rows, :] = (standardize(x4)[0] * np_ref[4, 0:1, :] + np_ref[4, 1:2, :]).astype(BF16)
        d4, gain4, bias4 = norm_back(x4, np_ref[4, 0:1, :], cot_ref[rows, :].astype(F32))
        g2 = (0.5 * d4).astype(BF16)
        s.g2[rows, :] = g2
        d_n4 = jnp.zeros((LEN, D), F32)
        for i in range(shards):
            d_inner = (nt(g2, s.ffn2[i, 1]) * swish_slope(s.inner2[i])).astype(BF16)
            s.din[i, rows, :] = d_inner
            d_n4 = d_n4 + nt(d_inner, s.ffn2[i, 0])
        d3, gain3, bias3 = norm_back(x3, np_ref[3, 0:1, :], d_n4)
        d3 = d3 + d4
        s.d3[rows, :] = d3
        gc = d3.astype(BF16)
        s.gc[rows, :] = gc
        d_normal = nt(gc, s.mix[6]) * mask * (sigma * (1.0 + normal * (1.0 - sigma)))
        s.d_normal[rows, :] = d_normal
        for i, part in enumerate((gain3, bias3, gain4, bias4)):
            s.norm_grad[6 + i : 7 + i, :] += part
        s.bn_grad[0:1, :] += jnp.sum(d_normal * xhat, axis=0, keepdims=True)
        s.bn_grad[1:2, :] += jnp.sum(d_normal, axis=0, keepdims=True)

    each(middle)

    sem_ids = itertools.count()

    def move(src, dst, peer):
        i = next(sem_ids)
        return pltpu.make_async_remote_copy(
            src_ref=src, dst_ref=dst, send_sem=s.reduce_send.at[i], recv_sem=s.reduce_recv.at[i],
            device_id=peer, device_id_type=MESH,
        )

    def add(target, other):
        return (target.astype(F32) + other.astype(F32)).astype(BF16)

    landing = [0]

    def chain(c, first, length):
        window = pl.ds(first, length)
        flights = [
            move(s.chunk.at[c, last, window], s.near.at[c, 1, window], {"tensor": near}),
            move(s.chunk.at[c, near, window], s.near.at[c, 0, window], {"tensor": near}),
        ]
        for flight in flights:
            flight.start()
        yield
        flights[0].wait()
        s.acc[c, 1, window] = add(s.chunk[c, far, window], s.near[c, 1, window])
        flight = move(s.acc.at[c, 1, window], s.far.at[c, window], {"tensor": far})
        flight.start()
        flights[1].wait()
        s.acc[c, 0, window] = add(s.chunk[c, t, window], s.near[c, 0, window])
        yield
        flight.wait()
        s.acc[c, 0, window] = add(s.acc[c, 0, window], s.far[c, window])
        offset, size, trail = first, length, []
        for stride, radix, cut, piece in plan_of(dp_count, length):
            digit = (d // stride) % radix
            base = landing[0]
            landing[0] += radix * piece

            def slot(i):
                return pl.ds(pl.multiple_of(base + i * piece, 16), piece)

            def part(i):
                return pl.ds(pl.multiple_of(offset + i * piece if cut else offset, 16), piece)

            flights = []
            for k in range(1, radix):
                other = (digit + k) % radix
                peer = {"dp": d + (other - digit) * stride}
                flights.append(move(s.acc.at[c, 0, part(other)], s.land.at[slot(digit)], peer))
                flights[-1].start()
            s.land[slot(digit)] = s.acc[c, 0, part(digit)]
            yield
            for flight in flights:
                flight.wait()
            total = s.land[slot(0)].astype(F32)
            for i in range(1, radix):
                total = total + s.land[slot(i)].astype(F32)
            s.acc[c, 0, part(digit)] = total.astype(BF16)
            if cut:
                trail.append((stride, radix, offset))
                offset, size = offset + digit * piece, piece
        here = pl.ds(pl.multiple_of(offset, 16), size)
        red_o[c, here] = s.acc[c, 0, here]
        for stride, radix, before in trail[::-1]:
            digit = (d // stride) % radix
            here = pl.ds(pl.multiple_of(offset, 16), size)
            flights = []
            for k in range(1, radix):
                peer = {"dp": d + ((digit + k) % radix - digit) * stride}
                flights.append(move(red_o.at[c, here], red_o.at[c, here], peer))
                flights[-1].start()
            yield
            for flight in flights:
                flight.wait()
            offset, size = before, size * radix

    live = []

    def begin(i):
        live.append(chain(*CHAINS[i]))
        next(live[-1])

    def pump():
        for item in list(live):
            if next(item, item) is item:
                live.remove(item)

    def spread_rows(c, first, left, right):
        full = tn(left, right).astype(BF16)
        for i in range(shards):
            s.chunk[c, i, first : first + PADH, :] = full[PADH * i : PADH * (i + 1), :]

    totals = ("total_dp", "total_tensor")
    count_of = dict(counts)

    def sems_of(name):
        return [getattr(s, name + side) for side in ("_send", "_recv")]

    s.total_dp[d] = s.bn_grad[...]
    share_start("dp", dp_count, s.total_dp, sems_of("total_dp"))
    for i in range(shards):
        s.chunk[0, i, 0:D, :] = tn(s.n4[...], s.din[i]).astype(BF16)
        s.chunk[0, i, D : 2 * D, :] = tn(s.g2[...], s.act2[i]).astype(BF16)
        s.chunk[0, i, 2 * D :, :] = jnp.zeros((512 - 2 * D, D), BF16)
    begin(0)
    share_finish("dp", dp_count, s.total_dp, sems_of("total_dp"))
    s.total_tensor[t] = lax.fori_loop(1, dp_count, lambda i, a: a + s.total_dp[i], s.total_dp[0])
    share_start("tensor", shards, s.total_tensor, sems_of("total_tensor"))
    spread_rows(1, 3 * PADH, s.act3[...], s.gc[...])
    share_finish("tensor", shards, s.total_tensor, sems_of("total_tensor"))
    bn_sums = lax.fori_loop(1, shards, lambda i, a: a + s.total_tensor[i], s.total_tensor[0])
    s.bn[4:6, :] = bn_sums[0:2, :]

    def conv_back(u):
        rows = rows_of(u)
        mask = row_mask(length_of(u))
        mean, inv_std, gain, bias, sum_gain, sum_bias, inv_count = [s.bn[i : i + 1, :] for i in range(7)]
        xhat = (s.mid[rows, :] - mean) * inv_std
        d_mid = inv_std * gain * (s.d_normal[rows, :] - mask * ((sum_bias + xhat * sum_gain) * inv_count))
        value = s.value[rows, :]
        sigma = sigmoid(s.gate[rows, :])
        gated = value * sigma * mask
        for half, lanes in enumerate(HALVES):
            s.pad_f[half, 8 : 8 + LEN, :] = gated[:, lanes]
            s.pad_m[half, 8 : 8 + LEN, :] = d_mid[:, lanes]
            d_gated = jnp.zeros((LEN, 128), F32)
            mid_half = d_mid[:, lanes]
            for j in range(KS):
                d_gated = d_gated + s.pad_m[half, 15 - j : 15 - j + LEN, :] * s.small[j : j + 1, lanes]
                s.depth_grad[j : j + 1, lanes] += jnp.sum(
                    s.pad_f[half, 1 + j : 1 + j + LEN, :] * mid_half, axis=0, keepdims=True
                )
            d_gated = d_gated * mask
            sig = sigma[:, lanes]
            s.d_value[rows, lanes] = (d_gated * sig).astype(BF16)
            s.d_gate[rows, lanes] = (d_gated * value[:, lanes] * sig * (1.0 - sig)).astype(BF16)
        d_n3 = nn(s.d_value[rows, :], s.mix[4]) + nn(s.d_gate[rows, :], s.mix[5])
        d2, gain2, bias2 = norm_back(s.x2[rows, :], np_ref[2, 0:1, :], d_n3)
        d2 = d2 + s.d3[rows, :]
        s.d2[rows, :] = d2
        s.ga[rows, :] = d2.astype(BF16)
        for i, part in enumerate((gain2, bias2)):
            s.norm_grad[4 + i : 5 + i, :] += part

    each(conv_back, 0, utts // 2)
    pump()
    each(conv_back, utts // 2, utts)
    pump()
    eye = (
        lax.broadcasted_iota(jnp.int32, (16, D), 0) == lax.broadcasted_iota(jnp.int32, (16, D), 1)
    ).astype(BF16)
    spread_rows(1, 4 * PADH, s.d_value[...], s.n3[...])
    spread_rows(1, 5 * PADH, s.d_gate[...], s.n3[...])
    spread_rows(1, 6 * PADH, s.mixture[...], s.ga[...])
    spread_rows(1, 7 * PADH, s.depth_grad[...].astype(BF16), eye)
    begin(1)

    def attend_back(u):
        rows = rows_of(u)
        d_mix = nt(s.ga[rows, :], s.mix[3]).astype(BF16)
        for half, lanes in enumerate(HALVES):
            q, k, v, dm = s.q[rows, lanes], s.k[rows, lanes], s.v[rows, lanes], d_mix[:, lanes]
            dq = jnp.zeros((LEN, 128), F32)
            dk = jnp.zeros((LEN, 128), F32)
            dv = jnp.zeros((LEN, 128), F32)
            for side in range(2):
                probs = s.probs[u, 2 * half + side]
                dm_side = dm * masks[side]
                d_probs = nt(dm_side, v)
                dv = dv + tn(probs.astype(BF16), dm_side)
                row_sum = jnp.sum(probs * d_probs, axis=-1, keepdims=True)
                d_scores = (probs * (d_probs - row_sum)).astype(BF16)
                dq = dq + nn(d_scores, k * masks[side])
                dk = dk + tn(d_scores, q * masks[side])
            s.dq[rows, lanes] = (dq * HEAD ** (-0.5)).astype(BF16)
            s.dk[rows, lanes] = (dk * HEAD ** (-0.5)).astype(BF16)
            s.dv[rows, lanes] = dv.astype(BF16)
        d_n2 = nn(s.dq[rows, :], s.mix[0]) + nn(s.dk[rows, :], s.mix[1]) + nn(s.dv[rows, :], s.mix[2])
        d1, gain1, bias1 = norm_back(s.x1[rows, :], np_ref[1, 0:1, :], d_n2)
        d1 = d1 + s.d2[rows, :]
        s.d1[rows, :] = d1
        s.g1[rows, :] = (0.5 * d1).astype(BF16)
        s.d_n1[rows, :] = jnp.zeros((LEN, D), F32)
        for i, part in enumerate((gain1, bias1)):
            s.norm_grad[2 + i : 3 + i, :] += part

    each(attend_back, 0, utts // 2)
    pump()
    each(attend_back, utts // 2, utts)
    pump()
    spread_rows(1, 0, s.dq[...], s.n2[...])
    spread_rows(1, PADH, s.dk[...], s.n2[...])
    spread_rows(1, 2 * PADH, s.dv[...], s.n2[...])
    begin(2)
    for i in range(shards):
        s.chunk[2, i, 256 : 256 + D, :] = tn(s.g1[...], s.act1[i]).astype(BF16)
        s.chunk[2, i, 256 + D :, :] = jnp.zeros((256 - D, D), BF16)
        s.chunk[2, i, D:256, :] = jnp.zeros((256 - D, D), BF16)
    begin(3)

    for place, shard in enumerate((last, near, far, t)):
        def feed_back(u):
            rows = rows_of(u, 2 * LEN)
            d_inner = (nt(s.g1[rows, :], s.ffn1[shard, 1]) * swish_slope(s.inner1[shard, rows, :])).astype(BF16)
            s.din1[place, rows, :] = d_inner
            s.d_n1[rows, :] += nt(d_inner, s.ffn1[shard, 0])

        each(feed_back, 0, utts // 2)
        s.chunk[2, shard, 0:D, :] = tn(s.n1[...], s.din1[place]).astype(BF16)
        if place == 1:
            begin(4)
        elif place != 2:
            pump()

    def norm_zero(u):
        rows = rows_of(u)
        d0, gain0, bias0 = norm_back(x_ref[rows, :].astype(F32), np_ref[0, 0:1, :], s.d_n1[rows, :])
        ig_o[rows, :] = d0 + s.d1[rows, :]
        for i, part in enumerate((gain0, bias0)):
            s.norm_grad[i : i + 1, :] += part

    each(norm_zero)
    s.norm_dp[d] = s.norm_grad[...]
    share_start("dp", dp_count, s.norm_dp, sems_of("norm_dp"))
    pump()
    pump()
    share_finish("dp", dp_count, s.norm_dp, sems_of("norm_dp"))
    s.norm_tensor[t] = lax.fori_loop(1, dp_count, lambda i, a: a + s.norm_dp[i], s.norm_dp[0])
    share_start("tensor", shards, s.norm_tensor, sems_of("norm_tensor"))
    pump()
    share_finish("tensor", shards, s.norm_tensor, sems_of("norm_tensor"))
    norm_sums = lax.fori_loop(1, shards, lambda i, a: a + s.norm_tensor[i], s.norm_tensor[0])
    lng_o[...] = norm_sums
    while live:
        pump()

    def square_of(a):
        a = a.astype(F32)
        return total_of(a * a)

    own_block = lax.broadcasted_iota(jnp.int32, (1, wide), 1) // PADH == t
    gb = s.bn[4:6, :]
    gbn_o[...] = jnp.zeros_like(gbn_o)
    for i in range(4):
        @pl.when(t == i)
        def _():
            gbn_o[0:2, 0:PADH] = gb[:, i * PADH : (i + 1) * PADH]

    square = square_of(red_o[0]) + square_of(red_o[1]) + square_of(red_o[2])
    square = square + total_of(jnp.where(own_block, gb * gb, 0.0))
    s.square[t] = jnp.broadcast_to(square, (8, 128))
    share_start("tensor", shards, s.square, sems_of("square"))
    share_finish("tensor", shards, s.square, sems_of("square"))
    total = s.square[0] + s.square[1] + s.square[2] + s.square[3]
    tot_o[...] = total + jnp.broadcast_to(square_of(norm_sums), (8, 128))


def step_call(lengths, x, cot, norm_params, ffn_in, ffn_out, attn_in, attn_out, conv_in, conv_out, depth_kernel, bn_params):
    counts = tuple((axis, lax.axis_size(axis)) for axis in ("dp", "tensor"))
    dp_count, shards = counts[0][1], counts[1][1]
    frames = x.shape[0]
    utts = frames // LEN
    wide = 4 * PADH
    low = lambda *dims: pltpu.VMEM(dims, BF16)
    full = lambda *dims: pltpu.VMEM(dims, F32)
    copies = copy_count(dp_count)
    scratch = {
        "ffn1": low(shards, 2, D, D), "ffn2": low(shards, 2, D, D), "mix": low(7, wide, D),
        "small_parts": full(shards, 24, 128), "small": full(24, wide),
        "x1": full(frames, D), "x2": full(frames, D), "d1": full(frames, D), "d2": full(frames, D),
        "d3": full(frames, D), "d_n1": full(frames, D),
        "n1": low(frames, D), "n2": low(frames, D), "n3": low(frames, D), "n4": low(frames, D),
        "inner1": full(shards, frames, D), "act1": low(shards, frames, D), "din1": low(shards, frames, D),
        "inner2": full(shards, LEN, D), "act2": low(shards, frames, D), "din": low(shards, frames, D),
        "q": low(frames, wide), "k": low(frames, wide), "v": low(frames, wide), "mixture": low(frames, wide),
        "dq": low(frames, wide), "dk": low(frames, wide), "dv": low(frames, wide),
        "d_value": low(frames, wide), "d_gate": low(frames, wide), "act3": low(frames, wide),
        "probs": full(utts, 4, LEN, LEN), "value": full(frames, wide), "gate": full(frames, wide),
        "mid": full(frames, wide), "d_normal": full(frames, wide),
        "g1": low(frames, D), "g2": low(frames, D), "ga": low(frames, D), "gc": low(frames, D),
        "pad_f": full(2, LEN + 16, 128), "pad_m": full(2, LEN + 16, 128), "stat": full(utts, 8, wide),
        "bn": full(8, wide), "depth_grad": full(16, wide), "norm_grad": full(16, D), "bn_grad": full(8, wide),
        "chunk": low(3, shards, 512, D), "near": low(3, 2, 512, D), "acc": low(3, 2, 512, D), "far": low(3, 512, D),
        "land": low(landing_rows(dp_count), D),
        "square": full(shards, 8, 128),
        "gather_send": pltpu.SemaphoreType.DMA((12,)), "gather_recv": pltpu.SemaphoreType.DMA((12,)),
        "reduce_send": pltpu.SemaphoreType.DMA((copies,)), "reduce_recv": pltpu.SemaphoreType.DMA((copies,)),
    }
    for name, rows, width in (("moment", 8, wide), ("total", 8, wide), ("norm", 16, D)):
        for axis, count in counts:
            scratch[name + "_" + axis] = full(count, rows, width)
    for name, count in [(a + "_" + axis, count) for a in ("moment", "total", "norm") for axis, count in counts] + [
        ("square", shards)
    ]:
        for side in ("_send", "_recv"):
            scratch[name + side] = pltpu.SemaphoreType.DMA((count,))
    return pl.pallas_call(
        functools.partial(step_kernel, counts, tuple(scratch)),
        in_specs=[SMEM_SPEC] + [VMEM_SPEC] * 11,
        out_specs=[VMEM_SPEC] * 6,
        out_shape=[
            shape((frames, D), BF16), shape((frames, D)), shape((3, 512, D), BF16), shape((16, D)), shape((8, 128)),
            shape((8, 128)),
        ],
        scratch_shapes=list(scratch.values()),
        compiler_params=pltpu.CompilerParams(collective_id=0, has_side_effects=True, vmem_limit_bytes=VMEM_CAP),
        name="step_part",
    )(lengths, x, cot, norm_params, ffn_in, ffn_out, attn_in, attn_out, conv_in, conv_out, depth_kernel, bn_params)


def local(
    block_input, lengths, cotangent, norm_params, bn_params, ffn_in, ffn_out, attn_in, attn_out, conv_in,
    depth_kernel, conv_out, stat_wide, stat_head, stat_hidden, stat_kernel, norm_second, bn_second, step_count,
):
    attn_in, conv_in = attn_in.swapaxes(1, 2), conv_in.transpose(2, 0, 1)
    stat_head, stat_kernel = stat_head.swapaxes(1, 2), stat_kernel.swapaxes(0, 1)
    block_out, input_grad, reduced, lng, total_square, gbn = step_call(
        lengths, block_input, cotangent, norm_params, ffn_in, ffn_out, attn_in, attn_out, conv_in, conv_out,
        depth_kernel, bn_params,
    )
    weights = (ffn_in, ffn_out, attn_in, attn_out, conv_in, depth_kernel, conv_out)
    outs = list(
        update_call(
            step_count, total_square, reduced, lng, gbn, weights, (stat_wide, stat_head, stat_hidden, stat_kernel),
            norm_params, norm_second, bn_params, bn_second,
        )
    )
    for i in (5, 12):
        outs[i] = outs[i].swapaxes(1, 2)
    for i in (7, 14):
        outs[i] = outs[i].transpose(1, 2, 0)
    outs[22] = outs[22].swapaxes(1, 2)
    outs[24] = outs[24].swapaxes(0, 1)
    return (block_out, input_grad, outs[0][0, :1], *outs[1:])


def solution(mesh):
    weights_specs = (
        P(None, None, "tensor"), P(None, "tensor", None), P(None, None, "tensor"), P("tensor", None),
        P(None, None, "tensor"), P(None, "tensor"), P("tensor", None),
    )
    stat_specs = (
        P("tensor", None, None, None), P("tensor", None, None, None), P("tensor", None, None, None),
        P("tensor", None, None),
    )
    frames = P(("dp", "tensor"), None)
    channels = P(None, "tensor")
    return jax.shard_map(
        local,
        mesh=mesh,
        in_specs=(frames, P("dp"), frames, P(), channels, *weights_specs, *stat_specs, P(), channels, P()),
        out_specs=(
            frames, frames, P(), P(), channels, *weights_specs, *weights_specs, P(), channels, P(), channels,
            *stat_specs,
        ),
        check_vma=False,
    )
```

time: 424 us -> 149 us (0.35)
  blocking collectives: 163 us -> 0 us
  waiting for transfers between devices: 110 us -> 0 us
  Pallas kernels: 93 us -> 139 us
  between operations: 18.9 us -> 1.48 us
  local copies, waits for them, and re-layouts: 22.8 us -> 7.97 us
  other arithmetic: 14.8 us -> 0 us
    psum x4 -> x0, blocking collectives: 126 us -> none  [the longest x1 40.6 us: local(): lax.psum(power_here + count_here * (mean_here - mean) ** 2, ('dp', 'tenso...]
    psum x1 -> x0, waiting for transfers between devices: 72 us -> none  [local(): reduced = lax.psum(chunks, 'dp').reshape(3, ROWS, D)]
    pallas_call x3 -> x1, Pallas kernels: 45.2 us -> 106 us  [step_call(): pl.pallas_call(functools.partial(step_kernel, counts, tuple(scratch)), in...]
    reduce_scatter x1 -> x0, waiting for transfers between devices: 38.3 us -> none  [local(): chunks = lax.psum_scatter(chunks, 'tensor', scatter_dimension=0, tiled=True)]
    all_gather x4 -> x0, blocking collectives: 37.7 us -> none  [the longest x2 22.6 us: local(): ffn_one, ffn_two = [lax.all_gather(a, 'tensor') for a in (ffn_one, ffn_two)]]
    pallas_call x1, Pallas kernels: 47.8 us -> 32.7 us  [update_call(): pl.pallas_call(update_kernel, grid=(1,), in_specs=[SMEM_SPEC] + [one(a) f...]
    unnamed x42 -> x4, local copies, waits for them, and re-layouts: 19 us -> 7.97 us
    reduce_sum x5 -> x0, other arithmetic: 4.82 us -> none  [the longest x1 2.14 us: local(): jnp.sum(high * high) - jnp.sum(norm_rows * norm_rows) + jnp.sum(gbn * gbn)]
  transfers between devices with their start and end apart: 2 -> 0, of which waited for: 2 -> 0; matrix products, arithmetic and copies ran while one was open for 1% -> 0% of each run, Pallas kernels for 0% -> 0%
where the time goes in v4:
time: 149 us; the launch traced here: 148 us
  Pallas kernels  139 us (93%)
  local copies, waits for them, and re-layouts  7.97 us (5%)
    pallas_call x1, Pallas kernels, step_call(): pl.pallas_call(functools.partial(step_kernel, counts, tuple(scratch)), in...  106 us
    pallas_call x1, Pallas kernels, update_call(): pl.pallas_call(update_kernel, grid=(1,), in_specs=[SMEM_SPEC] + [one(a) f...  32.7 us
    unnamed x4, local copies, waits for them, and re-layouts  7.97 us

profile of v4, /device:TPU:0, one launch (start us, length us, event | category | flops | bytes accessed | tf_op | source)
XLA Modules:
  0.0 148.4 jit_solution(15648086359191981371)
XLA Ops:
  1.3 1.9 %copy.46.x_ref = bf16[768,240]{1,0:T(8,128)(2,1)} copy(bf16[768,240]{0,1:T(8,128)(2,1)} %param.19) | data formatting | bytes 737280 | tf_op args[0]
  3.2 1.9 %copy.47.cot_ref = bf16[768,240]{1,0:T(8,128)(2,1)} copy(bf16[768,240]{0,1:T(8,128)(2,1)} %param.21) | data formatting | bytes 737280 | tf_op args[2]
  5.1 106.2 %step_part.1 = (bf16[768,240]{1,0:T(8,128)(2,1)}, f32[768,240]{1,0:T(8,128)}, bf16[3,512,240]{2,1,0:T(8,128)(2,1)}, f32[16,240]{1,0:T(8,128)}, f32[8,128]{1,0:T(8,128)}, /*index=5*/f32[8,128]{1,0:T(8,128)}) custom-call(s32[16]{0:T(128)} %lens_ref.1, bf16[768,240]{1,0:T(8,128)(2,1)} %copy.46.x_ref, bf16[768,240]{1,0:T(8,128)(2,1)} %copy.47.cot_ref, ...), custom_call_target="tpu_custom_call" | custom-call | tf_op jit(solution)/shard_map/step_part/pallas_call | solution.py:946
  111.3 1.9 %copy.48 = bf16[768,240]{0,1:T(8,128)(2,1)} copy(bf16[768,240]{1,0:T(8,128)(2,1)} %get-tuple-element.89) | data formatting | bytes 737280
  113.2 2.3 %copy.49 = f32[768,240]{0,1:T(8,128)} copy(f32[768,240]{1,0:T(8,128)} %get-tuple-element.90) | data formatting | bytes 1474560
  115.5 32.7 %update_part.1 = (f32[1,128]{1,0:T(1,128)}, f32[5,2,240]{2,1,0:T(2,128)}, f32[2,60]{1,0:T(2,128)}, f32[2,240,240]{2,1,0:T(8,128)}, f32[2,240,240]{2,1,0:T(8,128)...) custom-call(s32[1]{0:T(128)S(6)} %copy.50.step_ref, ...), custom_call_target="tpu_custom_call" | custom-call | tf_op jit(solution)/shard_map/update_part/pallas_call | solution.py:302

commit v5 on v4

--- a/solution.py
+++ b/solution.py
@@ -148,7 +148,7 @@
     for i in range(4):
         member, is_out = i // 2, i % 2
         chunk = (2, 0)[member]
-        start = is_out * (D, 256)[chunk // 2]
+        start = is_out * 256
         low = red_ref[chunk, start : start + D, :]
         wide_c = sw_ref[0, 2 * is_out + member, 0:1, 0:1]
         hidden_c = sd_ref[0, 2 * is_out + member, 0:1, 0:1]
@@ -391,12 +391,13 @@
     return mean, lax.fori_loop(0, count, power, blank), total
 
 
-CHAINS = ((0, 0, 512), (1, 256, 256), (1, 0, 256), (2, 256, 256), (2, 0, 256))
-
-
-def plan_of(dp_count, length):
+CHAINS = tuple((c, start, 256, 2) for c, start in ((0, 0), (0, 256), (1, 256), (1, 0), (2, 256), (2, 0)))
+TAIL = (2, 5, 4, 0, 1, 5, 3, 0, 2, 1, 4, 5, 2, 3, 4, 5, 3, 4, 5)
+
+
+def plan_of(dp_count, length, most):
     bits = bits_of(dp_count)
-    radices = [2] * (bits % 2) + [4] * (bits // 2)
+    radices = [2 ** (bits % most)] * (bits % most > 0) + [2**most] * (bits // most)
     plan, stride = [], 1
     for radix in radices:
         cut = length % (16 * radix) == 0
@@ -407,12 +408,12 @@
 
 
 def landing_rows(dp_count):
-    return sum(radix * piece for _, _, n in CHAINS for _, radix, _, piece in plan_of(dp_count, n))
+    return sum(radix * piece for _, _, n, m in CHAINS for _, radix, _, piece in plan_of(dp_count, n, m))
 
 
 def copy_count(dp_count):
     return sum(
-        3 + sum((radix - 1) * (1 + cut) for _, radix, cut, _ in plan_of(dp_count, n)) for _, _, n in CHAINS
+        3 + sum((radix - 1) * (1 + cut) for _, radix, cut, _ in plan_of(dp_count, n, m)) for _, _, n, m in CHAINS
     )
 
 
@@ -431,7 +432,7 @@
     s = types.SimpleNamespace(**dict(zip(names, scratch)))
     dp_count = dict(counts)["dp"]
     shards = s.ffn1.shape[0]
-    frames = x_ref.shape[0]
+    frames = x_ref.shape[1]
     utts = frames // LEN
     t, d = lax.axis_index("tensor"), lax.axis_index("dp")
     near, far = flip(t, 0), flip(t, 1)
@@ -454,10 +455,15 @@
     greet_axes(counts)
 
     own = pl.ds(pl.multiple_of(t * PADH, PADH), PADH)
+
+    def mix_part(first, count):
+        return lambda i: s.mix.at[pl.ds(first, count), pl.ds(pl.multiple_of(i * PADH, PADH), PADH), :]
+
     parts = (
         lambda i: s.small_parts.at[i],
         lambda i: s.ffn1.at[i],
-        lambda i: s.mix.at[:, pl.ds(pl.multiple_of(i * PADH, PADH), PADH), :],
+        mix_part(0, 4),
+        mix_part(4, 3),
         lambda i: s.ffn2.at[i],
     )
 
@@ -481,29 +487,37 @@
     def last_here(g):
         weight_copy(g, far, near, 2).wait()
 
-    s.small_parts[t] = jnp.zeros((24, 128), F32)
-    s.small_parts[t, 0:KS, 0:HEAD] = dk_ref[...]
-    s.small_parts[t, 16:18, 0:HEAD] = bp_ref[...]
+    def all_here(g):
+        near_here(g)
+        last_here(g)
+
     s.ffn1[t, 0] = fi_ref[0].astype(BF16)
     s.ffn1[t, 1] = fo_ref[0].astype(BF16)
-    greeted(counts)
-    launch(1)
+    x0 = x_ref[...].astype(F32).T
+    s.x1[...] = x0
+    s.x0[...] = x0.astype(BF16)
+    s.cot[...] = cot_ref[...].astype(F32).T.astype(BF16)
     blank = jnp.zeros((PADH - HEAD, D), F32)
     pieces = [ai_ref[m] for m in range(3)] + [ao_ref[...]] + [ci_ref[:, m, :] for m in range(2)] + [co_ref[...]]
     for i, piece in enumerate(pieces):
         s.mix[i, own, :] = jnp.concatenate([piece, blank], axis=0).astype(BF16)
+    s.small_parts[t] = jnp.zeros((24, 128), F32)
+    s.small_parts[t, 0:KS, 0:HEAD] = dk_ref[...]
+    s.small_parts[t, 16:18, 0:HEAD] = bp_ref[...]
+    greeted(counts)
+    launch(1)
     launch(2)
     launch(0)
+    launch(3)
     s.ffn2[t, 0] = fi_ref[1].astype(BF16)
     s.ffn2[t, 1] = fo_ref[1].astype(BF16)
-    launch(3)
+    launch(4)
     for ref in (s.pad_f, s.pad_m, s.depth_grad, s.norm_grad, s.bn_grad):
         ref[...] = jnp.zeros_like(ref)
 
     def norm_one(u):
         rows = rows_of(u)
-        x0 = x_ref[rows, :].astype(F32)
-        s.x1[rows, :] = x0
+        x0 = s.x1[rows, :]
         s.n1[rows, :] = (standardize(x0)[0] * np_ref[0, 0:1, :] + np_ref[0, 1:2, :]).astype(BF16)
 
     each(norm_one)
@@ -526,12 +540,10 @@
     feed_forward(far)
     last_here(1)
     feed_forward(last)
-    relay(2)
-    relay(0)
-    near_here(2)
-    near_here(0)
-    last_here(2)
-    last_here(0)
+    for g in (2, 0, 3):
+        relay(g)
+    for g in (2, 0, 3):
+        all_here(g)
     for i in range(2):
         s.small[:, 128 * i : 128 * i + PADH] = s.small_parts[2 * i, :, 0:PADH]
         s.small[:, 128 * i + PADH : 128 * i + 128] = s.small_parts[2 * i + 1, :, 0:PADH]
@@ -591,11 +603,11 @@
         slots[me] = jnp.concatenate([*held, jnp.zeros((5, wide), F32)], axis=0)
         share_start(axis, count, slots, sems)
         if axis == "dp":
-            relay(3)
-            near_here(3)
+            relay(4)
+            near_here(4)
         share_finish(axis, count, slots, sems)
         held = pool(slots, count)
-    last_here(3)
+    last_here(4)
     mean, power, total = held
     inv_std = lax.rsqrt(power / total + 1e-05)
     inv_count = 1.0 / total
@@ -624,8 +636,8 @@
             s.act2[i, rows, :] = active
             total = total + nn(active, s.ffn2[i, 1])
         x4 = x3 + 0.5 * total
-        out_o[rows, :] = (standardize(x4)[0] * np_ref[4, 0:1, :] + np_ref[4, 1:2, :]).astype(BF16)
-        d4, gain4, bias4 = norm_back(x4, np_ref[4, 0:1, :], cot_ref[rows, :].astype(F32))
+        s.out[rows, :] = (standardize(x4)[0] * np_ref[4, 0:1, :] + np_ref[4, 1:2, :]).astype(BF16)
+        d4, gain4, bias4 = norm_back(x4, np_ref[4, 0:1, :], s.cot[rows, :].astype(F32))
         g2 = (0.5 * d4).astype(BF16)
         s.g2[rows, :] = g2
         d_n4 = jnp.zeros((LEN, D), F32)
@@ -660,27 +672,32 @@
         return (target.astype(F32) + other.astype(F32)).astype(BF16)
 
     landing = [0]
-
-    def chain(c, first, length):
-        window = pl.ds(first, length)
+    squares = []
+
+    def square_of(a):
+        a = a.astype(F32)
+        return total_of(a * a)
+
+    def chain(c, start, length, most):
+        window = pl.ds(start, length)
         flights = [
             move(s.chunk.at[c, last, window], s.near.at[c, 1, window], {"tensor": near}),
             move(s.chunk.at[c, near, window], s.near.at[c, 0, window], {"tensor": near}),
         ]
         for flight in flights:
             flight.start()
-        yield
+        yield True
         flights[0].wait()
         s.acc[c, 1, window] = add(s.chunk[c, far, window], s.near[c, 1, window])
         flight = move(s.acc.at[c, 1, window], s.far.at[c, window], {"tensor": far})
         flight.start()
         flights[1].wait()
-        s.acc[c, 0, window] = add(s.chunk[c, t, window], s.near[c, 0, window])
-        yield
+        yield True
         flight.wait()
-        s.acc[c, 0, window] = add(s.acc[c, 0, window], s.far[c, window])
-        offset, size, trail = first, length, []
-        for stride, radix, cut, piece in plan_of(dp_count, length):
+        pair = s.chunk[c, t, window].astype(F32) + s.near[c, 0, window].astype(F32)
+        s.acc[c, 0, window] = (pair + s.far[c, window].astype(F32)).astype(BF16)
+        offset, size, trail, copies = start, length, [], 1
+        for stride, radix, cut, piece in plan_of(dp_count, length, most):
             digit = (d // stride) % radix
             base = landing[0]
             landing[0] += radix * piece
@@ -698,7 +715,7 @@
                 flights.append(move(s.acc.at[c, 0, part(other)], s.land.at[slot(digit)], peer))
                 flights[-1].start()
             s.land[slot(digit)] = s.acc[c, 0, part(digit)]
-            yield
+            yield True
             for flight in flights:
                 flight.wait()
             total = s.land[slot(0)].astype(F32)
@@ -708,8 +725,11 @@
             if cut:
                 trail.append((stride, radix, offset))
                 offset, size = offset + digit * piece, piece
+            else:
+                copies *= radix
         here = pl.ds(pl.multiple_of(offset, 16), size)
         red_o[c, here] = s.acc[c, 0, here]
+        squares.append(square_of(s.acc[c, 0, here]) * (1.0 / copies))
         for stride, radix, before in trail[::-1]:
             digit = (d // stride) % radix
             here = pl.ds(pl.multiple_of(offset, 16), size)
@@ -718,21 +738,21 @@
                 peer = {"dp": d + ((digit + k) % radix - digit) * stride}
                 flights.append(move(red_o.at[c, here], red_o.at[c, here], peer))
                 flights[-1].start()
-            yield
+            yield True
             for flight in flights:
                 flight.wait()
             offset, size = before, size * radix
 
-    live = []
+    live = {}
 
     def begin(i):
-        live.append(chain(*CHAINS[i]))
-        next(live[-1])
-
-    def pump():
-        for item in list(live):
-            if next(item, item) is item:
-                live.remove(item)
+        live[i] = chain(*CHAINS[i])
+        next(live[i])
+
+    def pump(*chosen):
+        for i in chosen or tuple(live):
+            if i in live and next(live[i], None) is None:
+                del live[i]
 
     def spread_rows(c, first, left, right):
         full = tn(left, right).astype(BF16)
@@ -747,14 +767,19 @@
 
     s.total_dp[d] = s.bn_grad[...]
     share_start("dp", dp_count, s.total_dp, sems_of("total_dp"))
+    for c in (0, 2):
+        for i in range(shards):
+            for first in (0, 256):
+                s.chunk[c, i, first + D : first + 256, :] = jnp.zeros((256 - D, D), BF16)
     for i in range(shards):
         s.chunk[0, i, 0:D, :] = tn(s.n4[...], s.din[i]).astype(BF16)
-        s.chunk[0, i, D : 2 * D, :] = tn(s.g2[...], s.act2[i]).astype(BF16)
-        s.chunk[0, i, 2 * D :, :] = jnp.zeros((512 - 2 * D, D), BF16)
     begin(0)
     share_finish("dp", dp_count, s.total_dp, sems_of("total_dp"))
     s.total_tensor[t] = lax.fori_loop(1, dp_count, lambda i, a: a + s.total_dp[i], s.total_dp[0])
     share_start("tensor", shards, s.total_tensor, sems_of("total_tensor"))
+    for i in range(shards):
+        s.chunk[0, i, 256 : 256 + D, :] = tn(s.g2[...], s.act2[i]).astype(BF16)
+    begin(1)
     spread_rows(1, 3 * PADH, s.act3[...], s.gc[...])
     share_finish("tensor", shards, s.total_tensor, sems_of("total_tensor"))
     bn_sums = lax.fori_loop(1, shards, lambda i, a: a + s.total_tensor[i], s.total_tensor[0])
@@ -791,10 +816,8 @@
         for i, part in enumerate((gain2, bias2)):
             s.norm_grad[4 + i : 5 + i, :] += part
 
-    each(conv_back, 0, utts // 2)
-    pump()
-    each(conv_back, utts // 2, utts)
-    pump()
+    each(conv_back)
+    pump(0, 1)
     eye = (
         lax.broadcasted_iota(jnp.int32, (16, D), 0) == lax.broadcasted_iota(jnp.int32, (16, D), 1)
     ).astype(BF16)
@@ -802,7 +825,7 @@
     spread_rows(1, 5 * PADH, s.d_gate[...], s.n3[...])
     spread_rows(1, 6 * PADH, s.mixture[...], s.ga[...])
     spread_rows(1, 7 * PADH, s.depth_grad[...].astype(BF16), eye)
-    begin(1)
+    begin(2)
 
     def attend_back(u):
         rows = rows_of(u)
@@ -834,18 +857,18 @@
             s.norm_grad[2 + i : 3 + i, :] += part
 
     each(attend_back, 0, utts // 2)
-    pump()
+    pump(2)
     each(attend_back, utts // 2, utts)
-    pump()
+    pump(0)
     spread_rows(1, 0, s.dq[...], s.n2[...])
     spread_rows(1, PADH, s.dk[...], s.n2[...])
     spread_rows(1, 2 * PADH, s.dv[...], s.n2[...])
-    begin(2)
+    begin(3)
+    pump(1)
     for i in range(shards):
         s.chunk[2, i, 256 : 256 + D, :] = tn(s.g1[...], s.act1[i]).astype(BF16)
-        s.chunk[2, i, 256 + D :, :] = jnp.zeros((256 - D, D), BF16)
-        s.chunk[2, i, D:256, :] = jnp.zeros((256 - D, D), BF16)
-    begin(3)
+    begin(4)
+    pump(3)
 
     for place, shard in enumerate((last, near, far, t)):
         def feed_back(u):
@@ -856,37 +879,26 @@
 
         each(feed_back, 0, utts // 2)
         s.chunk[2, shard, 0:D, :] = tn(s.n1[...], s.din1[place]).astype(BF16)
+        if place == 0:
+            pump(0, 2, 4, 1)
         if place == 1:
-            begin(4)
-        elif place != 2:
-            pump()
+            begin(5)
+        if place == 2:
+            pump(3, 2, 5, 0)
+        if place == 3:
+            pump(4, 1)
 
     def norm_zero(u):
         rows = rows_of(u)
-        d0, gain0, bias0 = norm_back(x_ref[rows, :].astype(F32), np_ref[0, 0:1, :], s.d_n1[rows, :])
-        ig_o[rows, :] = d0 + s.d1[rows, :]
+        d0, gain0, bias0 = norm_back(s.x0[rows, :].astype(F32), np_ref[0, 0:1, :], s.d_n1[rows, :])
+        s.d1[rows, :] += d0
         for i, part in enumerate((gain0, bias0)):
             s.norm_grad[i : i + 1, :] += part
 
     each(norm_zero)
     s.norm_dp[d] = s.norm_grad[...]
     share_start("dp", dp_count, s.norm_dp, sems_of("norm_dp"))
-    pump()
-    pump()
-    share_finish("dp", dp_count, s.norm_dp, sems_of("norm_dp"))
-    s.norm_tensor[t] = lax.fori_loop(1, dp_count, lambda i, a: a + s.norm_dp[i], s.norm_dp[0])
-    share_start("tensor", shards, s.norm_tensor, sems_of("norm_tensor"))
-    pump()
-    share_finish("tensor", shards, s.norm_tensor, sems_of("norm_tensor"))
-    norm_sums = lax.fori_loop(1, shards, lambda i, a: a + s.norm_tensor[i], s.norm_tensor[0])
-    lng_o[...] = norm_sums
-    while live:
-        pump()
-
-    def square_of(a):
-        a = a.astype(F32)
-        return total_of(a * a)
-
+    pump(3)
     own_block = lax.broadcasted_iota(jnp.int32, (1, wide), 1) // PADH == t
     gb = s.bn[4:6, :]
     gbn_o[...] = jnp.zeros_like(gbn_o)
@@ -895,19 +907,41 @@
         def _():
             gbn_o[0:2, 0:PADH] = gb[:, i * PADH : (i + 1) * PADH]
 
-    square = square_of(red_o[0]) + square_of(red_o[1]) + square_of(red_o[2])
-    square = square + total_of(jnp.where(own_block, gb * gb, 0.0))
-    s.square[t] = jnp.broadcast_to(square, (8, 128))
-    share_start("tensor", shards, s.square, sems_of("square"))
-    share_finish("tensor", shards, s.square, sems_of("square"))
-    total = s.square[0] + s.square[1] + s.square[2] + s.square[3]
-    tot_o[...] = total + jnp.broadcast_to(square_of(norm_sums), (8, 128))
+    out_o[...] = s.out[...].astype(F32).T.astype(BF16)
+    for i in TAIL[:4]:
+        pump(i)
+    share_finish("dp", dp_count, s.norm_dp, sems_of("norm_dp"))
+    s.norm_tensor[t] = lax.fori_loop(1, dp_count, lambda i, a: a + s.norm_dp[i], s.norm_dp[0])
+    share_start("tensor", shards, s.norm_tensor, sems_of("norm_tensor"))
+    ig_o[...] = s.d1[...].T
+    for i in TAIL[4:8]:
+        pump(i)
+    share_finish("tensor", shards, s.norm_tensor, sems_of("norm_tensor"))
+    norm_sums = lax.fori_loop(1, shards, lambda i, a: a + s.norm_tensor[i], s.norm_tensor[0])
+    lng_o[...] = norm_sums
+    rest = list(TAIL[8:])
+    while len(squares) < len(CHAINS):
+        pump(*([rest.pop(0)] if rest else []))
+    square = functools.reduce(lambda a, b: a + b, squares)
+    square = square + total_of(jnp.where(own_block, gb * gb, 0.0)) * (1.0 / dp_count)
+    s.square_dp[d] = jnp.broadcast_to(square, (8, 128))
+    share_start("dp", dp_count, s.square_dp, sems_of("square_dp"))
+    for i in rest[:-1]:
+        pump(i)
+    share_finish("dp", dp_count, s.square_dp, sems_of("square_dp"))
+    s.square_tensor[t] = lax.fori_loop(1, dp_count, lambda i, a: a + s.square_dp[i], s.square_dp[0])
+    share_start("tensor", shards, s.square_tensor, sems_of("square_tensor"))
+    while live:
+        pump()
+    share_finish("tensor", shards, s.square_tensor, sems_of("square_tensor"))
+    square = lax.fori_loop(1, shards, lambda i, a: a + s.square_tensor[i], s.square_tensor[0])
+    tot_o[...] = square + jnp.broadcast_to(square_of(norm_sums), (8, 128))
 
 
 def step_call(lengths, x, cot, norm_params, ffn_in, ffn_out, attn_in, attn_out, conv_in, conv_out, depth_kernel, bn_params):
     counts = tuple((axis, lax.axis_size(axis)) for axis in ("dp", "tensor"))
     dp_count, shards = counts[0][1], counts[1][1]
-    frames = x.shape[0]
+    frames = x.shape[1]
     utts = frames // LEN
     wide = 4 * PADH
     low = lambda *dims: pltpu.VMEM(dims, BF16)
@@ -918,6 +952,7 @@
         "small_parts": full(shards, 24, 128), "small": full(24, wide),
         "x1": full(frames, D), "x2": full(frames, D), "d1": full(frames, D), "d2": full(frames, D),
         "d3": full(frames, D), "d_n1": full(frames, D),
+        "x0": low(frames, D), "cot": low(frames, D), "out": low(frames, D),
         "n1": low(frames, D), "n2": low(frames, D), "n3": low(frames, D), "n4": low(frames, D),
         "inner1": full(shards, frames, D), "act1": low(shards, frames, D), "din1": low(shards, frames, D),
         "inner2": full(shards, LEN, D), "act2": low(shards, frames, D), "din": low(shards, frames, D),
@@ -931,24 +966,20 @@
         "bn": full(8, wide), "depth_grad": full(16, wide), "norm_grad": full(16, D), "bn_grad": full(8, wide),
         "chunk": low(3, shards, 512, D), "near": low(3, 2, 512, D), "acc": low(3, 2, 512, D), "far": low(3, 512, D),
         "land": low(landing_rows(dp_count), D),
-        "square": full(shards, 8, 128),
-        "gather_send": pltpu.SemaphoreType.DMA((12,)), "gather_recv": pltpu.SemaphoreType.DMA((12,)),
+        "gather_send": pltpu.SemaphoreType.DMA((15,)), "gather_recv": pltpu.SemaphoreType.DMA((15,)),
         "reduce_send": pltpu.SemaphoreType.DMA((copies,)), "reduce_recv": pltpu.SemaphoreType.DMA((copies,)),
     }
-    for name, rows, width in (("moment", 8, wide), ("total", 8, wide), ("norm", 16, D)):
+    for name, rows, width in (("moment", 8, wide), ("total", 8, wide), ("norm", 16, D), ("square", 8, 128)):
         for axis, count in counts:
             scratch[name + "_" + axis] = full(count, rows, width)
-    for name, count in [(a + "_" + axis, count) for a in ("moment", "total", "norm") for axis, count in counts] + [
-        ("square", shards)
-    ]:
-        for side in ("_send", "_recv"):
-            scratch[name + side] = pltpu.SemaphoreType.DMA((count,))
+            for side in ("_send", "_recv"):
+                scratch[name + "_" + axis + side] = pltpu.SemaphoreType.DMA((count,))
     return pl.pallas_call(
         functools.partial(step_kernel, counts, tuple(scratch)),
         in_specs=[SMEM_SPEC] + [VMEM_SPEC] * 11,
         out_specs=[VMEM_SPEC] * 6,
         out_shape=[
-            shape((frames, D), BF16), shape((frames, D)), shape((3, 512, D), BF16), shape((16, D)), shape((8, 128)),
+            shape((D, frames), BF16), shape((D, frames)), shape((3, 512, D), BF16), shape((16, D)), shape((8, 128)),
             shape((8, 128)),
         ],
         scratch_shapes=list(scratch.values()),
@@ -964,7 +995,7 @@
     attn_in, conv_in = attn_in.swapaxes(1, 2), conv_in.transpose(2, 0, 1)
     stat_head, stat_kernel = stat_head.swapaxes(1, 2), stat_kernel.swapaxes(0, 1)
     block_out, input_grad, reduced, lng, total_square, gbn = step_call(
-        lengths, block_input, cotangent, norm_params, ffn_in, ffn_out, attn_in, attn_out, conv_in, conv_out,
+        lengths, block_input.T, cotangent.T, norm_params, ffn_in, ffn_out, attn_in, attn_out, conv_in, conv_out,
         depth_kernel, bn_params,
     )
     weights = (ffn_in, ffn_out, attn_in, attn_out, conv_in, depth_kernel, conv_out)
@@ -980,7 +1011,7 @@
         outs[i] = outs[i].transpose(1, 2, 0)
     outs[22] = outs[22].swapaxes(1, 2)
     outs[24] = outs[24].swapaxes(0, 1)
-    return (block_out, input_grad, outs[0][0, :1], *outs[1:])
+    return (block_out.T, input_grad.T, outs[0][0, :1], *outs[1:])
 
 
 def solution(mesh):

time: 149 us -> 134 us (0.90)
  Pallas kernels: 139 us -> 131 us
  local copies, waits for them, and re-layouts: 7.97 us -> 1.61 us
    pallas_call x1, Pallas kernels: 106 us -> 98 us  [step_call(): pl.pallas_call(functools.partial(step_kernel, counts, tuple(scratch)), in...]
    unnamed x4 -> x6, local copies, waits for them, and re-layouts: 7.97 us -> 1.61 us
where the time goes in v5:
time: 134 us
  Pallas kernels  131 us (98%)
  local copies, waits for them, and re-layouts  1.61 us (1%)
  between operations  1.35 us (1%)
    pallas_call x1, Pallas kernels, step_call(): pl.pallas_call(functools.partial(step_kernel, counts, tuple(scratch)), in...  98 us
    pallas_call x1, Pallas kernels, update_call(): pl.pallas_call(update_kernel, grid=(1,), in_specs=[SMEM_SPEC] + [one(a) f...  32.9 us

profile of v5, /device:TPU:0, one launch (start us, length us, event | category | flops | bytes accessed | tf_op | source)
XLA Modules:
  0.0 133.9 jit_solution(1761903905228533332)
XLA Ops:
  1.3 98.0 %step_part.1 = (bf16[240,768]{1,0:T(8,128)(2,1)}, f32[240,768]{1,0:T(8,128)}, bf16[3,512,240]{2,1,0:T(8,128)(2,1)}, f32[16,240]{1,0:T(8,128)}, f32[8,128]{1,0:T(8,128)}, /*index=5*/f32[8,128]{1,0:T(8,128)}) custom-call(s32[16]{0:T(128)} %lens_ref.1, bf16[240,768]{1,0:T(8,128)(2,1)} %bitcast.21, bf16[240,768]{1,0:T(8,128)(2,1)} %bitcast.22, ...), custom_call_target="tpu_custom_call" | custom-call | tf_op jit(solution)/shard_map/step_part/pallas_call | solution.py:977
  99.3 0.0 copy-start.1
  99.3 0.0 copy-start
  99.3 32.9 %update_part.1 = (f32[1,128]{1,0:T(1,128)}, f32[5,2,240]{2,1,0:T(2,128)}, f32[2,60]{1,0:T(2,128)}, f32[2,240,240]{2,1,0:T(8,128)}, f32[2,240,240]{2,1,0:T(8,128)...) custom-call(s32[1]{0:T(128)S(6)} %copy.48.step_ref, ...), custom_call_target="tpu_custom_call" | custom-call | tf_op jit(solution)/shard_map/update_part/pallas_call | solution.py:302
  132.2 0.0 copy-done.1
  132.3 0.7 copy.49
  133.0 0.0 copy-done
  133.0 0.9 copy.50
Async XLA Ops:
  99.3 32.9 %copy-start.1 = (bf16[240,768]{1,0:T(8,128)(2,1)S(1)}, bf16[240,768]{1,0:T(8,128)(2,1)}, u32[]{:S(2)}) copy-start(bf16[240,768]{1,0:T(8,128)(2,1)} %get-tuple-element.58) | copy-start | bytes 1105924
  99.3 33.7 %copy-start = (f32[240,768]{1,0:T(8,128)S(1)}, f32[240,768]{1,0:T(8,128)}, u32[]{:S(2)}) copy-start(f32[240,768]{1,0:T(8,128)} %get-tuple-element.59) | copy-start | bytes 2211844

commit v6 on v5

--- a/solution.py
+++ b/solution.py
@@ -115,13 +115,31 @@
 
 
 def update_kernel(
-    step_ref, tot_ref, red_ref, lng_ref, gbn_ref, fi_ref, fo_ref, ai_ref, ao_ref, ci_ref, dk_ref, co_ref,
-    sw_ref, sh_ref, sd_ref, sk_ref, np_ref, ns_ref, bp_ref, bs_ref,
-    gn_o, cn_o, cb_o, cfi_o, cfo_o, cai_o, cao_o, cci_o, cdk_o, cco_o,
+    step_ref, tot_ref, red_ref, lng_ref, gbn_ref, fi_far, fo_far, ai_ref, ao_ref, ci_ref, dk_ref, co_ref,
+    sw_ref, sh_ref, sd_ref, sk_ref, np_ref, ns_ref, bp_ref, bs_ref, rows_far, back_far,
+    gn_o, cn_o, cb_o, cfi_far, cfo_far, cai_o, cao_o, cci_o, cdk_o, cco_o,
     nfi_o, nfo_o, nai_o, nao_o, nci_o, ndk_o, nco_o, nn_o, nb_o, nns_o, nbs_o,
-    nsw_o, nsh_o, nsd_o, nsk_o,
-    mat_f, mat_b, dir_f, dir_b,
+    nsw_far, nsh_o, nsd_far, nsk_o, turned_far, back_o,
+    mat_f, mat_b, dir_f, dir_b, fi_ref, fo_ref, rows_sc, back_sc, cfi_o, cfo_o, nsw_o, nsd_o, turned_sc, turned_back,
+    in_sem, out_sem,
 ):
+    fetches = [
+        pltpu.make_async_copy(src, dst, in_sem.at[i])
+        for i, (src, dst) in enumerate(
+            ((rows_far, rows_sc), (back_far, back_sc), (fi_far, fi_ref), (fo_far, fo_ref))
+        )
+    ]
+    for fetch in fetches:
+        fetch.start()
+    stores = [
+        pltpu.make_async_copy(src, dst, out_sem.at[i])
+        for i, (src, dst) in enumerate(
+            (
+                (nsw_o, nsw_far), (nsd_o, nsd_far), (cfi_o, cfi_far), (cfo_o, cfo_far), (turned_sc, turned_far),
+                (turned_back, back_o),
+            )
+        )
+    ]
     steps = jnp.full((1, 1), step_ref[0], jnp.int32).astype(F32)
     rate = PEAK_RATE * jnp.minimum(steps / WARM_STEPS, jnp.sqrt(WARM_STEPS / steps))
     grad_norm = jnp.sqrt(tot_ref[0:1, 0:1])
@@ -231,10 +249,29 @@
 
     def coarse_step(i, carry):
         advance(False)
+        if width < frames:
+            turn(i)
         return carry
 
+    for store in stores[:4]:
+        store.start()
     advance(True)
-    lax.fori_loop(0, ROOT_ITERS - 2, coarse_step, 0)
+    for fetch in fetches:
+        fetch.wait()
+    frames = rows_sc.shape[0]
+    steps = ROOT_ITERS - 2
+    width = frames // steps if frames % (128 * steps) == 0 else frames
+
+    def turn(i):
+        here = pl.ds(pl.multiple_of(i * width, width), width)
+        turned_sc[:, here] = rows_sc[here, :].astype(F32).T.astype(BF16)
+        turned_back[:, here] = back_sc[here, :].T
+
+    if width == frames:
+        turn(0)
+    lax.fori_loop(0, steps, coarse_step, 0)
+    for store in stores[4:]:
+        store.start()
     for k in range(2):
         for mats, dirs, count in ((mat_f, dir_f, 4), (mat_b, dir_b, 2)):
             for i in range(count):
@@ -272,6 +309,8 @@
             weight = weight_ref[at]
             clip_o[at] = clipped
             new_o[at] = weight - graft(weight, direction) * direction
+    for store in stores:
+        store.wait()
 
 
 def shape(dims, dtype=F32):
@@ -285,35 +324,41 @@
 
 SMEM_SPEC = pl.BlockSpec(memory_space=pltpu.SMEM)
 VMEM_SPEC = pl.BlockSpec(memory_space=pltpu.VMEM)
+ANY_SPEC = pl.BlockSpec(memory_space=pl.ANY)
 PARAMS = pltpu.CompilerParams(vmem_limit_bytes=VMEM_CAP)
 
 
-def update_call(step_count, total_square, reduced, lng, gbn, weights, stats, norm_params, norm_second, bn_params, bn_second):
+def update_call(step_count, total_square, reduced, lng, gbn, weights, stats, norm_params, norm_second, bn_params, bn_second, rows, back):
     stat_wide, stat_head, stat_hidden, stat_kernel = stats
     corner = lambda a: pl.BlockSpec((1, a.shape[1], 8, 128), lambda i: (0, 0, 0, 0))
     one = lambda a: whole(a.shape)
     n_stat = lambda a: whole(a.shape)
     out_arrays = [
         shape((1, 128)), norm_params, bn_params, *weights, *weights, norm_params, bn_params, norm_params, bn_params,
-        stat_wide, stat_head, stat_hidden, stat_kernel,
+        stat_wide, stat_head, stat_hidden, stat_kernel, shape((D, rows.shape[0]), BF16), shape((D, rows.shape[0])),
     ]
+    far_out = (3, 4, 21, 23, 25, 26)
     in_arrays = [total_square, reduced, lng, gbn, *weights]
     wide = 4 * PADH
     return pl.pallas_call(
         update_kernel,
         grid=(1,),
-        in_specs=[SMEM_SPEC] + [one(a) for a in in_arrays]
+        in_specs=[SMEM_SPEC] + [ANY_SPEC if i in (4, 5) else one(a) for i, a in enumerate(in_arrays)]
         + [corner(stat_wide), one(stat_head), corner(stat_hidden), one(stat_kernel)]
-        + [one(a) for a in (norm_params, norm_second, bn_params, bn_second)],
-        out_specs=[one(a) for a in out_arrays],
-        out_shape=[shape(a.shape) for a in out_arrays],
+        + [one(a) for a in (norm_params, norm_second, bn_params, bn_second)] + [ANY_SPEC] * 2,
+        out_specs=[ANY_SPEC if i in far_out else one(a) for i, a in enumerate(out_arrays)],
+        out_shape=[shape(a.shape, a.dtype) for a in out_arrays],
         scratch_shapes=[
             pltpu.VMEM((8, D, D), F32), pltpu.VMEM((4, wide, wide), F32),
             pltpu.VMEM((4, D, D), F32), pltpu.VMEM((2, D, wide), F32),
+            pltpu.VMEM(weights[0].shape, F32), pltpu.VMEM(weights[1].shape, F32),
+            pltpu.VMEM(rows.shape, BF16), pltpu.VMEM(back.shape, F32),
+        ] + [pltpu.VMEM(out_arrays[i].shape, out_arrays[i].dtype) for i in (3, 4, 21, 23, 25, 26)] + [
+            pltpu.SemaphoreType.DMA((4,)), pltpu.SemaphoreType.DMA((6,)),
         ],
         compiler_params=PARAMS,
         name="update_part",
-    )(step_count, *in_arrays, *stats, norm_params, norm_second, bn_params, bn_second)
+    )(step_count, *in_arrays, *stats, norm_params, norm_second, bn_params, bn_second, rows, back)
 
 
 MESH = pl.DeviceIdType.MESH
@@ -426,13 +471,13 @@
 
 
 def step_kernel(
-    counts, names, lens_ref, x_ref, cot_ref, np_ref, fi_ref, fo_ref, ai_ref, ao_ref, ci_ref, co_ref, dk_ref, bp_ref,
+    counts, names, lens_ref, np_ref, ai_ref, ao_ref, ci_ref, co_ref, dk_ref, bp_ref, fi_far, x_far, fo_far, cot_far,
     out_o, ig_o, red_o, lng_o, tot_o, gbn_o, *scratch,
 ):
     s = types.SimpleNamespace(**dict(zip(names, scratch)))
     dp_count = dict(counts)["dp"]
     shards = s.ffn1.shape[0]
-    frames = x_ref.shape[1]
+    frames = x_far.shape[1]
     utts = frames // LEN
     t, d = lax.axis_index("tensor"), lax.axis_index("dp")
     near, far = flip(t, 0), flip(t, 1)
@@ -453,6 +498,13 @@
         lax.fori_loop(start, stop, turn, 0)
 
     greet_axes(counts)
+    fi_ref, x_ref, fo_ref, cot_ref = held_in = (s.fi, s.x, s.fo, s.cot_in)
+    fetches = [
+        pltpu.make_async_copy(src, dst, s.fetch.at[i])
+        for i, (src, dst) in enumerate(zip((fi_far, x_far, fo_far, cot_far), held_in))
+    ]
+    for fetch in fetches:
+        fetch.start()
 
     own = pl.ds(pl.multiple_of(t * PADH, PADH), PADH)
 
@@ -491,12 +543,6 @@
         near_here(g)
         last_here(g)
 
-    s.ffn1[t, 0] = fi_ref[0].astype(BF16)
-    s.ffn1[t, 1] = fo_ref[0].astype(BF16)
-    x0 = x_ref[...].astype(F32).T
-    s.x1[...] = x0
-    s.x0[...] = x0.astype(BF16)
-    s.cot[...] = cot_ref[...].astype(F32).T.astype(BF16)
     blank = jnp.zeros((PADH - HEAD, D), F32)
     pieces = [ai_ref[m] for m in range(3)] + [ao_ref[...]] + [ci_ref[:, m, :] for m in range(2)] + [co_ref[...]]
     for i, piece in enumerate(pieces):
@@ -504,6 +550,14 @@
     s.small_parts[t] = jnp.zeros((24, 128), F32)
     s.small_parts[t, 0:KS, 0:HEAD] = dk_ref[...]
     s.small_parts[t, 16:18, 0:HEAD] = bp_ref[...]
+    for fetch in fetches:
+        fetch.wait()
+    s.ffn1[t, 0] = fi_ref[0].astype(BF16)
+    s.ffn1[t, 1] = fo_ref[0].astype(BF16)
+    x0 = x_ref[...].astype(F32).T
+    s.x1[...] = x0
+    s.x0[...] = x0.astype(BF16)
+    s.cot[...] = cot_ref[...].astype(F32).T.astype(BF16)
     greeted(counts)
     launch(1)
     launch(2)
@@ -636,7 +690,7 @@
             s.act2[i, rows, :] = active
             total = total + nn(active, s.ffn2[i, 1])
         x4 = x3 + 0.5 * total
-        s.out[rows, :] = (standardize(x4)[0] * np_ref[4, 0:1, :] + np_ref[4, 1:2, :]).astype(BF16)
+        out_o[rows, :] = (standardize(x4)[0] * np_ref[4, 0:1, :] + np_ref[4, 1:2, :]).astype(BF16)
         d4, gain4, bias4 = norm_back(x4, np_ref[4, 0:1, :], s.cot[rows, :].astype(F32))
         g2 = (0.5 * d4).astype(BF16)
         s.g2[rows, :] = g2
@@ -891,7 +945,7 @@
     def norm_zero(u):
         rows = rows_of(u)
         d0, gain0, bias0 = norm_back(s.x0[rows, :].astype(F32), np_ref[0, 0:1, :], s.d_n1[rows, :])
-        s.d1[rows, :] += d0
+        ig_o[rows, :] = s.d1[rows, :] + d0
         for i, part in enumerate((gain0, bias0)):
             s.norm_grad[i : i + 1, :] += part
 
@@ -907,13 +961,11 @@
         def _():
             gbn_o[0:2, 0:PADH] = gb[:, i * PADH : (i + 1) * PADH]
 
-    out_o[...] = s.out[...].astype(F32).T.astype(BF16)
     for i in TAIL[:4]:
         pump(i)
     share_finish("dp", dp_count, s.norm_dp, sems_of("norm_dp"))
     s.norm_tensor[t] = lax.fori_loop(1, dp_count, lambda i, a: a + s.norm_dp[i], s.norm_dp[0])
     share_start("tensor", shards, s.norm_tensor, sems_of("norm_tensor"))
-    ig_o[...] = s.d1[...].T
     for i in TAIL[4:8]:
         pump(i)
     share_finish("tensor", shards, s.norm_tensor, sems_of("norm_tensor"))
@@ -952,7 +1004,9 @@
         "small_parts": full(shards, 24, 128), "small": full(24, wide),
         "x1": full(frames, D), "x2": full(frames, D), "d1": full(frames, D), "d2": full(frames, D),
         "d3": full(frames, D), "d_n1": full(frames, D),
-        "x0": low(frames, D), "cot": low(frames, D), "out": low(frames, D),
+        "fi": full(*ffn_in.shape), "fo": full(*ffn_out.shape), "x": low(D, frames), "cot_in": low(D, frames),
+        "fetch": pltpu.SemaphoreType.DMA((4,)),
+        "x0": low(frames, D), "cot": low(frames, D),
         "n1": low(frames, D), "n2": low(frames, D), "n3": low(frames, D), "n4": low(frames, D),
         "inner1": full(shards, frames, D), "act1": low(shards, frames, D), "din1": low(shards, frames, D),
         "inner2": full(shards, LEN, D), "act2": low(shards, frames, D), "din": low(shards, frames, D),
@@ -976,16 +1030,16 @@
                 scratch[name + "_" + axis + side] = pltpu.SemaphoreType.DMA((count,))
     return pl.pallas_call(
         functools.partial(step_kernel, counts, tuple(scratch)),
-        in_specs=[SMEM_SPEC] + [VMEM_SPEC] * 11,
+        in_specs=[SMEM_SPEC] + [VMEM_SPEC] * 7 + [ANY_SPEC] * 4,
         out_specs=[VMEM_SPEC] * 6,
         out_shape=[
-            shape((D, frames), BF16), shape((D, frames)), shape((3, 512, D), BF16), shape((16, D)), shape((8, 128)),
+            shape((frames, D), BF16), shape((frames, D)), shape((3, 512, D), BF16), shape((16, D)), shape((8, 128)),
             shape((8, 128)),
         ],
         scratch_shapes=list(scratch.values()),
         compiler_params=pltpu.CompilerParams(collective_id=0, has_side_effects=True, vmem_limit_bytes=VMEM_CAP),
         name="step_part",
-    )(lengths, x, cot, norm_params, ffn_in, ffn_out, attn_in, attn_out, conv_in, conv_out, depth_kernel, bn_params)
+    )(lengths, norm_params, attn_in, attn_out, conv_in, conv_out, depth_kernel, bn_params, ffn_in, x, ffn_out, cot)
 
 
 def local(
@@ -1002,7 +1056,7 @@
     outs = list(
         update_call(
             step_count, total_square, reduced, lng, gbn, weights, (stat_wide, stat_head, stat_hidden, stat_kernel),
-            norm_params, norm_second, bn_params, bn_second,
+            norm_params, norm_second, bn_params, bn_second, block_out, input_grad,
         )
     )
     for i in (5, 12):
@@ -1011,7 +1065,7 @@
         outs[i] = outs[i].transpose(1, 2, 0)
     outs[22] = outs[22].swapaxes(1, 2)
     outs[24] = outs[24].swapaxes(0, 1)
-    return (block_out.T, input_grad.T, outs[0][0, :1], *outs[1:])
+    return (outs[25].T, outs[26].T, outs[0][0, :1], *outs[1:25])
 
 
 def solution(mesh):

time: 134 us -> 131 us (0.978)
  local copies, waits for them, and re-layouts: 1.61 us -> 0 us
    unnamed x6 -> x0, local copies, waits for them, and re-layouts: 1.61 us -> none
where the time goes in v6:
time: 131 us
  Pallas kernels  130 us (99%)
  between operations  1.48 us (1%)
    pallas_call x1, Pallas kernels, step_call(): pl.pallas_call(functools.partial(step_kernel, counts, tuple(scratch)), in...  97.4 us
    pallas_call x1, Pallas kernels, update_call(): pl.pallas_call(update_kernel, grid=(1,), in_specs=[SMEM_SPEC] + [ANY_SPEC...  32.4 us

profile of v6, /device:TPU:0, one launch (start us, length us, event | category | flops | bytes accessed | tf_op | source)
XLA Modules:
  0.0 131.3 jit_solution(5038740080113249723)
XLA Ops:
  1.3 97.4 %step_part.1 = (bf16[768,240]{1,0:T(8,128)(2,1)}, f32[768,240]{1,0:T(8,128)}, bf16[3,512,240]{2,1,0:T(8,128)(2,1)}, f32[16,240]{1,0:T(8,128)}, f32[8,128]{1,0:T(8,128)}, /*index=5*/f32[8,128]{1,0:T(8,128)}) custom-call(s32[16]{0:T(128)} %lens_ref.1, f32[5,2,240]{2,1,0:T(2,128)} %np_ref.3, f32[3,60,240]{2,1,0:T(8,128)} %bitcast.16, f32[60,240]{1,0:T(8,128)} %ao_ref.3, ...), custom_call_target="tpu_custom_call" | custom-call | tf_op jit(solution)/shard_map/step_part/pallas_call | solution.py:1031
  98.7 32.4 %update_part.1 = (f32[1,128]{1,0:T(1,128)}, f32[5,2,240]{2,1,0:T(2,128)}, f32[2,60]{1,0:T(2,128)}, f32[2,240,240]{2,1,0:T(8,128)}, f32[2,240,240]{2,1,0:T(8,128)...) custom-call(s32[1]{0:T(128)S(6)} %copy.46.step_ref, ...), custom_call_target="tpu_custom_call" | custom-call | tf_op jit(solution)/shard_map/update_part/pallas_call | solution.py:343

commit v7 on v6

--- a/solution.py
+++ b/solution.py
@@ -100,7 +100,7 @@
         step = 0.0625 * square - 0.625 * own
         halves = split(step)
         once = mul_fine(halves, parts)[0]
-        twice = mul_fine(halves, split(once))[0]
+        twice = nn(halves[0], once.astype(BF16))
     else:
         low = own.astype(BF16)
         square, moved = stacked([low, rider], low)
@@ -462,6 +462,10 @@
     )
 
 
+def turn(a):
+    return a.astype(F32).T.astype(BF16)
+
+
 def swish_slope(inner):
     sigma = sigmoid(inner)
     return sigma * (1.0 + inner * (1.0 - sigma))
@@ -575,6 +579,7 @@
         s.n1[rows, :] = (standardize(x0)[0] * np_ref[0, 0:1, :] + np_ref[0, 1:2, :]).astype(BF16)
 
     each(norm_one)
+    s.n1_turned[...] = turn(s.n1[...])
 
     def feed_forward(shard):
         def body(u):
@@ -825,14 +830,16 @@
         for i in range(shards):
             for first in (0, 256):
                 s.chunk[c, i, first + D : first + 256, :] = jnp.zeros((256 - D, D), BF16)
+    turned = turn(s.n4[...])
     for i in range(shards):
-        s.chunk[0, i, 0:D, :] = tn(s.n4[...], s.din[i]).astype(BF16)
+        s.chunk[0, i, 0:D, :] = nn(turned, s.din[i]).astype(BF16)
     begin(0)
     share_finish("dp", dp_count, s.total_dp, sems_of("total_dp"))
     s.total_tensor[t] = lax.fori_loop(1, dp_count, lambda i, a: a + s.total_dp[i], s.total_dp[0])
     share_start("tensor", shards, s.total_tensor, sems_of("total_tensor"))
+    turned = turn(s.g2[...])
     for i in range(shards):
-        s.chunk[0, i, 256 : 256 + D, :] = tn(s.g2[...], s.act2[i]).astype(BF16)
+        s.chunk[0, i, 256 : 256 + D, :] = nn(turned, s.act2[i]).astype(BF16)
     begin(1)
     spread_rows(1, 3 * PADH, s.act3[...], s.gc[...])
     share_finish("tensor", shards, s.total_tensor, sems_of("total_tensor"))
@@ -919,8 +926,9 @@
     spread_rows(1, 2 * PADH, s.dv[...], s.n2[...])
     begin(3)
     pump(1)
+    turned = turn(s.g1[...])
     for i in range(shards):
-        s.chunk[2, i, 256 : 256 + D, :] = tn(s.g1[...], s.act1[i]).astype(BF16)
+        s.chunk[2, i, 256 : 256 + D, :] = nn(turned, s.act1[i]).astype(BF16)
     begin(4)
     pump(3)
 
@@ -932,7 +940,7 @@
             s.d_n1[rows, :] += nt(d_inner, s.ffn1[shard, 0])
 
         each(feed_back, 0, utts // 2)
-        s.chunk[2, shard, 0:D, :] = tn(s.n1[...], s.din1[place]).astype(BF16)
+        s.chunk[2, shard, 0:D, :] = nn(s.n1_turned[...], s.din1[place]).astype(BF16)
         if place == 0:
             pump(0, 2, 4, 1)
         if place == 1:
@@ -1006,7 +1014,7 @@
         "d3": full(frames, D), "d_n1": full(frames, D),
         "fi": full(*ffn_in.shape), "fo": full(*ffn_out.shape), "x": low(D, frames), "cot_in": low(D, frames),
         "fetch": pltpu.SemaphoreType.DMA((4,)),
-        "x0": low(frames, D), "cot": low(frames, D),
+        "n1_turned": low(D, frames), "x0": low(frames, D), "cot": low(frames, D),
         "n1": low(frames, D), "n2": low(frames, D), "n3": low(frames, D), "n4": low(frames, D),
         "inner1": full(shards, frames, D), "act1": low(shards, frames, D), "din1": low(shards, frames, D),
         "inner2": full(shards, LEN, D), "act2": low(shards, frames, D), "din": low(shards, frames, D),

time: 131 us -> 129 us (0.985)
  Pallas kernels: 130 us -> 128 us
    pallas_call x1, Pallas kernels: 32.4 us -> 30.9 us  [update_call(): pl.pallas_call(update_kernel, grid=(1,), in_specs=[SMEM_SPEC] + [ANY_SPEC...]
where the time goes in v7:
time: 129 us
  Pallas kernels  128 us (99%)
  between operations  1.48 us (1%)
    pallas_call x1, Pallas kernels, step_call(): pl.pallas_call(functools.partial(step_kernel, counts, tuple(scratch)), in...  96.9 us
    pallas_call x1, Pallas kernels, update_call(): pl.pallas_call(update_kernel, grid=(1,), in_specs=[SMEM_SPEC] + [ANY_SPEC...  30.9 us

profile of v7, /device:TPU:0, one launch (start us, length us, event | category | flops | bytes accessed | tf_op | source)
XLA Modules:
  0.0 129.2 jit_solution(6352689339533805355)
XLA Ops:
  1.3 96.9 %step_part.1 = (bf16[768,240]{1,0:T(8,128)(2,1)}, f32[768,240]{1,0:T(8,128)}, bf16[3,512,240]{2,1,0:T(8,128)(2,1)}, f32[16,240]{1,0:T(8,128)}, f32[8,128]{1,0:T(8,128)}, /*index=5*/f32[8,128]{1,0:T(8,128)}) custom-call(s32[16]{0:T(128)} %lens_ref.1, f32[5,2,240]{2,1,0:T(2,128)} %np_ref.3, f32[3,60,240]{2,1,0:T(8,128)} %bitcast.16, f32[60,240]{1,0:T(8,128)} %ao_ref.3, ...), custom_call_target="tpu_custom_call" | custom-call | tf_op jit(solution)/shard_map/step_part/pallas_call | solution.py:1039
  98.2 30.9 %update_part.1 = (f32[1,128]{1,0:T(1,128)}, f32[5,2,240]{2,1,0:T(2,128)}, f32[2,60]{1,0:T(2,128)}, f32[2,240,240]{2,1,0:T(8,128)}, f32[2,240,240]{2,1,0:T(8,128)...) custom-call(s32[1]{0:T(128)S(6)} %copy.46.step_ref, ...), custom_call_target="tpu_custom_call" | custom-call | tf_op jit(solution)/shard_map/update_part/pallas_call | solution.py:343
